TPU v7x, 32 devices: a whole 2x2x4 slice. The times are simulated.
32 devices in a mesh: dp: 4 (over x, core), ep: 8 (over z, y).
Axes of the slice: x: 2, y: 2, z: 4, core: 2. Of those that a mesh axis runs over, the one named last changes fastest.
Arguments:
- tokens: bfloat16 [4, 4096, 1280], P('dp', 'ep'), may hold values from -6 to 6
- cotangent: bfloat16 [4, 4096, 1280], P('dp', 'ep'), may hold values from -6 to 6
- expert_ids: int32 [4, 4096, 7], P('dp', 'ep'), may hold values from 0 to 15, all different within a row; in each aligned block of 512 rows (0 to 511, 512 to 1023, ..., all dimensions but the last counted through in order) at most 320 rows name the same one
- keep: int32 [4, 4096, 7], P('dp', 'ep'), may hold values 0 or 1
- gates: float32 [4, 4096, 7], P('dp', 'ep'), may hold values from 0.25 to 0.75
- norm1_gain: bfloat16 [1280], P(('dp', 'ep')), may hold values from 0.5 to 1.5
- norm2_gain: bfloat16 [1280], P(('dp', 'ep')), may hold values from 0.5 to 1.5
- w_query: bfloat16 [1280, 1280], P(('dp', 'ep')), may hold values from -0.25 to 0.25
- w_key: bfloat16 [1280, 1280], P(('dp', 'ep')), may hold values from -0.25 to 0.25
- w_value: bfloat16 [1280, 1280], P(('dp', 'ep')), may hold values from -0.15625 to 0.15625
- w_out: bfloat16 [1280, 1280], P(('dp', 'ep')), may hold values from -0.625 to 0.625
- shared_gate: bfloat16 [1280, 896], P(('dp', 'ep')), may hold values from -0.15625 to 0.15625
- shared_up: bfloat16 [1280, 896], P(('dp', 'ep')), may hold values from -0.15625 to 0.15625
- shared_down: bfloat16 [896, 1280], P(None, ('dp', 'ep')), may hold values from -0.375 to 0.375
- expert_gate: bfloat16 [16, 1280, 896], P('ep'), may hold values from -0.15625 to 0.15625
- expert_up: bfloat16 [16, 1280, 896], P('ep'), may hold values from -0.15625 to 0.15625
- expert_down: bfloat16 [16, 896, 1280], P('ep'), may hold values from -0.375 to 0.375
Outputs:
- output: bfloat16 [4, 4096, 1280], P('dp', 'ep')
- grad_input: float32 [4, 4096, 1280], P('dp', 'ep')
- grad_norm1_gain: float32 [1280], P(('dp', 'ep'))
- grad_norm2_gain: float32 [1280], P(('dp', 'ep'))
- grad_w_query: float32 [1280, 1280], P(('dp', 'ep'))
- grad_w_key: float32 [1280, 1280], P(('dp', 'ep'))
- grad_w_value: float32 [1280, 1280], P(('dp', 'ep'))
- grad_w_out: float32 [1280, 1280], P(('dp', 'ep'))
- grad_shared_gate: float32 [1280, 896], P(('dp', 'ep'))
- grad_shared_up: float32 [1280, 896], P(('dp', 'ep'))
- grad_shared_down: float32 [896, 1280], P(None, ('dp', 'ep'))
- grad_expert_gate: float32 [16, 1280, 896], P('ep', 'dp')
- grad_expert_up: float32 [16, 1280, 896], P('ep', 'dp')
- grad_expert_down: float32 [16, 896, 1280], P('ep', None, 'dp')
Inputs may be any that keep to these rules, and one draw needn't show every extreme that they name: `expert_ids`: each token names 7 different experts; among the tokens of one device (aligned blocks of 512 tokens of a sequence) no expert is named by more than 320.
All inputs are finite; a program needn't handle non-finite values. No bound on the sum of `keep` on one device may be relied on, other than what follows from the above.
Results may differ from a plain program's by a relative error of at most 0.025.
Values may be sent and summed in bfloat16 or wider, within the bound.
No kernel may reach another device: no remote copies, remote signals or barrier semaphores. Data moves between devices by JAX's collectives and lax.ppermute only.
A program may use at most 320 MiB of HBM per device.

v0:
```python
import math

import jax
import jax.numpy as jnp
from jax import lax
from jax.sharding import PartitionSpec as P

HEADS = 10
HEAD = 128


epsilon = 1e-06
negative = -1e30


def angles(first, length, head_dim):
    half = head_dim // 2
    freqs = jnp.exp(jnp.arange(half, dtype=jnp.float32) * (-2.0 * math.log(10000.0) / head_dim))
    places = (first + jnp.arange(length, dtype=jnp.int32)).astype(jnp.float32)
    turned = places[:, None] * freqs[None, :]
    return (jnp.cos(turned)[:, None, :], jnp.sin(turned)[:, None, :])


def rotate(values, cosine, sine):
    half = values.shape[-1] // 2
    first_half = values[..., :half]
    second_half = values[..., half:]
    return jnp.concatenate(
        [first_half * cosine - second_half * sine, second_half * cosine + first_half * sine],
        axis=-1,
    )


def rotate_back(grads, cosine, sine):
    half = grads.shape[-1] // 2
    first_half = grads[..., :half]
    second_half = grads[..., half:]
    return jnp.concatenate(
        [first_half * cosine + second_half * sine, second_half * cosine - first_half * sine],
        axis=-1,
    )


def rms_norm(values, gain):
    inverse = lax.rsqrt(jnp.mean(values * values, axis=-1, keepdims=True) + epsilon)
    normed = values * inverse
    return (normed, inverse, normed * gain)


def norm_back(grad_out, normed, inverse, gain):
    grad_normed = grad_out * gain
    gain_grad = jnp.sum(grad_out * normed, axis=0)
    grad_values = inverse * (
        grad_normed - normed * jnp.mean(grad_normed * normed, axis=-1, keepdims=True)
    )
    return (grad_values, gain_grad)


def swiglu_back(grad_act, gate_pre, up_pre):
    sigma = jax.nn.sigmoid(gate_pre)
    grad_up = (grad_act * gate_pre * sigma).astype(jnp.bfloat16)
    grad_gate = (grad_act * up_pre * sigma * (1.0 + gate_pre * (1.0 - sigma))).astype(jnp.bfloat16)
    return (grad_gate, grad_up)


def by_blocks(step, state, pieces):
    length = pieces[0].shape[0]

    def advance(block_no, inner):
        parts = tuple((lax.dynamic_slice_in_dim(item, block_no * 512, 512, 0) for item in pieces))
        return step(inner, parts, block_no * 512)

    return lax.fori_loop(0, length // 512, advance, state)


def score_grads(
    query_part,
    grad_part,
    log_part,
    delta_part,
    query_places,
    key_part,
    value_part,
    key_places,
    scale_factor,
):
    scores = (
        jnp.einsum("qhd,khd->hqk", query_part, key_part, preferred_element_type=jnp.float32)
        * scale_factor
    )
    visible = query_places[:, None] >= key_places[None, :]
    probs = jnp.where(visible[None], jnp.exp(scores - log_part[:, :, None]), 0.0)
    grad_probs = jnp.einsum(
        "qhd,khd->hqk", grad_part, value_part, preferred_element_type=jnp.float32
    )
    grad_scores = (probs * (grad_probs - delta_part[:, :, None])).astype(jnp.bfloat16)
    return (probs.astype(jnp.bfloat16), grad_scores)


def shards(
    tokens,
    cotangent,
    expert_ids,
    keep,
    gates,
    norm1_gain,
    norm2_gain,
    w_query,
    w_key,
    w_value,
    w_out,
    shared_gate,
    shared_up,
    shared_down,
    expert_gate,
    expert_up,
    expert_down,
):
    gathered = (
        lax.all_gather(norm1_gain, ("dp", "ep"), axis=0, tiled=True),
        lax.all_gather(norm2_gain, ("dp", "ep"), axis=0, tiled=True),
        lax.all_gather(w_query, ("dp", "ep"), axis=0, tiled=True),
        lax.all_gather(w_key, ("dp", "ep"), axis=0, tiled=True),
        lax.all_gather(w_value, ("dp", "ep"), axis=0, tiled=True),
        lax.all_gather(w_out, ("dp", "ep"), axis=0, tiled=True),
        lax.all_gather(shared_gate, ("dp", "ep"), axis=0, tiled=True),
        lax.all_gather(shared_up, ("dp", "ep"), axis=0, tiled=True),
        lax.all_gather(shared_down, ("dp", "ep"), axis=1, tiled=True),
    )
    (
        gain_one,
        gain_two,
        full_query,
        full_key,
        full_value,
        full_out,
        full_gate,
        full_up,
        full_down,
    ) = gathered
    gain_one = gain_one.astype(jnp.float32)
    gain_two = gain_two.astype(jnp.float32)
    residual = tokens[0].astype(jnp.float32)
    rows, width = residual.shape
    scale_factor = 1.0 / math.sqrt(HEAD)
    offset = lax.axis_index("ep") * rows
    places = offset + jnp.arange(rows, dtype=jnp.int32)
    last_place = offset + rows - 1
    cosine, sine = angles(offset, rows, HEAD)
    normed_one, inverse_one, scaled_one = rms_norm(residual, gain_one)
    hidden_one = scaled_one.astype(jnp.bfloat16)
    query_pre = jnp.dot(hidden_one, full_query, preferred_element_type=jnp.float32).reshape(
        rows, HEADS, HEAD
    )
    key_pre = jnp.dot(hidden_one, full_key, preferred_element_type=jnp.float32).reshape(
        rows, HEADS, HEAD
    )
    value_pre = jnp.dot(hidden_one, full_value, preferred_element_type=jnp.float32)
    queries = rotate(query_pre, cosine, sine).astype(jnp.bfloat16)
    keys = rotate(key_pre, cosine, sine).astype(jnp.bfloat16)
    values_flat = value_pre.astype(jnp.bfloat16)
    values = values_flat.reshape(rows, HEADS, HEAD)
    keys_flat = keys.reshape(rows, width)
    queries_flat = queries.reshape(rows, width)

    def forward_step(state, pieces, first):
        length = pieces[0].shape[0]
        key_part = pieces[0].reshape(length, HEADS, HEAD)
        value_part = pieces[1].reshape(length, HEADS, HEAD)

        def forward_compute(inner):
            best, norm_sum, accum = inner
            scores = (
                jnp.einsum("qhd,khd->hqk", queries, key_part, preferred_element_type=jnp.float32)
                * scale_factor
            )
            visible = places[:, None] >= (first + jnp.arange(length, dtype=jnp.int32))[None, :]
            scores = jnp.where(visible[None], scores, negative)
            new_best = jnp.maximum(best, jnp.max(scores, axis=-1))
            weights = jnp.where(visible[None], jnp.exp(scores - new_best[:, :, None]), 0.0)
            factor = jnp.exp(best - new_best)
            norm_sum = norm_sum * factor + jnp.sum(weights, axis=-1)
            accum = accum * factor.T[:, :, None] + jnp.einsum(
                "hqk,khd->qhd",
                weights.astype(jnp.bfloat16),
                value_part,
                preferred_element_type=jnp.float32,
            )
            return (new_best, norm_sum, accum)

        return lax.cond(first <= last_place, forward_compute, lambda inner: inner, state)

    start_state = (
        jnp.full((HEADS, rows), negative, jnp.float32),
        jnp.zeros((HEADS, rows), jnp.float32),
        jnp.zeros((rows, HEADS, HEAD), jnp.float32),
    )
    best, norm_sum, accum = by_blocks(
        forward_step,
        start_state,
        (
            lax.all_gather(keys_flat, "ep", axis=0, tiled=True),
            lax.all_gather(values_flat, "ep", axis=0, tiled=True),
        ),
    )
    attended = accum / norm_sum.T[:, :, None]
    log_sum = best + jnp.log(norm_sum)
    attended_low = attended.reshape(rows, width).astype(jnp.bfloat16)
    middle = residual + jnp.dot(attended_low, full_out, preferred_element_type=jnp.float32)
    normed_two, inverse_two, scaled_two = rms_norm(middle, gain_two)
    hidden_two = scaled_two.astype(jnp.bfloat16)
    shared_gate_pre = jnp.dot(hidden_two, full_gate, preferred_element_type=jnp.float32)
    shared_up_pre = jnp.dot(hidden_two, full_up, preferred_element_type=jnp.float32)
    shared_act = (jax.nn.silu(shared_gate_pre) * shared_up_pre).astype(jnp.bfloat16)
    shared_branch = jnp.dot(shared_act, full_down, preferred_element_type=jnp.float32)
    choices_per = expert_ids.shape[-1]
    local_experts = expert_gate.shape[0]
    ep_size = lax.axis_size("ep")
    experts_all = ep_size * local_experts
    capacity = min(rows, rows * choices_per * 10 // (7 * experts_all))
    slot_total = experts_all * capacity
    flat_ids = expert_ids[0].reshape(-1)
    keep_flat = keep[0].reshape(-1)
    one_hot = (flat_ids[:, None] == jnp.arange(experts_all, dtype=jnp.int32)[None, :]).astype(
        jnp.int32
    )
    ranks = jnp.sum((jnp.cumsum(one_hot, axis=0) - one_hot) * one_hot, axis=1)
    slot_of = jnp.where(keep_flat == 1, flat_ids * capacity + ranks, slot_total)
    safe_slot = jnp.minimum(slot_of, slot_total - 1)
    token_of = jnp.arange(rows * choices_per, dtype=jnp.int32) // choices_per
    send_rows = jnp.take(hidden_two, token_of, axis=0)
    send = jnp.zeros((slot_total, width), jnp.bfloat16).at[slot_of].set(send_rows, mode="drop")
    send = send.reshape(ep_size, local_experts, capacity, width)
    received = lax.all_to_all(send, "ep", split_axis=0, concat_axis=0, tiled=True)
    gate_pre = jnp.einsum(
        "secd,edf->secf", received, expert_gate, preferred_element_type=jnp.float32
    )
    up_pre = jnp.einsum("secd,edf->secf", received, expert_up, preferred_element_type=jnp.float32)
    activated = (jax.nn.silu(gate_pre) * up_pre).astype(jnp.bfloat16)
    produced = jnp.einsum(
        "secf,efd->secd", activated, expert_down, preferred_element_type=jnp.float32
    ).astype(jnp.bfloat16)
    returned = lax.all_to_all(produced, "ep", split_axis=0, concat_axis=0, tiled=True).reshape(
        slot_total, width
    )
    picked = jnp.take(returned, safe_slot, axis=0).reshape(rows, choices_per, width)
    keep_float = keep[0].astype(jnp.float32)
    weight_rows = gates[0] * keep_float
    routed = jnp.einsum("tk,tkd->td", weight_rows, picked, preferred_element_type=jnp.float32)
    output = (middle + shared_branch + routed).astype(jnp.bfloat16)
    grad_out = cotangent[0].astype(jnp.float32)
    grad_low = cotangent[0]
    grad_rows = (
        (weight_rows[:, :, None] * grad_out[:, None, :])
        .astype(jnp.bfloat16)
        .reshape(rows * choices_per, width)
    )
    grad_send = jnp.zeros((slot_total, width), jnp.bfloat16).at[slot_of].set(grad_rows, mode="drop")
    grad_send = grad_send.reshape(ep_size, local_experts, capacity, width)
    grad_received = lax.all_to_all(grad_send, "ep", split_axis=0, concat_axis=0, tiled=True)
    gate_pre = jnp.einsum(
        "secd,edf->secf", received, expert_gate, preferred_element_type=jnp.float32
    )
    up_pre = jnp.einsum("secd,edf->secf", received, expert_up, preferred_element_type=jnp.float32)
    activated = (jax.nn.silu(gate_pre) * up_pre).astype(jnp.bfloat16)
    grad_act = jnp.einsum(
        "secd,efd->secf", grad_received, expert_down, preferred_element_type=jnp.float32
    )
    grad_expert_down = jnp.einsum(
        "secf,secd->efd", activated, grad_received, preferred_element_type=jnp.float32
    )
    grad_gate_pre, grad_up_pre = swiglu_back(grad_act, gate_pre, up_pre)
    grad_expert_gate = jnp.einsum(
        "secd,secf->edf", received, grad_gate_pre, preferred_element_type=jnp.float32
    )
    grad_expert_up = jnp.einsum(
        "secd,secf->edf", received, grad_up_pre, preferred_element_type=jnp.float32
    )
    grad_sent = jnp.einsum(
        "secf,edf->secd", grad_gate_pre, expert_gate, preferred_element_type=jnp.float32
    )
    grad_sent = (
        grad_sent
        + jnp.einsum("secf,edf->secd", grad_up_pre, expert_up, preferred_element_type=jnp.float32)
    ).astype(jnp.bfloat16)
    grad_back = lax.all_to_all(grad_sent, "ep", split_axis=0, concat_axis=0, tiled=True).reshape(
        slot_total, width
    )
    grad_picked = jnp.take(grad_back, safe_slot, axis=0).reshape(rows, choices_per, width)
    grad_routed = jnp.einsum(
        "tk,tkd->td", keep_float, grad_picked, preferred_element_type=jnp.float32
    )
    expert_sums = (
        lax.psum_scatter(
            grad_expert_gate.astype(jnp.bfloat16), "dp", scatter_dimension=1, tiled=True
        ).astype(jnp.float32),
        lax.psum_scatter(
            grad_expert_up.astype(jnp.bfloat16), "dp", scatter_dimension=1, tiled=True
        ).astype(jnp.float32),
        lax.psum_scatter(
            grad_expert_down.astype(jnp.bfloat16), "dp", scatter_dimension=2, tiled=True
        ).astype(jnp.float32),
    )
    grad_shared_down = jnp.einsum(
        "tf,td->fd", shared_act, grad_low, preferred_element_type=jnp.float32
    )
    grad_shared_act = jnp.einsum(
        "td,fd->tf", grad_low, full_down, preferred_element_type=jnp.float32
    )
    grad_shared_gate_pre, grad_shared_up_pre = swiglu_back(
        grad_shared_act, shared_gate_pre, shared_up_pre
    )
    grad_shared_gate = jnp.einsum(
        "td,tf->df", hidden_two, grad_shared_gate_pre, preferred_element_type=jnp.float32
    )
    grad_shared_up = jnp.einsum(
        "td,tf->df", hidden_two, grad_shared_up_pre, preferred_element_type=jnp.float32
    )
    grad_hidden_two = jnp.einsum(
        "tf,df->td", grad_shared_gate_pre, full_gate, preferred_element_type=jnp.float32
    )
    grad_hidden_two = (
        grad_hidden_two
        + jnp.einsum("tf,df->td", grad_shared_up_pre, full_up, preferred_element_type=jnp.float32)
        + grad_routed
    )
    grad_norm_two, grad_gain_two = norm_back(grad_hidden_two, normed_two, inverse_two, gain_two)
    grad_middle = grad_out + grad_norm_two
    grad_branch = grad_middle.astype(jnp.bfloat16)
    grad_full_out = jnp.einsum(
        "te,td->ed", attended_low, grad_branch, preferred_element_type=jnp.float32
    )
    grad_attended = jnp.einsum(
        "td,ed->te", grad_branch, full_out, preferred_element_type=jnp.float32
    ).astype(jnp.bfloat16)
    grad_attended_flat = grad_attended
    grad_attended = grad_attended.reshape(rows, HEADS, HEAD)
    delta = jnp.einsum("thd,thd->ht", grad_attended, attended, preferred_element_type=jnp.float32)

    def query_side(state, pieces, first):
        length = pieces[0].shape[0]
        key_part = pieces[0].reshape(length, HEADS, HEAD)
        value_part = pieces[1].reshape(length, HEADS, HEAD)

        def query_compute(inner):
            probs_low, grad_scores = score_grads(
                queries,
                grad_attended,
                log_sum,
                delta,
                places,
                key_part,
                value_part,
                first + jnp.arange(length, dtype=jnp.int32),
                scale_factor,
            )
            return inner + jnp.einsum(
                "hqk,khd->qhd", grad_scores, key_part, preferred_element_type=jnp.float32
            )

        return lax.cond(first <= last_place, query_compute, lambda inner: inner, state)

    grad_queries = by_blocks(
        query_side,
        jnp.zeros((rows, HEADS, HEAD), jnp.float32),
        (
            lax.all_gather(keys_flat, "ep", axis=0, tiled=True),
            lax.all_gather(values_flat, "ep", axis=0, tiled=True),
        ),
    )
    grad_queries = grad_queries * scale_factor
    log_all, delta_all = (
        lax.all_gather(log_sum, "ep", axis=1, tiled=True),
        lax.all_gather(delta, "ep", axis=1, tiled=True),
    )

    def key_side(state, pieces, first):
        length = pieces[0].shape[0]
        query_part = pieces[0].reshape(length, HEADS, HEAD)
        grad_part = pieces[1].reshape(length, HEADS, HEAD)
        log_part = lax.dynamic_slice_in_dim(log_all, first, length, 1)
        delta_part = lax.dynamic_slice_in_dim(delta_all, first, length, 1)

        def key_compute(inner):
            probs_low, grad_scores = score_grads(
                query_part,
                grad_part,
                log_part,
                delta_part,
                first + jnp.arange(length, dtype=jnp.int32),
                keys,
                values,
                places,
                scale_factor,
            )
            key_sum = (
                inner[0]
                + jnp.einsum(
                    "hqk,qhd->khd", grad_scores, query_part, preferred_element_type=jnp.float32
                )
                * scale_factor
            )
            value_sum = inner[1] + jnp.einsum(
                "hqk,qhd->khd", probs_low, grad_part, preferred_element_type=jnp.float32
            )
            return (key_sum, value_sum)

        return lax.cond(first + length - 1 >= offset, key_compute, lambda inner: inner, state)

    zero_grads = jnp.zeros((rows, HEADS, HEAD), jnp.float32)
    grad_keys, grad_values = by_blocks(
        key_side,
        (zero_grads, zero_grads),
        (
            lax.all_gather(queries_flat, "ep", axis=0, tiled=True),
            lax.all_gather(grad_attended_flat, "ep", axis=0, tiled=True),
        ),
    )
    grad_values = grad_values.reshape(rows, width)
    grad_query_pre = (
        rotate_back(grad_queries, cosine, sine).astype(jnp.bfloat16).reshape(rows, width)
    )
    grad_key_pre = rotate_back(grad_keys, cosine, sine).astype(jnp.bfloat16).reshape(rows, width)
    grad_value_pre = grad_values.astype(jnp.bfloat16)
    grad_full_query = jnp.einsum(
        "td,te->de", hidden_one, grad_query_pre, preferred_element_type=jnp.float32
    )
    grad_full_key = jnp.einsum(
        "td,te->de", hidden_one, grad_key_pre, preferred_element_type=jnp.float32
    )
    grad_full_value = jnp.einsum(
        "td,te->de", hidden_one, grad_value_pre, preferred_element_type=jnp.float32
    )
    grad_hidden_one = jnp.einsum(
        "te,de->td", grad_query_pre, full_query, preferred_element_type=jnp.float32
    )
    grad_hidden_one = grad_hidden_one + jnp.einsum(
        "te,de->td", grad_key_pre, full_key, preferred_element_type=jnp.float32
    )
    grad_hidden_one = grad_hidden_one + jnp.einsum(
        "te,de->td", grad_value_pre, full_value, preferred_element_type=jnp.float32
    )
    grad_norm_one, grad_gain_one = norm_back(grad_hidden_one, normed_one, inverse_one, gain_one)
    grad_input = grad_middle + grad_norm_one
    dense_sums = (
        lax.psum_scatter(grad_gain_one, ("dp", "ep"), scatter_dimension=0, tiled=True),
        lax.psum_scatter(grad_gain_two, ("dp", "ep"), scatter_dimension=0, tiled=True),
        lax.psum_scatter(grad_full_query, ("dp", "ep"), scatter_dimension=0, tiled=True),
        lax.psum_scatter(grad_full_key, ("dp", "ep"), scatter_dimension=0, tiled=True),
        lax.psum_scatter(grad_full_value, ("dp", "ep"), scatter_dimension=0, tiled=True),
        lax.psum_scatter(grad_full_out, ("dp", "ep"), scatter_dimension=0, tiled=True),
        lax.psum_scatter(grad_shared_gate, ("dp", "ep"), scatter_dimension=0, tiled=True),
        lax.psum_scatter(grad_shared_up, ("dp", "ep"), scatter_dimension=0, tiled=True),
        lax.psum_scatter(grad_shared_down, ("dp", "ep"), scatter_dimension=1, tiled=True),
    )
    return (
        output[None],
        grad_input[None],
        dense_sums[0],
        dense_sums[1],
        dense_sums[2],
        dense_sums[3],
        dense_sums[4],
        dense_sums[5],
        dense_sums[6],
        dense_sums[7],
        dense_sums[8],
        expert_sums[0],
        expert_sums[1],
        expert_sums[2],
    )


def solution(mesh):
    in_specs = (
        P("dp", "ep", None),
        P("dp", "ep", None),
        P("dp", "ep", None),
        P("dp", "ep", None),
        P("dp", "ep", None),
        P(("dp", "ep")),
        P(("dp", "ep")),
        P(("dp", "ep"), None),
        P(("dp", "ep"), None),
        P(("dp", "ep"), None),
        P(("dp", "ep"), None),
        P(("dp", "ep"), None),
        P(("dp", "ep"), None),
        P(None, ("dp", "ep")),
        P("ep", None, None),
        P("ep", None, None),
        P("ep", None, None),
    )
    out_specs = (
        P("dp", "ep", None),
        P("dp", "ep", None),
        P(("dp", "ep")),
        P(("dp", "ep")),
        P(("dp", "ep"), None),
        P(("dp", "ep"), None),
        P(("dp", "ep"), None),
        P(("dp", "ep"), None),
        P(("dp", "ep"), None),
        P(("dp", "ep"), None),
        P(None, ("dp", "ep")),
        P("ep", "dp", None),
        P("ep", "dp", None),
        P("ep", None, "dp"),
    )
    return jax.shard_map(shards, mesh=mesh, in_specs=in_specs, out_specs=out_specs, check_vma=False)
```

profile of v0, /device:TPU:12, one launch (start us, length us, event | category | flops | bytes accessed | tf_op | source)
XLA Modules:
  0.0 3684.8 jit_solution(14748036280805860703)
XLA Ops:
  11.2 41.7 %all-reduce.8 = (bf16[1280]{0:T(1024)(128)(2,1)S(1)}, bf16[1280]{0:T(1024)(128)(2,1)S(1)}) all-reduce(bf16[1280]{0:T(1024)(128)(2,1)S(1)} %dynamic-update-slice, bf16[1280]{0:T(1024)(128)(2,1)S(1)} %dynamic-update-slice.1), channel_id=1, replica_groups=mesh['dp'=4,'ep'=8] {'dp','ep'}, use_global_device_ids=true, to_apply=%add | all-reduce | flops 2560 | bytes 10240
  54.6 16.1 all-gather.18.cloned.1.call-done
  76.7 55.1 %all-gather.16.cloned.1.call-done = bf16[1280,1280]{1,0:T(8,128)(2,1)} async-done(((bf16[40,1280]{1,0:T(8,128)(2,1)}), bf16[1280,1280]{1,0:T(8,128)(2,1)}) %all-gather.16.cloned.1.call-update) | async-done | bytes 3276816 | tf_op jit(solution)/shard_map/all_gather | solution.py:122
  137.4 55.5 %all-gather.12.cloned.1.call-done = bf16[1280,1280]{1,0:T(8,128)(2,1)} async-done(((bf16[40,1280]{1,0:T(8,128)(2,1)}), bf16[1280,1280]{1,0:T(8,128)(2,1)}) %all-gather.12.cloned.1.call-update) | async-done | bytes 3276816 | tf_op jit(solution)/shard_map/all_gather | solution.py:123
  218.4 124.2 %all-gather.20.cloned.1.call-done = bf16[4096,1280]{1,0:T(8,128)(2,1)} async-done(((bf16[512,1280]{1,0:T(8,128)(2,1)}), bf16[4096,1280]{1,0:T(8,128)(2,1)}) %all-gather.20.cloned.1.call-update) | async-done | bytes 10485776 | tf_op jit(solution)/shard_map/all_gather | solution.py:203
  357.0 137.2 %all-gather.14.cloned.1.call-done = bf16[4096,1280]{0,1:T(8,128)(2,1)} async-done(((bf16[512,1280]{0,1:T(8,128)(2,1)}), bf16[4096,1280]{0,1:T(8,128)(2,1)}) %all-gather.14.cloned.1.call-update) | async-done | bytes 10485776 | tf_op jit(solution)/shard_map/all_gather | solution.py:202
  496.0 53.9 %while.56 = (s32[]{:T(128)}, f32[10,512]{1,0:T(8,128)S(1)}, f32[10,512]{1,0:T(8,128)S(1)}, f32[512,10,128]{2,0,1:T(8,128)}, s32[]{:T(128)}, /*index=5*/bf16[4096...) while((s32[]{:T(128)}, f32[10,512]{1,0:T(8,128)S(1)}, ...), condition=%wide.region_6.7_spmd.clone, body=%wide.region_1.6_spmd.clone.sunk | while | flops 1377845248 | bytes 47264056 | solution.py:73
  562.5 57.0 %scatter_custom_fusion = bf16[5120,1280]{1,0:T(8,128)(2,1)} fusion(s32[3584]{0:T(1024)S(1)} %fusion.139, pred[3584]{0:T(1024)(128)(4,1)S(1)} %compare_and_fusion.1, bf16[]{:T(256)} %constant.266.clone.1, bf16[]{:T(256)} %constant.272.clone.1, bf16[512,1280]{1,0:T(8,128)(2,1)S(1)} %multiply_convert_fusion.6, s32[4096]{0:T(1024)S(1)} %pad_clamp_fusion.1), kind=kCustom, calls=%fused_computation.102 | custom fusion | flops 4587520 | bytes 14438404 | tf_op jit(solution)/shard_map/scatter | solution.py:232
  619.6 59.2 %all-to-all-start = ((bf16[8,2,320,1280]{3,2,1,0:T(8,128)(2,1)}), bf16[8,2,320,1280]{3,2,1,0:T(8,128)(2,1)}, u32[]{:S(2)}, u32[]{:S(2)}) async-start(bf16[8,2,320,1280]{3,2,1,0:T(8,128)(2,1)} %bitcast.292), calls=%async_computation | async-start | bytes 26214400 | tf_op jit(solution)/shard_map/all_to_all | solution.py:234
  686.6 19.4 mul.494
  706.5 26.1 scatter_custom_fusion.1
  732.5 227.4 %all-to-all-done = bf16[8,2,320,1280]{3,2,1,0:T(8,128)(2,1)} async-done(((bf16[8,2,320,1280]{3,2,1,0:T(8,128)(2,1)}), bf16[8,2,320,1280]{3,2,1,0:T(8,128)(2,1)}, u32[]{:S(2)}, u32[]{:S(2)}) %all-to-all-start) | async-done | bytes 13107232 | tf_op jit(solution)/shard_map/all_to_all | solution.py:234
  969.1 21.8 fusion.59
  990.9 20.4 fusion.61
  1011.3 238.1 %all-to-all-done.2 = bf16[8,2,320,1280]{3,2,1,0:T(8,128)(2,1)} async-done(((bf16[8,2,320,1280]{3,2,1,0:T(8,128)(2,1)}), bf16[8,2,320,1280]{3,2,1,0:T(8,128)(2,1)}, u32[]{:S(2)}, u32[]{:S(2)}) %all-to-all-start.2) | async-done | bytes 13107232 | tf_op jit(solution)/shard_map/all_to_all | solution.py:260
  1249.3 33.6 fusion.49
  1283.0 22.5 fusion.83
  1305.4 23.6 fusion.63
  1349.4 17.6 convert_bitcast_fusion
  1372.8 256.2 %all-to-all-done.3 = bf16[8,2,320,1280]{3,2,1,0:T(8,128)(2,1)} async-done(((bf16[8,2,320,1280]{3,2,1,0:T(8,128)(2,1)}), bf16[8,2,320,1280]{3,2,1,0:T(8,128)(2,1)}, u32[]{:S(2)}, u32[]{:S(2)}) %all-to-all-start.3) | async-done | bytes 13107232 | tf_op jit(solution)/shard_map/all_to_all | solution.py:286
  1641.9 303.0 %all-gather.24.cloned.1.call-done = bf16[1280,896]{1,0:T(8,128)(2,1)} async-done(((bf16[40,896]{1,0:T(8,128)(2,1)}), bf16[1280,896]{1,0:T(8,128)(2,1)}) %all-gather.24.cloned.1.call-update) | async-done | bytes 2293776 | tf_op jit(solution)/shard_map/all_gather | solution.py:126
  1949.2 54.6 %all-gather.26.cloned.1.call-done = bf16[1280,896]{1,0:T(8,128)(2,1)} async-done(((bf16[40,896]{1,0:T(8,128)(2,1)}), bf16[1280,896]{1,0:T(8,128)(2,1)}) %all-gather.26.cloned.1.call-update) | async-done | bytes 2293776 | tf_op jit(solution)/shard_map/all_gather | solution.py:127
  2008.3 54.6 %all-gather.28.cloned.1.call-done = bf16[896,1280]{0,1:T(8,128)(2,1)} async-done(((bf16[896,40]{0,1:T(8,128)(2,1)}), bf16[896,1280]{0,1:T(8,128)(2,1)}) %all-gather.28.cloned.1.call-update) | async-done | bytes 2293776 | tf_op jit(solution)/shard_map/all_gather | solution.py:128
  2072.0 26.0 gather_fusion.1
  2097.9 25.6 gather_fusion
  2167.5 19.8 bitcast_convert_fusion.2
  2187.3 19.6 bitcast_convert_fusion.1
  2207.0 19.9 bitcast_convert_fusion
  2256.7 31.2 all_gather.59
  2294.3 73.7 %while.57 = (s32[]{:T(128)}, f32[512,10,128]{2,0,1:T(8,128)}, s32[]{:T(128)}, bf16[4096,1280]{0,1:T(8,128)(2,1)}, bf16[512,10,128]{2,0,1:T(8,128)(2,1)S(1)}, /*i...) while((s32[]{:T(128)}, f32[512,10,128]{2,0,1:T(8,128)}, ...), condition=%wide.region_17.19_spmd.clone, body=%wide.region_14.18_spmd.clone.sunk | while | flops 2029913088 | bytes 38588696 | solution.py:73
  2294.3 18.3 conditional.11
  2312.6 18.3 conditional.11
  2330.8 18.7 conditional.11
  2349.5 18.3 conditional.11
  2370.2 104.7 %all_gather.61 = f32[10,4096]{1,0:T(8,128)S(1)} all-gather(f32[10,512]{1,0:T(8,128)S(1)} %get-tuple-element.1765), channel_id=1, replica_groups=mesh['dp'=4,'ep'=8] {'ep'}, dimensions={1}, use_global_device_ids=true | all-gather | bytes 184320 | tf_op jit(solution)/shard_map/all_gather | solution.py:374
  2495.1 118.8 %while.58 = (s32[]{:T(128)}, f32[512,10,128]{2,0,1:T(8,128)}, f32[512,10,128]{2,0,1:T(8,128)}, s32[]{:T(128)}, bf16[4096,1280]{0,1:T(8,128)(2,1)}, /*index=5*/bf...) while((s32[]{:T(128)}, f32[512,10,128]{2,0,1:T(8,128)}, ...), condition=%wide.region_21.23_spmd.clone.clone, body=%wide.region_18.22_spmd.clone.clone.sunk | while | flops 2712798208 | bytes 108421544 | solution.py:73
  2495.1 23.3 conditional.12
  2518.4 24.9 conditional.12
  2543.3 23.4 conditional.12
  2566.6 23.8 conditional.12
  2590.4 23.4 conditional.12
  2684.7 114.7 %all-reduce.7 = (f32[1280]{0:T(1024)S(1)}, f32[1280]{0:T(1024)S(1)}) all-reduce(f32[1280]{0:T(1024)S(1)} %get-tuple-element.1271, f32[1280]{0:T(1024)S(1)} %copy-done.67), channel_id=2, replica_groups=mesh['dp'=4,'ep'=8] {'dp','ep'}, use_global_device_ids=true, to_apply=%region_24.26.clone | all-reduce | flops 2560 | bytes 20480
  2804.9 109.5 %reduce-scatter.36.cloned.1.call-done = f32[40,896]{1,0:T(8,128)} async-done(((f32[1280,896]{1,0:T(8,128)}), f32[40,896]{1,0:T(8,128)}) %reduce-scatter.36.cloned.1.call-update) | async-done | bytes 143376
  2914.4 146.0 %reduce-scatter.38.cloned.1.call-done = f32[896,40]{0,1:T(8,128)} async-done(((f32[896,1280]{0,1:T(8,128)}), f32[896,40]{0,1:T(8,128)}) %reduce-scatter.38.cloned.1.call-update) | async-done | bytes 143376
  3060.3 154.4 %reduce-scatter.26.cloned.1.call-done = f32[40,1280]{1,0:T(8,128)} async-done(((f32[1280,1280]{1,0:T(8,128)}), f32[40,1280]{1,0:T(8,128)}) %reduce-scatter.26.cloned.1.call-update) | async-done | bytes 204816 | tf_op jit(solution)/shard_map/reduce_scatter | solution.py:451
  3214.7 154.8 %reduce-scatter.20.cloned.1.call-done = f32[40,1280]{1,0:T(8,128)} async-done(((f32[1280,1280]{1,0:T(8,128)}), f32[40,1280]{1,0:T(8,128)}) %reduce-scatter.20.cloned.1.call-update) | async-done | bytes 204816 | tf_op jit(solution)/shard_map/reduce_scatter | solution.py:448
  3369.5 153.9 %reduce-scatter.22.cloned.1.call-done = f32[40,1280]{1,0:T(8,128)} async-done(((f32[1280,1280]{1,0:T(8,128)}), f32[40,1280]{1,0:T(8,128)}) %reduce-scatter.22.cloned.1.call-update) | async-done | bytes 204816 | tf_op jit(solution)/shard_map/reduce_scatter | solution.py:449
  3523.4 154.2 %reduce-scatter.24.cloned.1.call-done = f32[40,1280]{1,0:T(8,128)} async-done(((f32[1280,1280]{1,0:T(8,128)}), f32[40,1280]{1,0:T(8,128)}) %reduce-scatter.24.cloned.1.call-update) | async-done | bytes 204816 | tf_op jit(solution)/shard_map/reduce_scatter | solution.py:450
  (468 shorter events, 622.6 us)
Async XLA Ops:
  7.2 63.5 %all-gather.18.cloned.1.call-start = ((), (), s32[]{:S(2)}) async-start(), calls=%async_computation.17 | async-start | bytes 3379200 | tf_op jit(solution)/shard_map/all_gather | solution.py:124
  7.9 123.9 %all-gather.16.cloned.1.call-start = ((), (), s32[]{:S(2)}) async-start(), calls=%async_computation.16 | async-start | bytes 3379200 | tf_op jit(solution)/shard_map/all_gather | solution.py:122
  8.7 184.2 %all-gather.12.cloned.1.call-start = ((), (), s32[]{:S(2)}) async-start(), calls=%async_computation.14 | async-start | bytes 3379200 | tf_op jit(solution)/shard_map/all_gather | solution.py:123
  9.4 333.2 %all-gather.20.cloned.1.call-start = ((), (), s32[]{:S(2)}) async-start(), calls=%async_computation.18 | async-start | bytes 11796480 | tf_op jit(solution)/shard_map/all_gather | solution.py:203
  52.9 149.9 %copy-start.65 = (f32[1280]{0:T(1024)}, f32[1280]{0:T(1024)S(1)}, u32[]{:S(2)}) copy-start(f32[1280]{0:T(1024)S(1)} %convert_element_type.240) | copy-start | bytes 15364
  54.5 148.2 %copy-start.69 = (f32[512]{0:T(512)}, f32[512]{0:T(512)S(1)}, u32[]{:S(2)}) copy-start(f32[512]{0:T(512)S(1)} %add_rsqrt_fusion.1) | copy-start | bytes 6148
  76.0 418.2 %all-gather.14.cloned.1.call-start = ((), (), s32[]{:S(2)}) async-start(), calls=%async_computation.15 | async-start | bytes 11796480 | tf_op jit(solution)/shard_map/all_gather | solution.py:202
  76.6 128.1 %copy-start.43 = (f32[512,64]{0,1:T(8,128)}, f32[512,64]{0,1:T(8,128)S(1)}, u32[]{:S(2)}) copy-start(f32[512,64]{0,1:T(8,128)S(1)} %get-tuple-element.1375) | copy-start | bytes 393220
  76.7 128.1 %copy-start.45 = (f32[512,64]{0,1:T(8,128)}, f32[512,64]{0,1:T(8,128)S(1)}, u32[]{:S(2)}) copy-start(f32[512,64]{0,1:T(8,128)S(1)} %get-tuple-element.1376) | copy-start | bytes 393220
  206.9 349.8 %all-gather.22.cloned.1.call-start = ((), (), s32[]{:S(2)}) async-start(), calls=%async_computation.19 | async-start | bytes 3379200 | tf_op jit(solution)/shard_map/all_gather | solution.py:125
  208.1 352.7 %copy-start.54 = (f32[1280]{0:T(1024)}, f32[1280]{0:T(1024)S(1)}, u32[]{:S(2)}) copy-start(f32[1280]{0:T(1024)S(1)} %convert_element_type.251) | copy-start | bytes 15364
  560.8 58.8 %copy-start.63 = (f32[512]{0:T(512)}, f32[512]{0:T(512)S(1)}, u32[]{:S(2)}) copy-start(f32[512]{0:T(512)S(1)} %add_rsqrt_fusion) | copy-start | bytes 6148
  562.5 57.0 %copy-start.8 = (bf16[512,1280]{1,0:T(8,128)(2,1)}, bf16[512,1280]{1,0:T(8,128)(2,1)S(1)}, u32[]{:S(2)}) copy-start(bf16[512,1280]{1,0:T(8,128)(2,1)S(1)} %multiply_convert_fusion.6) | copy-start | bytes 3932164
  619.6 59.2 %copy-start.19 = (bf16[1,512,1280]{2,1,0:T(8,128)(2,1)S(1)}, bf16[1,512,1280]{2,1,0:T(8,128)(2,1)}, u32[]{:S(2)}) copy-start(bf16[1,512,1280]{2,1,0:T(8,128)(2,1)} %param.32) | copy-start | bytes 3932164
  619.6 340.4 %all-to-all-start = ((bf16[8,2,320,1280]{3,2,1,0:T(8,128)(2,1)}), bf16[8,2,320,1280]{3,2,1,0:T(8,128)(2,1)}, u32[]{:S(2)}, u32[]{:S(2)}) async-start(bf16[8,2,320,1280]{3,2,1,0:T(8,128)(2,1)} %bitcast.292), calls=%async_computation | async-start | bytes 26214400 | tf_op jit(solution)/shard_map/all_to_all | solution.py:234
  686.6 19.5 copy-start.61
  960.0 30.9 slice-start
  960.0 289.4 %all-to-all-start.2 = ((bf16[8,2,320,1280]{3,2,1,0:T(8,128)(2,1)}), bf16[8,2,320,1280]{3,2,1,0:T(8,128)(2,1)}, u32[]{:S(2)}, u32[]{:S(2)}) async-start(bf16[8,2,320,1280]{3,2,1,0:T(8,128)(2,1)} %bitcast.293), calls=%async_computation.2 | async-start | bytes 26214400 | tf_op jit(solution)/shard_map/all_to_all | solution.py:260
  969.0 21.8 slice-start.1
  1340.7 288.2 %all-to-all-start.3 = ((bf16[8,2,320,1280]{3,2,1,0:T(8,128)(2,1)}), bf16[8,2,320,1280]{3,2,1,0:T(8,128)(2,1)}, u32[]{:S(2)}, u32[]{:S(2)}) async-start(bf16[8,2,320,1280]{3,2,1,0:T(8,128)(2,1)} %copy.108), calls=%async_computation.3 | async-start | bytes 26214400 | tf_op jit(solution)/shard_map/all_to_all | solution.py:286
  1372.8 267.3 %copy-start.49 = (pred[1,512,7]{2,1,0:T(8,128)(4,1)S(1)}, pred[1,512,7]{2,1,0:T(8,128)(4,1)}, u32[]{:S(2)}) copy-start(pred[1,512,7]{2,1,0:T(8,128)(4,1)} %copy-done.48) | copy-start | bytes 10756
  1372.8 267.6 %copy-start.57 = (s32[1,512,7]{1,0,2:T(1,128)S(1)}, s32[1,512,7]{1,0,2:T(1,128)}, u32[]{:S(2)}) copy-start(s32[1,512,7]{1,0,2:T(1,128)} %param.34) | copy-start | bytes 43012
  1372.8 268.5 %copy-start.51 = (s32[3584]{0:T(1024)S(1)}, s32[3584]{0:T(1024)}, u32[]{:S(2)}) copy-start(s32[3584]{0:T(1024)} %copy-done.50) | copy-start | bytes 43012
  1372.8 268.5 %copy-start.53 = (s32[3584]{0:T(1024)S(1)}, s32[3584]{0:T(1024)}, u32[]{:S(2)}) copy-start(s32[3584]{0:T(1024)} %copy-done.52) | copy-start | bytes 43012
  1372.8 572.1 %copy-start.9 = (bf16[512,1280]{1,0:T(8,128)(2,1)S(1)}, bf16[512,1280]{1,0:T(8,128)(2,1)}, u32[]{:S(2)}) copy-start(bf16[512,1280]{1,0:T(8,128)(2,1)} %copy-done.8) | copy-start | bytes 3932164
  1628.9 469.0 %all-to-all-start.1 = ((bf16[8,2,320,1280]{3,2,1,0:T(8,128)(2,1)}), bf16[8,2,320,1280]{3,2,1,0:T(8,128)(2,1)}, u32[]{:S(2)}, u32[]{:S(2)}) async-start(bf16[8,2,320,1280]{3,2,1,0:T(8,128)(2,1)} %copy.105), calls=%async_computation.1 | async-start | bytes 26214400 | tf_op jit(solution)/shard_map/all_to_all | solution.py:243
  1637.6 307.2 %all-gather.24.cloned.1.call-start = ((), (), s32[]{:S(2)}) async-start(), calls=%async_computation.20 | async-start | bytes 2365440 | tf_op jit(solution)/shard_map/all_gather | solution.py:126
  1638.3 365.5 %all-gather.26.cloned.1.call-start = ((), (), s32[]{:S(2)}) async-start(), calls=%async_computation.21 | async-start | bytes 2365440 | tf_op jit(solution)/shard_map/all_gather | solution.py:127
  1639.1 423.8 %all-gather.28.cloned.1.call-start = ((), (), s32[]{:S(2)}) async-start(), calls=%async_computation.22 | async-start | bytes 2365440 | tf_op jit(solution)/shard_map/all_gather | solution.py:128
  1639.8 837.0 %all-gather.32.cloned.1.call-start = ((), (), s32[]{:S(2)}) async-start(), calls=%async_computation.24 | async-start | bytes 11796480 | tf_op jit(solution)/shard_map/all_gather | solution.py:416
  1640.4 304.5 %copy-start.58 = (f32[1,512,7]{1,0,2:T(1,128)}, f32[1,512,7]{1,0,2:T(1,128)S(1)}, u32[]{:S(2)}) copy-start(f32[1,512,7]{1,0,2:T(1,128)S(1)} %convert_element_type.254) | copy-start | bytes 43012
  1949.2 113.7 %copy-start.20 = (bf16[1,512,1280]{2,1,0:T(8,128)(2,1)S(1)}, bf16[1,512,1280]{2,1,0:T(8,128)(2,1)}, u32[]{:S(2)}) copy-start(bf16[1,512,1280]{2,1,0:T(8,128)(2,1)} %param.32) | copy-start | bytes 3932164
  2097.9 25.6 copy-start.68
  2138.6 13.6 copy-start.34
  2166.7 324.8 %all-gather.30.cloned.1.call-start = ((), (), s32[]{:S(2)}) async-start(), calls=%async_computation.23 | async-start | bytes 11796480 | tf_op jit(solution)/shard_map/all_gather | solution.py:415
  2167.4 472.4 %reduce-scatter.28.cloned.1.call-start = ((), (), s32[]{:S(2)}) async-start(), calls=%async_computation.29 | async-start | bytes 5734400 | tf_op jit(solution)/shard_map/reduce_scatter | solution.py:294
  2187.2 455.4 %reduce-scatter.30.cloned.1.call-start = ((), (), s32[]{:S(2)}) async-start(), calls=%async_computation.30 | async-start | bytes 5734400 | tf_op jit(solution)/shard_map/reduce_scatter | solution.py:297
  2206.9 438.5 %reduce-scatter.32.cloned.1.call-start = ((), (), s32[]{:S(2)}) async-start(), calls=%async_computation.31 | async-start | bytes 5734400 | tf_op jit(solution)/shard_map/reduce_scatter | solution.py:300
  2226.9 578.0 %reduce-scatter.34.cloned.1.call-start = ((), (), s32[]{:S(2)}) async-start(), calls=%async_computation.32 | async-start | bytes 4730880
  2233.6 680.7 %reduce-scatter.36.cloned.1.call-start = ((), (), s32[]{:S(2)}) async-start(), calls=%async_computation.33 | async-start | bytes 4730880
  2237.4 823.0 %reduce-scatter.38.cloned.1.call-start = ((), (), s32[]{:S(2)}) async-start(), calls=%async_computation.34 | async-start | bytes 4730880
  2242.3 972.4 %reduce-scatter.26.cloned.1.call-start = ((), (), s32[]{:S(2)}) async-start(), calls=%async_computation.28 | async-start | bytes 6758400 | tf_op jit(solution)/shard_map/reduce_scatter | solution.py:451
  2250.1 1119.4 %reduce-scatter.20.cloned.1.call-start = ((), (), s32[]{:S(2)}) async-start(), calls=%async_computation.25 | async-start | bytes 6758400 | tf_op jit(solution)/shard_map/reduce_scatter | solution.py:448
  2252.8 35.1 copy-start.24
  2626.2 897.2 %reduce-scatter.22.cloned.1.call-start = ((), (), s32[]{:S(2)}) async-start(), calls=%async_computation.26 | async-start | bytes 6758400 | tf_op jit(solution)/shard_map/reduce_scatter | solution.py:449
  2631.3 1046.3 %reduce-scatter.24.cloned.1.call-start = ((), (), s32[]{:S(2)}) async-start(), calls=%async_computation.27 | async-start | bytes 6758400 | tf_op jit(solution)/shard_map/reduce_scatter | solution.py:450
  2661.8 8.6 copy-start.42
  2680.7 119.9 %copy-start.13 = (f32[512,1280]{1,0:T(8,128)S(1)}, f32[512,1280]{1,0:T(8,128)}, u32[]{:S(2)}) copy-start(f32[512,1280]{1,0:T(8,128)} %copy-done.11) | copy-start | bytes 7864324
  (64 other events, 241.4 us)
Sparse Core Ops, SparseCore 0:
  10.9 59.7 all-gather.17
  73.5 58.2 all-gather.15
  134.6 58.2 all-gather.11
  194.9 147.5 all-gather.19
  345.0 149.1 all-gather.13
  496.9 59.6 all-gather.21
  1641.3 303.5 all-gather.23
  1947.7 56.1 all-gather.25
  2006.7 56.1 all-gather.27
  2166.8 152.7 all-gather.31
  2322.3 151.7 all-gather.29
  2476.5 49.1 reduce-scatter.27
  2528.4 46.9 reduce-scatter.29
  2577.9 46.9 reduce-scatter.31
  2627.7 140.3 reduce-scatter.33
  2770.9 143.4 reduce-scatter.35
  2917.2 143.1 reduce-scatter.37
  3063.2 151.5 reduce-scatter.25
  3217.7 151.7 reduce-scatter.19
  3372.3 151.0 reduce-scatter.21
  3526.4 151.1 reduce-scatter.23
where the time goes:
time: 3700 us; the launch traced here: 3680 us
  waiting for transfers between devices  2400 us (65%)
  matrix products  494 us (13%)
  blocking collectives  292 us (8%)
  local copies, waits for them, and re-layouts  247 us (7%)
  other arithmetic  146 us (4%)
  starting transfers between devices  87.2 us (2%)
    all_gather x1, waiting for transfers between devices, shards(): lax.all_gather(shared_gate, ('dp', 'ep'), axis=0, tiled=True)  303 us
    unnamed x24, waiting for transfers between devices  261 us
    all_to_all x1, waiting for transfers between devices, shards(): lax.all_to_all(grad_sent, 'ep', split_axis=0, concat_axis=0, tiled=True)  256 us
    all_to_all x1, waiting for transfers between devices, shards(): lax.all_to_all(grad_send, 'ep', split_axis=0, concat_axis=0, tiled=True)  238 us
    all_to_all x1, waiting for transfers between devices, shards(): lax.all_to_all(send, 'ep', split_axis=0, concat_axis=0, tiled=True)  227 us
    unnamed x2, blocking collectives  156 us
    reduce_scatter x1, waiting for transfers between devices, shards(): lax.psum_scatter(grad_full_query, ('dp', 'ep'), scatter_dimension=0, tile...  155 us
    reduce_scatter x1, waiting for transfers between devices, shards(): lax.psum_scatter(grad_full_out, ('dp', 'ep'), scatter_dimension=0, tiled=...  154 us
  transfers between devices with their start and end apart: 25, of which 18 were waited for; matrix products, arithmetic and copies ran while one was open for 18% of the time, Pallas kernels for 0%

commit v1 on v0

v1 whole, which is shorter than its diff:
```python
import math

import jax
import jax.numpy as jnp
from jax import lax
from jax.experimental import pallas as pl
from jax.experimental.pallas import tpu as pltpu
from jax.sharding import PartitionSpec as P

HEADS = 10
HEAD = 128
MAIN = 8
epsilon = 1e-06
negative = -1e30
bf16 = jnp.bfloat16
f32 = jnp.float32
VMEM_LIMIT = 64 * 1024 * 1024 - 128 * 1024


def dot(a, b):
    return jnp.dot(a, b, preferred_element_type=f32)


def dot_nt(a, b):
    return lax.dot_general(a, b, (((1,), (1,)), ((), ())), preferred_element_type=f32)


def dot_tn(a, b):
    return lax.dot_general(a, b, (((0,), (0,)), ((), ())), preferred_element_type=f32)


def tie(*values):
    return lax.optimization_barrier(values)


def after(value, *others):
    return lax.optimization_barrier((value, others))[0]


def cycle_of(size):
    if size == 16:
        return [0, 1, 2, 3, 7, 6, 5, 9, 10, 11, 15, 14, 13, 12, 8, 4]
    return list(range(0, size, 2)) + list(range(size - 1, 0, -2))


def spec(shape, index, single=False):
    if single:
        return pl.BlockSpec(shape, index, pipeline_mode=pl.Buffered(1))
    return pl.BlockSpec(shape, index)


class Ring:
    def __init__(self, size):
        self.size = size
        self.half = size // 2
        self.order = cycle_of(size)
        place = [0] * size
        for at, member in enumerate(self.order):
            place[member] = at
        self.forward = [(self.order[i], self.order[(i + 1) % size]) for i in range(size)]
        self.backward = [(self.order[i], self.order[(i - 1) % size]) for i in range(size)]
        self.place = jnp.array(place, jnp.int32)[lax.axis_index("ep")]

    def member(self, offset):
        return jnp.array(self.order, jnp.int32)[(self.place + offset) % self.size]

    def step(self, up, down, number):
        if number == self.half:
            cut = up.shape[0] // 2
            up, down = up[:cut], down[cut:]
        return lax.ppermute(up, "ep", self.forward), lax.ppermute(down, "ep", self.backward)

    def gather(self, own, visit):
        up, down, arrived, done = own, own, (own,), None
        for step in range(1, self.half + 1):
            if done is not None:
                up, down, done = lax.optimization_barrier((up, down, done))
            up, down = self.step(up, down, step)
            done = visit(step - 1, arrived)
            arrived = (up, down)
        visit(self.half, arrived)

    def scatter_step(self, parts, came, number):
        cut = parts[0].shape[0] // 2
        away = self.half - number + 1
        if number == 1:
            up, down = parts[away][:cut], parts[away][cut:]
        else:
            ahead, behind = parts[away], parts[-away]
            up, down = came
            if number == 2:
                up = jnp.concatenate([(ahead[:cut].astype(f32) + up.astype(f32)).astype(bf16), ahead[cut:]], axis=0)
                down = jnp.concatenate([behind[:cut], (behind[cut:].astype(f32) + down.astype(f32)).astype(bf16)], axis=0)
            else:
                up = (ahead.astype(f32) + up.astype(f32)).astype(bf16)
                down = (behind.astype(f32) + down.astype(f32)).astype(bf16)
        return lax.ppermute(up, "ep", self.forward), lax.ppermute(down, "ep", self.backward)

    def scatter_end(self, parts, came):
        return parts[0].astype(f32) + came[0].astype(f32) + came[1].astype(f32)


def qkv_kernel(base_ref, tok_ref, gain_ref, w_ref, cos_ref, sin_ref, *rest):
    hid_ref, qkv_ref = rest[-2:]
    x = tok_ref[...].astype(f32)
    inverse = lax.rsqrt(jnp.mean(x * x, axis=-1, keepdims=True) + epsilon)
    hidden = (x * inverse * gain_ref[...]).astype(bf16)
    hid_ref[...] = hidden
    out = dot(hidden, w_ref[...])
    cosine, sine = cos_ref[...], sin_ref[...]
    for slot in range(6):
        u = out[:, slot * HEAD : (slot + 1) * HEAD]
        if slot % 3 != 2:
            u = u * cosine + pltpu.roll(u, HEAD // 2, 1) * sine
        qkv_ref[:, slot * HEAD : (slot + 1) * HEAD] = u.astype(bf16)


def qkv_piece(base, piece, tile, gain, w_cat, cosine, sine, buffers):
    rows, width = piece.shape
    length = cosine.shape[0]
    cols = w_cat.shape[1]
    aliased = () if buffers is None else tuple(buffers)
    n_in = 6
    return pl.pallas_call(
        qkv_kernel,
        out_shape=(jax.ShapeDtypeStruct((length, width), bf16), jax.ShapeDtypeStruct((length, cols), bf16)),
        grid_spec=pltpu.PrefetchScalarGridSpec(
            num_scalar_prefetch=1,
            grid=(rows // tile,),
            in_specs=[
                pl.BlockSpec((tile, width), lambda i, b: (i, 0)),
                pl.BlockSpec((1, width), lambda i, b: (0, 0)),
                pl.BlockSpec((width, cols), lambda i, b: (0, 0)),
                pl.BlockSpec((tile, HEAD), lambda i, b: (b[0] + i, 0)),
                pl.BlockSpec((tile, HEAD), lambda i, b: (b[0] + i, 0)),
            ]
            + [pl.BlockSpec(memory_space=pl.ANY)] * len(aliased),
            out_specs=[
                pl.BlockSpec((tile, width), lambda i, b: (b[0] + i, 0)),
                pl.BlockSpec((tile, cols), lambda i, b: (b[0] + i, 0)),
            ],
        ),
        input_output_aliases={n_in + i: i for i in range(len(aliased))},
        compiler_params=pltpu.CompilerParams(vmem_limit_bytes=32 * 1024 * 1024),
        cost_estimate=pl.CostEstimate(
            flops=2 * rows * width * cols, bytes_accessed=4 * rows * width + 2 * (rows + width) * cols, transcendentals=0
        ),
        name="norm_project_rotate",
    )(base, piece, gain, w_cat, cosine, sine, *aliased)


def attention_forward(own, qkv, blocks, rows, main_rows, side_rows):
    scale = math.log2(math.e) / math.sqrt(HEAD)
    length = qkv.shape[0]
    tall = main_rows + side_rows

    def kernel(own_ref, qkv_ref, low_ref, att_ref, lse_ref):
        block = pl.program_id(0)

        def piece(col, offset, count):
            first = pl.multiple_of(block * rows + offset, 32)
            return qkv_ref[pl.ds(first, count), col : col + HEAD]

        offsets = (own_ref[0], own_ref[1])
        counts = (main_rows, side_rows)
        queries = [piece(3 * HEAD * i, offsets[i], counts[i]) for i in range(2)]

        def step(i, at, state, diagonal):
            best, total, acc = state
            first = pl.multiple_of(at * rows, rows)
            col = 3 * HEAD * i
            keys = qkv_ref[pl.ds(first, rows), col + HEAD : col + 2 * HEAD]
            values = qkv_ref[pl.ds(first, rows), col + 2 * HEAD : col + 3 * HEAD]
            scores = dot_nt(queries[i], keys) * scale
            if diagonal:
                q_at = lax.broadcasted_iota(jnp.int32, scores.shape, 0) + offsets[i]
                k_at = lax.broadcasted_iota(jnp.int32, scores.shape, 1)
                scores = jnp.where(q_at >= k_at, scores, negative)
            top = jnp.maximum(best, jnp.max(scores, axis=1, keepdims=True))
            weights = jnp.exp2(scores - top)
            factor = jnp.exp2(best - top)
            total = total * factor + jnp.sum(weights, axis=1, keepdims=True)
            acc = acc * factor + dot(weights.astype(bf16), values)
            return top, total, acc

        def both(at, states, diagonal=False):
            return tuple(step(i, at, states[i], diagonal) for i in range(2))

        start = tuple(
            (jnp.full((c, 1), negative, f32), jnp.zeros((c, 1), f32), jnp.zeros((c, HEAD), f32)) for c in counts
        )
        states = lax.fori_loop(0, block, both, start)
        states = both(block, states, True)
        at = 0
        for i in range(2):
            best, total, acc = states[i]
            attended = acc / total
            low_ref[0, at : at + counts[i]] = attended.astype(bf16)
            att_ref[0, at : at + counts[i]] = attended
            lse = jnp.broadcast_to(best + jnp.log2(total), (counts[i], HEAD))
            lse_ref[0, :, at : at + counts[i]] = jnp.transpose(lse)[0:8]
            at += counts[i]

    return pl.pallas_call(
        kernel,
        out_shape=(
            jax.ShapeDtypeStruct((blocks, tall, HEAD), bf16),
            jax.ShapeDtypeStruct((blocks, tall, HEAD), f32),
            jax.ShapeDtypeStruct((blocks, 8, tall), f32),
        ),
        grid_spec=pltpu.PrefetchScalarGridSpec(
            num_scalar_prefetch=1,
            grid=(blocks,),
            in_specs=[spec((length, qkv.shape[1]), lambda s, o: (0, 0), True)],
            out_specs=[
                pl.BlockSpec((1, tall, HEAD), lambda s, o: (s, 0, 0)),
                pl.BlockSpec((1, tall, HEAD), lambda s, o: (s, 0, 0)),
                pl.BlockSpec((1, 8, tall), lambda s, o: (s, 0, 0)),
            ],
        ),
        compiler_params=pltpu.CompilerParams(vmem_limit_bytes=48 * 1024 * 1024),
        cost_estimate=pl.CostEstimate(
            flops=4 * length * tall * blocks * HEAD // 2, bytes_accessed=16 * length * HEAD, transcendentals=length * tall * blocks // 2
        ),
        name="attention_forward",
    )(own, qkv)


def attention_backward(own, qkv, grads, attended, lse, cosine, sine, blocks, rows, count, slot, start):
    scale = 1.0 / math.sqrt(HEAD)
    scale_two = math.log2(math.e) * scale
    length = qkv.shape[0]
    tall = grads.shape[1]
    cols = 3 * HEAD
    here = slice(start, start + count)

    def kernel(own_ref, qkv_ref, grad_ref, att_ref, lse_ref, cos_ref, sin_ref, out_ref, key_sum, value_sum):
        block = pl.program_id(0)
        offset = own_ref[slot]

        @pl.when(block == 0)
        def _():
            key_sum[...] = jnp.zeros_like(key_sum)
            value_sum[...] = jnp.zeros_like(value_sum)
            if count < rows:
                out_ref[:, :HEAD] = jnp.zeros((length, HEAD), bf16)

        mine = pl.multiple_of(block * rows + offset, 32)
        queries = qkv_ref[pl.ds(mine, count), :HEAD]
        grad = grad_ref[0, here]
        lse_row = lse_ref[0, 0:1, here]
        product = grad.astype(f32) * att_ref[0, here]
        delta = jnp.sum(jnp.transpose(product), axis=0, keepdims=True)

        def step(at, dq, diagonal=False):
            first = pl.multiple_of(at * rows, rows)
            keys = qkv_ref[pl.ds(first, rows), HEAD : 2 * HEAD]
            values = qkv_ref[pl.ds(first, rows), 2 * HEAD :]
            scores = dot_nt(keys, queries) * scale_two
            if diagonal:
                k_at = lax.broadcasted_iota(jnp.int32, scores.shape, 0)
                q_at = lax.broadcasted_iota(jnp.int32, scores.shape, 1) + offset
                scores = jnp.where(q_at >= k_at, scores, negative)
            probs = jnp.exp2(scores - lse_row)
            grad_probs = dot_nt(values, grad)
            grad_scores = (probs * (grad_probs - delta)).astype(bf16)
            value_sum[pl.ds(first, rows)] += dot(probs.astype(bf16), grad)
            key_sum[pl.ds(first, rows)] += dot(grad_scores, queries)
            return dq + dot_tn(grad_scores, keys)

        dq = step(block, lax.fori_loop(0, block, step, jnp.zeros((count, HEAD), f32)), True)

        def turn_back(value, first, size):
            cosine_part = cos_ref[pl.ds(first, size)]
            sine_part = sin_ref[pl.ds(first, size)]
            value = value * scale
            return (value * cosine_part - pltpu.roll(value, HEAD // 2, 1) * sine_part).astype(bf16)

        out_ref[pl.ds(mine, count), :HEAD] = turn_back(dq, mine, count)

        @pl.when(block == blocks - 1)
        def _():
            def finish(at, carry):
                first = pl.multiple_of(at * rows, rows)
                out_ref[pl.ds(first, rows), HEAD : 2 * HEAD] = turn_back(key_sum[pl.ds(first, rows)], first, rows)
                out_ref[pl.ds(first, rows), 2 * HEAD :] = value_sum[pl.ds(first, rows)].astype(bf16)
                return carry

            lax.fori_loop(0, blocks, finish, 0)

    return pl.pallas_call(
        kernel,
        out_shape=jax.ShapeDtypeStruct((length, cols), bf16),
        grid_spec=pltpu.PrefetchScalarGridSpec(
            num_scalar_prefetch=1,
            grid=(blocks,),
            in_specs=[
                spec((length, cols), lambda s, o: (0, slot), True),
                pl.BlockSpec((1, tall, HEAD), lambda s, o: (s, 0, 0)),
                pl.BlockSpec((1, tall, HEAD), lambda s, o: (s, 0, 0)),
                pl.BlockSpec((1, 8, tall), lambda s, o: (s, 0, 0)),
                spec((length, HEAD), lambda s, o: (0, 0), True),
                spec((length, HEAD), lambda s, o: (0, 0), True),
            ],
            out_specs=spec((length, cols), lambda s, o: (0, 0), True),
            scratch_shapes=[pltpu.VMEM((length, HEAD), f32)] * 2,
        ),
        compiler_params=pltpu.CompilerParams(vmem_limit_bytes=40 * 1024 * 1024),
        cost_estimate=pl.CostEstimate(
            flops=10 * length * count * blocks * HEAD // 2, bytes_accessed=20 * length * HEAD, transcendentals=length * count * blocks // 2
        ),
        name="attention_backward",
    )(own, qkv, grads, attended, lse, cosine, sine)


def expert_call(sources, hidden, grads, rank_row, rank_col, route, w_gate, w_up, w_down, capacity, first, total, buffers):
    count = len(hidden)
    rows, width = hidden[0].shape
    local, _, inner = w_gate.shape
    aliased = () if buffers is None else tuple(buffers)
    widths = (width, width, inner, inner, inner)

    def kernel(sources_ref, *refs):
        h_refs, z_refs, row_refs, col_refs, gate_refs = (refs[i * count : (i + 1) * count] for i in range(5))
        wg_ref, wu_ref, wd_ref = refs[5 * count : 5 * count + 3]
        rest = refs[5 * count + 3 + len(aliased) :]
        outs_y, outs_x = rest[:count], rest[count : 2 * count]
        x_ref, dy_ref, a_ref, dg_ref, du_ref, keep_y, keep_x = rest[2 * count :]
        expert = pl.program_id(0)
        for p in range(count):
            slots = lax.broadcasted_iota(jnp.int32, (capacity, rows), 0).astype(f32)
            hit = slots == row_refs[p][0, expert]
            pick = jnp.where(hit, 1.0, 0.0).astype(bf16)
            gate = jnp.sum(jnp.where(hit, gate_refs[p][0, expert], 0.0), axis=1, keepdims=True)
            x = dot(pick, h_refs[p][...]).astype(bf16)
            dy = (dot(pick, z_refs[p][...]) * gate).astype(bf16)
            x_ref[0, p] = x
            dy_ref[0, p] = dy
            g = dot(x, wg_ref[0])
            u = dot(x, wu_ref[0])
            sigma = 1.0 / (1.0 + jnp.exp(-g))
            act = g * sigma
            a = (act * u).astype(bf16)
            a_ref[0, p] = a
            da = dot_nt(dy, wd_ref[0])
            du = (da * act).astype(bf16)
            dg = (da * u * sigma * (1.0 + g * (1.0 - sigma))).astype(bf16)
            du_ref[0, p] = du
            dg_ref[0, p] = dg
            y = dot(a, wd_ref[0]).astype(bf16)
            at = pl.multiple_of(expert * capacity, 16)
            keep_y[p, pl.ds(at, capacity)] = (y.astype(f32) * gate).astype(bf16)
            dx = dot_nt(dg, wg_ref[0]) + dot_nt(du, wu_ref[0])
            keep_x[p, pl.ds(at, capacity)] = dx.astype(bf16)

        @pl.when(expert == local - 1)
        def _():
            for p in range(count):
                slots = lax.broadcasted_iota(jnp.int32, (rows, capacity), 1).astype(f32)
                place = jnp.concatenate(
                    [jnp.where(slots == col_refs[p][0, e], 1.0, 0.0).astype(bf16) for e in range(local)], axis=1
                )
                outs_y[p][...] = dot(place, keep_y[p]).astype(bf16)
                outs_x[p][...] = dot(place, keep_x[p]).astype(bf16)

    piece = jax.ShapeDtypeStruct((rows, width), bf16)
    by_expert = lambda e, s: (e, 0, 0)
    slot = lambda e, s: (e, first // count, 0, 0)

    def of_source(shape):
        zeros = (0,) * (len(shape) - 1)
        return [pl.BlockSpec(shape, lambda e, s, p=p: (s[p],) + zeros, pipeline_mode=pl.Buffered(1)) for p in range(count)]

    return pl.pallas_call(
        kernel,
        out_shape=[piece] * (2 * count) + [jax.ShapeDtypeStruct((local, total, capacity, w), bf16) for w in widths],
        grid_spec=pltpu.PrefetchScalarGridSpec(
            num_scalar_prefetch=1,
            grid=(local,),
            in_specs=[spec((rows, width), lambda e, s: (0, 0), True)] * (2 * count)
            + of_source((1, local, 1, rows))
            + of_source((1, local, rows, 1))
            + of_source((1, local, 1, rows))
            + [
                pl.BlockSpec((1, width, inner), by_expert),
                pl.BlockSpec((1, width, inner), by_expert),
                pl.BlockSpec((1, inner, width), by_expert),
            ]
            + [pl.BlockSpec(memory_space=pl.ANY)] * len(aliased),
            out_specs=[spec((rows, width), lambda e, s: (0, 0), True)] * (2 * count)
            + [pl.BlockSpec((1, count, capacity, w), slot) for w in widths],
            scratch_shapes=[pltpu.VMEM((count, local * capacity, width), bf16)] * 2,
        ),
        input_output_aliases={1 + 5 * count + 3 + i: 2 * count + i for i in range(len(aliased))},
        compiler_params=pltpu.CompilerParams(vmem_limit_bytes=VMEM_LIMIT),
        cost_estimate=pl.CostEstimate(
            flops=count * 2 * local * capacity * width * (6 * inner + 4 * rows),
            bytes_accessed=2 * local * (3 * width * inner + count * capacity * (2 * width + 3 * inner)) + count * 8 * rows * width,
            transcendentals=count * local * capacity * inner,
        ),
        name="experts",
    )(
        sources,
        *hidden,
        *grads,
        *[rank_row] * count,
        *[rank_col] * count,
        *[route] * count,
        w_gate,
        w_up,
        w_down,
        *aliased,
    )


def swiglu_back(grad_act, gate_pre, up_pre):
    sigma = jax.nn.sigmoid(gate_pre)
    grad_up = (grad_act * gate_pre * sigma).astype(bf16)
    grad_gate = (grad_act * up_pre * sigma * (1.0 + gate_pre * (1.0 - sigma))).astype(bf16)
    return grad_gate, grad_up


def shards(
    tokens, cotangent, expert_ids, keep, gates, norm1_gain, norm2_gain, w_query, w_key, w_value, w_out,
    shared_gate, shared_up, shared_down, expert_gate, expert_up, expert_down,
):
    ep = lax.axis_size("ep")
    me = lax.axis_index("ep")
    ring = Ring(ep)
    half = ring.half
    token_rows = tokens[0]
    grad_low = cotangent[0]
    rows, width = token_rows.shape
    length = rows * ep
    local = expert_gate.shape[0]
    inner = expert_gate.shape[2]
    experts = local * ep
    shard = w_query.shape[0]
    copies = ep // MAIN
    sharers = MAIN // (HEADS - MAIN)
    main_rows = rows // copies
    side_rows = rows // (sharers * copies)
    tall = main_rows + side_rows
    capacity = min(rows, rows * 10 // experts)
    main_part = me % copies
    side_part = ((me // copies) % sharers) * copies + main_part
    own = jnp.stack([main_part * main_rows, side_part * side_rows]).astype(jnp.int32)

    gains = jnp.concatenate([norm1_gain[:, None], norm2_gain[:, None], jnp.zeros((shard, HEAD - 2), bf16)], axis=1)
    messages = []
    for member in range(ep):
        main_head = member // copies
        side_head = MAIN + main_head // sharers
        messages.append(
            jnp.concatenate(
                [
                    weight[:, head * HEAD : (head + 1) * HEAD]
                    for head in (main_head, side_head)
                    for weight in (w_query, w_key, w_value)
                ]
                + [gains],
                axis=1,
            )
        )
    head_rows = lax.all_to_all(jnp.stack(messages), "ep", 0, 0, tiled=True)

    chosen = expert_ids[0][:, :, None] == jnp.arange(experts, dtype=jnp.int32)[None, None, :]
    weight_here = gates[0] * keep[0].astype(f32)
    route = jnp.sum(jnp.where(chosen, weight_here[:, :, None], 0.0), axis=1)
    route = lax.all_to_all(route.T.reshape(ep, local, rows), "ep", 0, 0, tiled=True)
    used = route > 0.0
    before = (jnp.arange(rows)[:, None] < jnp.arange(rows)[None, :]).astype(bf16)
    rank = dot(used.astype(bf16).reshape(ep * local, rows), before).reshape(ep, local, rows)
    rank = jnp.where(used, rank, -1.0)

    freqs = jnp.exp(jnp.arange(HEAD // 2, dtype=f32) * (-2.0 * math.log(10000.0) / HEAD))
    turned = jnp.arange(length, dtype=jnp.int32).astype(f32)[:, None] * freqs[None, :]
    cosine, sine = jnp.cos(turned), jnp.sin(turned)
    cosine = jnp.concatenate([cosine, cosine], axis=1)
    sine = jnp.concatenate([-sine, sine], axis=1)

    tile = rows // 2
    arrivals, known = [], {}

    def project(steps):
        for step in steps:
            for i, part in enumerate(arrivals[step]):
                offset = 0 if step == 0 else (half if step == half else (-step, step)[i])
                base = 2 * ring.member(offset) + (i if step == half else 0)
                known["buffers"] = qkv_piece(
                    base.astype(jnp.int32).reshape(1), part, tile, known["gains"][0], known["w_cat"], cosine, sine,
                    known.get("buffers"),
                )

    up, down = token_rows, token_rows
    arrivals.append((token_rows,))
    for step in range(1, half + 1):
        up, down = ring.step(up, down, step)
        if step == 1:
            head_rows, up, down = tie(head_rows, up, down)
            head_weights = lax.all_gather(head_rows.reshape(ep * shard, 7 * HEAD), "dp", axis=0, tiled=True)
            gain_rows = head_weights[:, 6 * HEAD : 6 * HEAD + 2].astype(f32).T
            gain_one, gain_two = gain_rows[0:1], gain_rows[1:2]
            w_cat = head_weights[:, : 6 * HEAD]
            known["gains"], known["w_cat"] = (gain_one, gain_two), w_cat
        if step == 2:
            route, rank, up, down = tie(route, rank, up, down)
        if step == half - 1:
            project(range(half - 1))
            packed = jnp.concatenate([w_out, shared_gate, shared_up, shared_down.T], axis=1)
            up, down, packed, known["buffers"] = tie(up, down, packed, known["buffers"])
            packed = lax.all_gather(packed, "ep", axis=0, tiled=True)
        arrivals.append((up, down))
    project([half - 1, half])
    hidden_all, qkv = known["buffers"]

    grad_pieces = {0: (grad_low,)}
    grad_low, qkv = tie(grad_low, qkv)
    grad_pieces[1] = ring.step(grad_low, grad_low, 1)

    low, attended, lse = attention_forward(own, qkv, ep, rows, main_rows, side_rows)
    low, grad_pieces[1], packed = tie(low, grad_pieces[1], packed)
    full_out = lax.all_gather(packed[:, :width], "dp", axis=0, tiled=True)
    grad_pieces[2] = ring.step(*grad_pieces[1], 2)
    heads_in = lax.all_to_all(low, "ep", 0, 0, tiled=True)
    main_in = heads_in[:, :main_rows].reshape(MAIN, rows, HEAD)
    side_in = heads_in[:, main_rows:].reshape(HEADS - MAIN, rows, HEAD)
    attended_low = jnp.concatenate([main_in, side_in], axis=0).transpose(1, 0, 2).reshape(rows, width)

    residual = token_rows.astype(f32)
    middle = residual + dot(attended_low, full_out)
    inverse_two = lax.rsqrt(jnp.mean(middle * middle, axis=-1, keepdims=True) + epsilon)
    normed_two = middle * inverse_two
    hidden_two = (normed_two * gain_two).astype(bf16)

    hidden_two, grad_pieces[2], packed = tie(hidden_two, grad_pieces[2], packed)
    packed = lax.all_gather(packed[:, width:], "dp", axis=0, tiled=True)
    full_gate = packed[:, :inner]
    full_up = packed[:, inner : 2 * inner]
    full_down_t = packed[:, 2 * inner :]

    rank_row, rank_col, route_row = rank[:, :, None, :], rank[:, :, :, None], route[:, :, None, :]
    part_y, part_x, buffers = {}, {}, [None]

    def run_experts(step, arrived):
        grads = grad_pieces[step]
        if step == half:
            group, first = (half,), ep - 1
        elif step == 0:
            group, first = (0,), ep - 2
        else:
            group, first = (-step, step), 2 * (step - 1)
        outs = expert_call(
            jnp.stack([ring.member(offset) for offset in group]).astype(jnp.int32),
            arrived,
            grads,
            rank_row,
            rank_col,
            route_row,
            expert_gate,
            expert_up,
            expert_down,
            capacity,
            first,
            ep,
            buffers[0],
        )
        for i, offset in enumerate(group):
            part_y[offset] = outs[i]
            part_x[offset] = outs[len(group) + i]
        buffers[0] = outs[2 * len(group) :]
        return outs[len(group)]

    def run_shared(hidden, grads):
        gate_pre = dot(hidden, full_gate)
        up_pre = dot(hidden, full_up)
        act = (jax.nn.silu(gate_pre) * up_pre).astype(bf16)
        grad_gate_pre, grad_up_pre = swiglu_back(dot(grads, full_down_t), gate_pre, up_pre)
        back = dot_nt(grad_gate_pre, full_gate) + dot_nt(grad_up_pre, full_up)
        grads_in = dot_tn(hidden, jnp.concatenate([grad_gate_pre, grad_up_pre], axis=1)).astype(bf16)
        return dot_nt(act, full_down_t), back, grads_in, dot_tn(grads, act).astype(bf16)

    up, down, arrived = hidden_two, hidden_two, (hidden_two,)
    for step in range(1, half + 1):
        if step < half:
            up, down = ring.step(up, down, step)
            if step >= 4:
                grad_pieces[step] = ring.step(*grad_pieces[step - 1], step)
        else:
            up = lax.ppermute(up, "ep", ring.forward)
            grad_pieces[step] = (lax.ppermute(grad_pieces[step - 1][1], "ep", ring.backward),)
        done = run_experts(step - 1, arrived)
        up, down, done, grad_pieces[step] = tie(up, down, done, grad_pieces[step])
        if step == 2:
            hidden_two, grad_low, done = tie(hidden_two, grad_low, done)
            shared = run_shared(hidden_two, grad_low)
            arrived = (up, down)
            if half > 3:
                grad_pieces[3] = ring.step(*grad_pieces[2], 3)
                grad_pieces[3], done, shared, arrived = tie(grad_pieces[3], done, shared, arrived)
            else:
                done, shared, arrived = tie(done, shared, arrived)
            dense = [lax.psum_scatter(item, "dp", scatter_dimension=0, tiled=True) for item in shared[2:]]
        else:
            arrived = (up, down) if step < half else (up,)
        if step == half:
            done, dense = tie(done, dense)
        part_x[(0 if step == 1 else 1 - step)] = done
    run_experts(half, arrived)
    shared_branch, grad_shared = shared[:2]
    saved_x, saved_dy, saved_a, saved_dg, saved_du = [
        item.reshape(local, ep * capacity, item.shape[-1]) for item in buffers[0]
    ]

    def by_rows(left, right):
        return jnp.einsum("ecd,ecf->edf", left, right, preferred_element_type=f32).astype(bf16)

    came, expert_grads = None, []
    for step in range(1, half + 1):
        came = ring.scatter_step(part_x, came, step)
        if step <= 3:
            left, right = ((saved_x, saved_dg), (saved_x, saved_du), (saved_dy, saved_a))[step - 1]
            item = by_rows(left, right)
            came, item = tie(came, item)
            if step < 3:
                item = lax.psum_scatter(item, "dp", scatter_dimension=1, tiled=True)
            expert_grads.append(item)
    came, expert_grads[0] = tie(came, expert_grads[0])
    grad_routed = ring.scatter_end(part_x, came)
    grad_hidden_two = grad_shared + grad_routed
    grad_gain_two = jnp.sum(grad_hidden_two * normed_two, axis=0)
    scaled = grad_hidden_two * gain_two
    grad_out = grad_low.astype(f32)
    grad_middle = grad_out + inverse_two * (
        scaled - normed_two * jnp.mean(scaled * normed_two, axis=-1, keepdims=True)
    )
    grad_branch = grad_middle.astype(bf16)
    grad_attended = dot_nt(grad_branch, full_out).astype(bf16)

    by_head = grad_attended.reshape(rows, HEADS, HEAD).transpose(1, 0, 2)
    heads_out = jnp.concatenate(
        [by_head[:MAIN].reshape(ep, main_rows, HEAD), by_head[MAIN:].reshape(ep, side_rows, HEAD)], axis=1
    )
    part_y[half], grad_routed = tie(part_y[half], grad_routed)
    came_y = ring.scatter_step(part_y, None, 1)
    heads_out, attended_low, grad_branch, grad_gain_two, came_y = tie(
        heads_out, attended_low, grad_branch, grad_gain_two, came_y
    )
    came_y = ring.scatter_step(part_y, came_y, 2)
    head_grads = lax.all_to_all(heads_out, "ep", 0, 0, tiled=True)
    grad_full_out = dot_tn(attended_low, grad_branch).astype(bf16)

    gain_high = grad_gain_two.astype(bf16)
    gain_rest = (grad_gain_two - gain_high.astype(f32)).astype(bf16)
    gain_columns = dot_tn(jnp.stack([gain_high, gain_rest]), jnp.eye(2, HEAD, dtype=bf16))
    head_grads, came_y, grad_full_out, expert_grads[1] = tie(head_grads, came_y, grad_full_out, expert_grads[1])
    dense.append(lax.psum_scatter(grad_full_out, "dp", scatter_dimension=0, tiled=True))
    for step in range(3, half):
        came_y = ring.scatter_step(part_y, came_y, step)
    grad_side = attention_backward(
        own, qkv, head_grads, attended, lse, cosine, sine, ep, rows, side_rows, 1, main_rows
    )
    grad_side, came_y, qkv, dense = tie(grad_side, came_y, qkv, dense)
    dense = lax.psum_scatter(jnp.concatenate(dense, axis=1), "ep", scatter_dimension=0, tiled=True).astype(f32)
    came_y = ring.scatter_step(part_y, came_y, half)
    grad_main = attention_backward(
        own, qkv, head_grads, attended, lse, cosine, sine, ep, rows, main_rows, 0, 0
    )
    grad_main, came_y = tie(grad_main, came_y)

    part_h = {}
    for offset in range(-half + 1, half + 1):
        first = ring.member(offset) * rows
        part_h[offset] = (
            dot_nt(lax.dynamic_slice_in_dim(grad_main, first, rows, 0), w_cat[:, : 3 * HEAD])
            + dot_nt(lax.dynamic_slice_in_dim(grad_side, first, rows, 0), w_cat[:, 3 * HEAD :])
        ).astype(bf16)
    hidden_all, part_h[half] = tie(hidden_all, part_h[half])
    head_sums = jnp.concatenate([dot_tn(hidden_all, grad_main), dot_tn(hidden_all, grad_side), gain_columns], axis=1)
    head_sums = head_sums.astype(bf16)
    came = None
    for step in range(1, half + 1):
        came = ring.scatter_step(part_h, came, step)
        if step == 1:
            next_parts = [part_h[offset] for offset in (half - 1, 1 - half)]
            came, head_sums, next_parts = tie(came, head_sums, next_parts)
            part_h[half - 1], part_h[1 - half] = next_parts
            head_sums = lax.psum_scatter(head_sums, "dp", scatter_dimension=0, tiled=True)
        if step == 2:
            came, part_h = tie(came, part_h)
        if step == 3:
            came, head_sums, dense, last = tie(came, head_sums, dense, expert_grads[2])
            head_sums = lax.all_to_all(head_sums.reshape(ep, shard, 7 * HEAD), "ep", 0, 0, tiled=True)
            expert_grads[2] = lax.psum_scatter(last, "dp", scatter_dimension=1, tiled=True)
    head_sums = head_sums.astype(f32)
    grad_hidden_one = ring.scatter_end(part_h, came)
    output = (middle + shared_branch + ring.scatter_end(part_y, came_y)).astype(bf16)
    main_sums = head_sums[:, :, : 3 * HEAD].reshape(MAIN, copies, shard, 3, HEAD).sum(1)
    gain_sums = head_sums[:, :, 6 * HEAD] + head_sums[:, :, 6 * HEAD + 1]
    side_sums = head_sums[:, :, 3 * HEAD : 6 * HEAD].reshape(HEADS - MAIN, sharers * copies, shard, 3, HEAD).sum(1)
    head_sums = jnp.concatenate([main_sums, side_sums], axis=0)
    projections = [head_sums[:, :, i].transpose(1, 0, 2).reshape(shard, width) for i in range(3)]
    grad_gain_one = sum(
        jnp.sum(w.astype(f32) * g, axis=1) for w, g in zip((w_query, w_key, w_value), projections)
    ) / norm1_gain.astype(f32)

    inverse_one = lax.rsqrt(jnp.mean(residual * residual, axis=-1, keepdims=True) + epsilon)
    normed_one = residual * inverse_one
    scaled = grad_hidden_one * gain_one
    grad_input = grad_middle + inverse_one * (
        scaled - normed_one * jnp.mean(scaled * normed_one, axis=-1, keepdims=True)
    )
    return (
        output[None],
        grad_input[None],
        grad_gain_one,
        gain_sums.sum(0),
        projections[0],
        projections[1],
        projections[2],
        dense[:, 3 * inner : 3 * inner + width],
        dense[:, :inner],
        dense[:, inner : 2 * inner],
        dense[:, 2 * inner : 3 * inner].T,
        expert_grads[0].astype(f32),
        expert_grads[1].astype(f32),
        expert_grads[2].astype(f32).transpose(0, 2, 1),
    )


def solution(mesh):
    by_token = P("dp", "ep", None)
    by_row = P(("dp", "ep"), None)
    in_specs = (
        (by_token,) * 5
        + (P(("dp", "ep")),) * 2
        + (by_row,) * 6
        + (P(None, ("dp", "ep")),)
        + (P("ep", None, None),) * 3
    )
    out_specs = (
        (by_token,) * 2
        + (P(("dp", "ep")),) * 2
        + (by_row,) * 6
        + (P(None, ("dp", "ep")), P("ep", "dp", None), P("ep", "dp", None), P("ep", None, "dp"))
    )
    return jax.shard_map(shards, mesh=mesh, in_specs=in_specs, out_specs=out_specs, check_vma=False)
```

time: 3700 us -> 963 us (0.26)
  waiting for transfers between devices: 2400 us -> 198 us
  matrix products: 494 us -> 148 us
  Pallas kernels: 0 us -> 295 us
  blocking collectives: 292 us -> 37.2 us
  local copies, waits for them, and re-layouts: 247 us -> 73.3 us
  other arithmetic: 146 us -> 99.7 us
    all_gather x11 -> x4, waiting for transfers between devices: 801 us -> 0.06 us  [the longest x1 0.02 us: shards(): full_out = lax.all_gather(packed[:, :width], 'dp', axis=0, tiled=True)]
    all_to_all x4, waiting for transfers between devices: 722 us -> 27 us  [the longest x1 23.1 us: shards(): heads_in = lax.all_to_all(low, 'ep', 0, 0, tiled=True)]
    reduce_scatter x7 -> x6, waiting for transfers between devices: 617 us -> 0.03 us  [the longest x2 0.02 us: shards(): item = lax.psum_scatter(item, 'dp', scatter_dimension=1, tiled=True)]
    dot_general x63 -> x34, matrix products: 494 us -> 148 us  [the longest x3 60.9 us: by_rows(): jnp.einsum('ecd,ecf->edf', left, right, preferred_element_type=f32)]
    pallas_call x0 -> x17, Pallas kernels: none -> 295 us  [the longest x5 169 us: expert_call(): pl.pallas_call(kernel, out_shape=[piece] * (2 * count) + [jax.ShapeDtypeS...]
    unnamed x24 -> x14, waiting for transfers between devices: 261 us -> 6.91 us
    ppermute x0 -> x46, waiting for transfers between devices: none -> 164 us  [the longest x12 79.7 us: scatter_step(): lax.ppermute(down, 'ep', self.backward)]
    unnamed x2 -> x0, blocking collectives: 156 us -> none
  transfers between devices with their start and end apart: 25 -> 62, of which waited for: 18 -> 21; matrix products, arithmetic and copies ran while one was open for 18% -> 30% of each run, Pallas kernels for 0% -> 31%
where the time goes in v1:
time: 963 us; the launch traced here: 956 us
  Pallas kernels  295 us (31%)
  waiting for transfers between devices  198 us (21%)
  matrix products  148 us (15%)
  other arithmetic  99.7 us (10%)
  local copies, waits for them, and re-layouts  73.3 us (8%)
  starting transfers between devices  71.5 us (7%)
  blocking collectives  37.2 us (4%)
  between operations  32.8 us (3%)
    pallas_call x5, Pallas kernels, expert_call(): pl.pallas_call(kernel, out_shape=[piece] * (2 * count) + [jax.ShapeDtypeS...  169 us
    ppermute x12, waiting for transfers between devices, scatter_step(): lax.ppermute(down, 'ep', self.backward)  79.7 us
    dot_general x3, matrix products, by_rows(): jnp.einsum('ecd,ecf->edf', left, right, preferred_element_type=f32)  60.9 us
    pallas_call x2, Pallas kernels, attention_backward(): pl.pallas_call(kernel, out_shape=jax.ShapeDtypeStruct((length, cols), bf1...  60.3 us
    ppermute x12, waiting for transfers between devices, scatter_step(): lax.ppermute(up, 'ep', self.forward)  45.7 us
    dot_general x20, matrix products, dot_nt(): lax.dot_general(a, b, (((1,), (1,)), ((), ())), preferred_element_type=f32)  44.4 us
    pallas_call x1, Pallas kernels, attention_forward(): pl.pallas_call(kernel, out_shape=(jax.ShapeDtypeStruct((blocks, tall, HEA...  40.5 us
    all_to_all x1, blocking collectives, shards(): head_rows = lax.all_to_all(jnp.stack(messages), 'ep', 0, 0, tiled=True)  37.2 us
  transfers between devices with their start and end apart: 62, of which 21 were waited for; matrix products, arithmetic and copies ran while one was open for 30% of the time, Pallas kernels for 31%

profile of v1, /device:TPU:12, one launch (start us, length us, event | category | flops | bytes accessed | tf_op | source)
XLA Modules:
  0.0 956.0 jit_solution(3460028231200843261)
XLA Ops:
  14.4 37.2 %all_to_all.25 = bf16[8,40,896]{2,1,0:T(8,128)(2,1)} all-to-all(bf16[8,40,896]{2,1,0:T(8,128)(2,1)S(1)} %bitcast_dynamic-update-slice_fusion), channel_id=1, replica_groups=mesh['dp'=4,'ep'=8] {'ep'}, dimensions={0} | all-to-all | bytes 1146880 | tf_op jit(solution)/shard_map/all_to_all | solution.py:465
  52.6 5.6 all-to-all-start
  60.2 7.5 fusion.34
  70.4 17.2 %collective-permute-done.2.tok_ref = bf16[512,1280]{1,0:T(8,128)(2,1)} collective-permute-done((bf16[512,1280]{1,0:T(8,128)(2,1)}, bf16[512,1280]{1,0:T(8,128)(2,1)}, u32[]{:S(2)}, u32[]{:S(2)}) %collective-permute-start.2) | collective-permute-done | bytes 1310752 | tf_op jit(solution)/shard_map/ppermute | solution.py:71
  111.9 3.8 norm_project_rotate.10
  118.1 3.6 norm_project_rotate.12
  121.8 3.6 norm_project_rotate.13
  139.2 3.6 norm_project_rotate.14
  142.8 3.7 norm_project_rotate.15
  151.1 4.4 collective-permute-done.6.tok_ref
  163.7 40.5 %attention_forward.1 = (bf16[8,640,128]{2,1,0:T(8,128)(2,1)}, f32[8,640,128]{2,1,0:T(8,128)S(1)}, f32[8,8,640]{2,1,0:T(8,128)S(1)}) custom-call(s32[2]{0:T(128)S(1)} %get-tuple-element.430.own_ref, bf16[4096,768]{1,0:T(8,128)(2,1)} %copy-done.2), custom_call_target="tpu_custom_call" | custom-call | flops 5368709120 | bytes 8388608 | tf_op jit(solution)/shard_map/attention_forward/pallas_call | solution.py:204
  209.0 6.8 all-to-all-start.2
  218.1 23.1 %all-to-all-done.2 = bf16[8,640,128]{2,1,0:T(8,128)(2,1)S(1)} async-done(((bf16[8,640,128]{2,1,0:T(8,128)(2,1)}), bf16[8,640,128]{2,1,0:T(8,128)(2,1)S(1)}, u32[]{:S(2)}, u32[]{:S(2)}) %all-to-all-start.2) | async-done | bytes 1310752 | tf_op jit(solution)/shard_map/all_to_all | solution.py:525
  244.0 4.5 multiply_reduce_fusion.2
  251.4 14.0 %collective-permute-done.10.refs_2_ = bf16[512,1280]{1,0:T(8,128)(2,1)} collective-permute-done((bf16[512,1280]{1,0:T(8,128)(2,1)}, bf16[512,1280]{1,0:T(8,128)(2,1)}, u32[]{:S(2)}, u32[]{:S(2)}) %collective-permute-start.10) | collective-permute-done | bytes 1310752 | tf_op jit(solution)/shard_map/ppermute | solution.py:71
  272.9 24.4 %experts.5 = (bf16[512,1280]{1,0:T(8,128)(2,1)}, bf16[512,1280]{1,0:T(8,128)(2,1)}, bf16[2,8,320,1280]{3,2,1,0:T(8,128)(2,1)}, bf16[2,8,320,1280]{3,2,1,0:T(8,12...) custom-call(s32[1]{0:T(128)} %get-tuple-element.421.sources_ref, ...), custom_call_target="tpu_custom_call" | custom-call | flops 12163481600 | bytes 25722880 | tf_op jit(solution)/shard_map/experts/pallas_call | solution.py:374
  299.3 40.0 %experts.6 = (bf16[512,1280]{1,0:T(8,128)(2,1)}, bf16[512,1280]{1,0:T(8,128)(2,1)}, bf16[512,1280]{1,0:T(8,128)(2,1)}, bf16[512,1280]{1,0:T(8,128)(2,1)}, bf16[2...) custom-call(s32[2]{0:T(128)} %get-tuple-element.431.sources_ref, ...), custom_call_target="tpu_custom_call", output_to_operand_aliasing={{4}: (14, {}), {5}: (15, {}), {6}: (16, {}), {7}: (17, {}),... | custom-call | flops 24326963200 | bytes 37683200 | tf_op jit(solution)/shard_map/experts/pallas_call | solution.py:374
  341.5 3.7 fusion.21
  358.0 4.3 convolution_convert_fusion.5
  362.3 6.3 convolution_convert_fusion.1
  368.6 5.5 convolution_add_fusion.8
  380.7 40.8 %experts.7 = (bf16[512,1280]{1,0:T(8,128)(2,1)}, bf16[512,1280]{1,0:T(8,128)(2,1)}, bf16[512,1280]{1,0:T(8,128)(2,1)}, bf16[512,1280]{1,0:T(8,128)(2,1)}, bf16[2...) custom-call(s32[2]{0:T(128)} %get-tuple-element.432.sources_ref, ...), custom_call_target="tpu_custom_call", output_to_operand_aliasing={{4}: (14, {}), {5}: (15, {}), {6}: (16, {}), {7}: (17, {}),... | custom-call | flops 24326963200 | bytes 37683200 | tf_op jit(solution)/shard_map/experts/pallas_call | solution.py:374
  423.6 41.0 %experts.8 = (bf16[512,1280]{1,0:T(8,128)(2,1)}, bf16[512,1280]{1,0:T(8,128)(2,1)}, bf16[512,1280]{1,0:T(8,128)(2,1)}, bf16[512,1280]{1,0:T(8,128)(2,1)}, bf16[2...) custom-call(s32[2]{0:T(128)} %get-tuple-element.433.sources_ref, ...), custom_call_target="tpu_custom_call", output_to_operand_aliasing={{4}: (14, {}), {5}: (15, {}), {6}: (16, {}), {7}: (17, {}),... | custom-call | flops 24326963200 | bytes 37683200 | tf_op jit(solution)/shard_map/experts/pallas_call | solution.py:374
  464.6 22.6 %experts.9 = (bf16[512,1280]{1,0:T(8,128)(2,1)}, bf16[512,1280]{1,0:T(8,128)(2,1)}, bf16[2,8,320,1280]{3,2,1,0:T(8,128)(2,1)}, bf16[2,8,320,1280]{3,2,1,0:T(8,12...) custom-call(s32[1]{0:T(128)} %get-tuple-element.426.sources_ref, ...), custom_call_target="tpu_custom_call", output_to_operand_aliasing={{2}: (9, {}), {3}: (10, {}), {4}: (11, {}), {5}: (12, {}), ... | custom-call | flops 12163481600 | bytes 25722880 | tf_op jit(solution)/shard_map/experts/pallas_call | solution.py:374
  490.6 19.7 %convolution_convert_fusion.4 = bf16[2,1280,896]{2,1,0:T(8,128)(2,1)} fusion(bf16[2,2560,1280]{2,1,0:T(8,128)(2,1)} %bitcast.136, bf16[2,2560,896]{2,1,0:T(8,128)(2,1)} %bitcast.142), kind=kOutput, calls=%fused_computation.4 | convolution fusion | flops 11746344960 | bytes 26869760 | tf_op jit(solution)/shard_map/ecd,ecf->edf/dot_general | solution.py:616
  515.6 21.2 %convolution_convert_fusion.3 = bf16[2,1280,896]{2,1,0:T(8,128)(2,1)} fusion(bf16[2,2560,1280]{2,1,0:T(8,128)(2,1)} %bitcast.137, bf16[2,2560,896]{2,1,0:T(8,128)(2,1)} %bitcast.143), kind=kOutput, calls=%fused_computation.3 | convolution fusion | flops 11746344960 | bytes 26869760 | tf_op jit(solution)/shard_map/ecd,ecf->edf/dot_general | solution.py:616
  546.4 20.0 %convolution_convert_fusion.2 = bf16[2,1280,896]{2,1,0:T(8,128)(2,1)} fusion(bf16[2,2560,1280]{2,1,0:T(8,128)(2,1)} %bitcast.138, bf16[2,2560,896]{2,1,0:T(8,128)(2,1)} %bitcast.141), kind=kOutput, calls=%fused_computation.2 | convolution fusion | flops 11746344960 | bytes 26869760 | tf_op jit(solution)/shard_map/ecd,ecf->edf/dot_general | solution.py:616
  576.3 17.8 %collective-permute-done.29 = bf16[512,1280]{1,0:T(8,128)(2,1)} collective-permute-done((bf16[512,1280]{1,0:T(8,128)(2,1)}, bf16[512,1280]{1,0:T(8,128)(2,1)}, u32[]{:S(2)}, u32[]{:S(2)}) %collective-permute-start.29) | collective-permute-done | bytes 1310752 | tf_op jit(solution)/shard_map/ppermute | solution.py:97
  596.4 4.0 multiply_reduce_fusion
  604.5 3.9 fusion.101
  614.6 12.2 %collective-permute-done.31 = bf16[256,1280]{1,0:T(8,128)(2,1)} collective-permute-done((bf16[256,1280]{1,0:T(8,128)(2,1)}, bf16[256,1280]{1,0:T(8,128)(2,1)}, u32[]{:S(2)}, u32[]{:S(2)}) %collective-permute-start.31) | collective-permute-done | bytes 655392 | tf_op jit(solution)/shard_map/ppermute | solution.py:97
  629.3 4.3 all-to-all-start.3
  644.6 32.7 %collective-permute-done.32 = bf16[512,1280]{1,0:T(8,128)(2,1)} collective-permute-done((bf16[512,1280]{1,0:T(8,128)(2,1)}, bf16[512,1280]{1,0:T(8,128)(2,1)}, u32[]{:S(2)}, u32[]{:S(2)}) %collective-permute-start.32) | collective-permute-done | bytes 1310752 | tf_op jit(solution)/shard_map/ppermute | solution.py:97
  697.1 22.7 %attention_backward.2 = bf16[4096,384]{1,0:T(8,128)(2,1)S(1)} custom-call(s32[2]{0:T(128)S(1)} %copy-done.26, bf16[4096,768]{1,0:T(8,128)(2,1)} %copy-done.2, bf16[8,640,128]{2,1,0:T(8,128)(2,1)S(1)} %all-to-all-done.3.grad_ref, f32[8,640,128]{2,1,0:T(8,128)S(1)} %copy-done.18, f32[8,8,640]{2,1,0:T(8,128)S(1)} %copy-done.23, f32[4096,128]{1,0:T(8,128)S(1)} %copy-done.4, ...), custom_call_target="tpu_custom_call" | custom-call | flops 2684354560 | bytes 10485760 | tf_op jit(solution)/shard_map/attention_backward/pallas_call | solution.py:291
  733.7 3.8 fusion.38
  749.4 37.6 %attention_backward.3 = bf16[4096,384]{1,0:T(8,128)(2,1)S(1)} custom-call(s32[2]{0:T(128)S(1)} %copy-done.26, bf16[4096,768]{1,0:T(8,128)(2,1)} %copy-done.2, bf16[8,640,128]{2,1,0:T(8,128)(2,1)S(1)} %all-to-all-done.3.grad_ref, f32[8,640,128]{2,1,0:T(8,128)S(1)} %copy-done.19, f32[8,8,640]{2,1,0:T(8,128)S(1)} %copy-done.24, f32[4096,128]{1,0:T(8,128)S(1)} %copy-done.4, ...), custom_call_target="tpu_custom_call" | custom-call | flops 10737418240 | bytes 10485760 | tf_op jit(solution)/shard_map/attention_backward/pallas_call | solution.py:291
  793.1 8.4 convolution_convert_fusion.7
  801.5 4.3 convolution_convert_fusion.8
  819.3 4.4 fusion.8
  828.5 16.1 %collective-permute-done.41 = bf16[512,1280]{1,0:T(8,128)(2,1)} collective-permute-done((bf16[512,1280]{1,0:T(8,128)(2,1)}, bf16[512,1280]{1,0:T(8,128)(2,1)}, u32[]{:S(2)}, u32[]{:S(2)}) %collective-permute-start.41) | collective-permute-done | bytes 1310752 | tf_op jit(solution)/shard_map/ppermute | solution.py:97
  844.5 3.9 collective-permute-done.40
  856.4 6.2 reduce-scatter.25.cloned.1.call-done
  864.8 15.3 %collective-permute-done.43 = bf16[512,1280]{1,0:T(8,128)(2,1)} collective-permute-done((bf16[512,1280]{1,0:T(8,128)(2,1)}, bf16[512,1280]{1,0:T(8,128)(2,1)}, u32[]{:S(2)}, u32[]{:S(2)}) %collective-permute-start.43) | collective-permute-done | bytes 1310752 | tf_op jit(solution)/shard_map/ppermute | solution.py:97
  889.5 4.2 fusion.30
  896.0 4.2 all-to-all-start.4
  908.1 3.9 all-to-all-done.4
  923.1 14.5 %collective-permute-done.45 = bf16[512,1280]{1,0:T(8,128)(2,1)S(1)} collective-permute-done((bf16[512,1280]{1,0:T(8,128)(2,1)}, bf16[512,1280]{1,0:T(8,128)(2,1)S(1)}, u32[]{:S(2)}, u32[]{:S(2)}) %collective-permute-start.45) | collective-permute-done | bytes 1310752 | tf_op jit(solution)/shard_map/ppermute | solution.py:97
  942.0 3.9 fusion.14
  (462 shorter events, 266.8 us)
Async XLA Ops:
  7.2 95.8 %all-gather.5.cloned.1.call-start = ((), (), s32[]{:S(2)}) async-start(), calls=%async_computation.13 | async-start | bytes 2867200 | tf_op jit(solution)/shard_map/all_gather | solution.py:501
  7.2 44.3 %collective-permute-start.1 = (bf16[512,1280]{1,0:T(8,128)(2,1)}, bf16[512,1280]{1,0:T(8,128)(2,1)S(1)}, u32[]{:S(2)}, u32[]{:S(2)}) collective-permute-start(bf16[512,1280]{1,0:T(8,128)(2,1)} %bitcast.131), channel_id=1, source_target_pairs={{0,1},{2,0},{4,2},{6,4},{7,6},{5,7},{3,5},{1,3},{8,9},{10,8},{12,1... | collective-permute-start | bytes 3932168 | tf_op jit(solution)/shard_map/ppermute | solution.py:71
  8.9 42.7 %collective-permute-start = (bf16[512,1280]{1,0:T(8,128)(2,1)}, bf16[512,1280]{1,0:T(8,128)(2,1)}, u32[]{:S(2)}, u32[]{:S(2)}) collective-permute-start(bf16[512,1280]{1,0:T(8,128)(2,1)} %bitcast.132), channel_id=1, source_target_pairs={{0,2},{2,4},{4,6},{6,7},{7,5},{5,3},{3,1},{1,0},{8,10},{10,12},{12... | collective-permute-start | bytes 3932168 | tf_op jit(solution)/shard_map/ppermute | solution.py:71
  58.1 148.3 %all-gather.7.cloned.1.call-start = ((), (), s32[]{:S(2)}) async-start(), calls=%async_computation.14 | async-start | bytes 2856960 | tf_op jit(solution)/shard_map/all_gather | solution.py:512
  58.1 29.5 %collective-permute-start.2 = (bf16[512,1280]{1,0:T(8,128)(2,1)}, bf16[512,1280]{1,0:T(8,128)(2,1)}, u32[]{:S(2)}, u32[]{:S(2)}) collective-permute-start(bf16[512,1280]{1,0:T(8,128)(2,1)} %collective-permute-done.tok_ref), channel_id=1, source_target_pairs={{0,2},{2,4},{4,6},{6,7},{7,5},{5,3},{3,1},{1,0},{8,10},{10,12},{12... | collective-permute-start | bytes 3932168 | tf_op jit(solution)/shard_map/ppermute | solution.py:71
  58.7 28.9 %collective-permute-start.3 = (bf16[512,1280]{1,0:T(8,128)(2,1)S(1)}, bf16[512,1280]{1,0:T(8,128)(2,1)}, u32[]{:S(2)}, u32[]{:S(2)}) collective-permute-start(bf16[512,1280]{1,0:T(8,128)(2,1)S(1)} %collective-permute-done.1.tok_ref), channel_id=1, source_target_pairs={{0,1},{2,0},{4,2},{6,4},{7,6},{5,7},{3,5},{1,3},{8,9},{10,8},{12,1... | collective-permute-start | bytes 3932168 | tf_op jit(solution)/shard_map/ppermute | solution.py:71
  87.6 40.4 %collective-permute-start.4 = (bf16[512,1280]{1,0:T(8,128)(2,1)}, bf16[512,1280]{1,0:T(8,128)(2,1)}, u32[]{:S(2)}, u32[]{:S(2)}) collective-permute-start(bf16[512,1280]{1,0:T(8,128)(2,1)} %collective-permute-done.2.tok_ref), channel_id=1, source_target_pairs={{0,2},{2,4},{4,6},{6,7},{7,5},{5,3},{3,1},{1,0},{8,10},{10,12},{12... | collective-permute-start | bytes 3932168 | tf_op jit(solution)/shard_map/ppermute | solution.py:71
  88.1 40.0 %collective-permute-start.5 = (bf16[512,1280]{1,0:T(8,128)(2,1)}, bf16[512,1280]{1,0:T(8,128)(2,1)}, u32[]{:S(2)}, u32[]{:S(2)}) collective-permute-start(bf16[512,1280]{1,0:T(8,128)(2,1)} %collective-permute-done.3.tok_ref), channel_id=1, source_target_pairs={{0,1},{2,0},{4,2},{6,4},{7,6},{5,7},{3,5},{1,3},{8,9},{10,8},{12,1... | collective-permute-start | bytes 3932168 | tf_op jit(solution)/shard_map/ppermute | solution.py:71
  128.1 115.9 %all-gather.9.cloned.1.call-start = ((), (), s32[]{:S(2)}) async-start(), calls=%async_computation.15 | async-start | bytes 4096000 | tf_op jit(solution)/shard_map/all_gather | solution.py:523
  159.3 47.1 %collective-permute-start.9 = (bf16[512,1280]{1,0:T(8,128)(2,1)}, bf16[512,1280]{1,0:T(8,128)(2,1)S(1)}, u32[]{:S(2)}, u32[]{:S(2)}) collective-permute-start(bf16[512,1280]{1,0:T(8,128)(2,1)} %bitcast.2.refs_1_), channel_id=1, source_target_pairs={{0,1},{2,0},{4,2},{6,4},{7,6},{5,7},{3,5},{1,3},{8,9},{10,8},{12,1... | collective-permute-start | bytes 3932168 | tf_op jit(solution)/shard_map/ppermute | solution.py:71
  161.8 44.6 %collective-permute-start.8 = (bf16[512,1280]{1,0:T(8,128)(2,1)}, bf16[512,1280]{1,0:T(8,128)(2,1)}, u32[]{:S(2)}, u32[]{:S(2)}) collective-permute-start(bf16[512,1280]{1,0:T(8,128)(2,1)} %bitcast.2.refs_1_), channel_id=1, source_target_pairs={{0,2},{2,4},{4,6},{6,7},{7,5},{5,3},{3,1},{1,0},{8,10},{10,12},{12... | collective-permute-start | bytes 3932168 | tf_op jit(solution)/shard_map/ppermute | solution.py:71
  209.0 32.1 %all-to-all-start.2 = ((bf16[8,640,128]{2,1,0:T(8,128)(2,1)}), bf16[8,640,128]{2,1,0:T(8,128)(2,1)S(1)}, u32[]{:S(2)}, u32[]{:S(2)}) async-start(bf16[8,640,128]{2,1,0:T(8,128)(2,1)} %get-tuple-element.214), calls=%async_computation.2 | async-start | bytes 2621440 | tf_op jit(solution)/shard_map/all_to_all | solution.py:525
  215.9 125.6 %all-gather.11.cloned.1.call-start = ((), (), s32[]{:S(2)}) async-start(), calls=%async_computation.16 | async-start | bytes 8601600 | tf_op jit(solution)/shard_map/all_gather | solution.py:537
  215.9 49.5 %collective-permute-start.10 = (bf16[512,1280]{1,0:T(8,128)(2,1)}, bf16[512,1280]{1,0:T(8,128)(2,1)}, u32[]{:S(2)}, u32[]{:S(2)}) collective-permute-start(bf16[512,1280]{1,0:T(8,128)(2,1)} %collective-permute-done.8.refs_2_), channel_id=1, source_target_pairs={{0,2},{2,4},{4,6},{6,7},{7,5},{5,3},{3,1},{1,0},{8,10},{10,12},{12... | collective-permute-start | bytes 3932168 | tf_op jit(solution)/shard_map/ppermute | solution.py:71
  216.4 49.0 %collective-permute-start.11 = (bf16[512,1280]{1,0:T(8,128)(2,1)}, bf16[512,1280]{1,0:T(8,128)(2,1)}, u32[]{:S(2)}, u32[]{:S(2)}) collective-permute-start(bf16[512,1280]{1,0:T(8,128)(2,1)} %copy-done.89), channel_id=1, source_target_pairs={{0,1},{2,0},{4,2},{6,4},{7,6},{5,7},{3,5},{1,3},{8,9},{10,8},{12,1... | collective-permute-start | bytes 3932168 | tf_op jit(solution)/shard_map/ppermute | solution.py:71
  266.7 246.8 %reduce-scatter.15.cloned.1.call-start = ((), (), s32[]{:S(2)}) async-start(), calls=%async_computation.18 | async-start | bytes 2867200 | tf_op jit(solution)/shard_map/reduce_scatter | solution.py:603
  266.8 30.5 %collective-permute-start.13 = (bf16[512,1280]{1,0:T(8,128)(2,1)}, bf16[512,1280]{1,0:T(8,128)(2,1)}, u32[]{:S(2)}, u32[]{:S(2)}) collective-permute-start(bf16[512,1280]{1,0:T(8,128)(2,1)} %multiply_convert_fusion.refs_0_), channel_id=1, source_target_pairs={{0,1},{2,0},{4,2},{6,4},{7,6},{5,7},{3,5},{1,3},{8,9},{10,8},{12,1... | collective-permute-start | bytes 3932168 | tf_op jit(solution)/shard_map/ppermute | solution.py:71
  267.4 29.9 %collective-permute-start.12 = (bf16[512,1280]{1,0:T(8,128)(2,1)}, bf16[512,1280]{1,0:T(8,128)(2,1)}, u32[]{:S(2)}, u32[]{:S(2)}) collective-permute-start(bf16[512,1280]{1,0:T(8,128)(2,1)} %multiply_convert_fusion.refs_0_), channel_id=1, source_target_pairs={{0,2},{2,4},{4,6},{6,7},{7,5},{5,3},{3,1},{1,0},{8,10},{10,12},{12... | collective-permute-start | bytes 3932168 | tf_op jit(solution)/shard_map/ppermute | solution.py:71
  297.3 42.1 %collective-permute-start.14 = (bf16[512,1280]{1,0:T(8,128)(2,1)}, bf16[512,1280]{1,0:T(8,128)(2,1)}, u32[]{:S(2)}, u32[]{:S(2)}) collective-permute-start(bf16[512,1280]{1,0:T(8,128)(2,1)} %collective-permute-done.12.refs_0_), channel_id=1, source_target_pairs={{0,2},{2,4},{4,6},{6,7},{7,5},{5,3},{3,1},{1,0},{8,10},{10,12},{12... | collective-permute-start | bytes 3932168 | tf_op jit(solution)/shard_map/ppermute | solution.py:71
  297.5 41.9 %collective-permute-start.15 = (bf16[512,1280]{1,0:T(8,128)(2,1)}, bf16[512,1280]{1,0:T(8,128)(2,1)}, u32[]{:S(2)}, u32[]{:S(2)}) collective-permute-start(bf16[512,1280]{1,0:T(8,128)(2,1)} %collective-permute-done.13.refs_1_), channel_id=1, source_target_pairs={{0,1},{2,0},{4,2},{6,4},{7,6},{5,7},{3,5},{1,3},{8,9},{10,8},{12,1... | collective-permute-start | bytes 3932168 | tf_op jit(solution)/shard_map/ppermute | solution.py:71
  339.4 34.7 %collective-permute-start.16 = (bf16[512,1280]{1,0:T(8,128)(2,1)}, bf16[512,1280]{1,0:T(8,128)(2,1)S(1)}, u32[]{:S(2)}, u32[]{:S(2)}) collective-permute-start(bf16[512,1280]{1,0:T(8,128)(2,1)} %collective-permute-done.10.refs_2_), channel_id=1, source_target_pairs={{0,2},{2,4},{4,6},{6,7},{7,5},{5,3},{3,1},{1,0},{8,10},{10,12},{12... | collective-permute-start | bytes 3932168 | tf_op jit(solution)/shard_map/ppermute | solution.py:71
  339.6 34.4 %collective-permute-start.17 = (bf16[512,1280]{1,0:T(8,128)(2,1)}, bf16[512,1280]{1,0:T(8,128)(2,1)S(1)}, u32[]{:S(2)}, u32[]{:S(2)}) collective-permute-start(bf16[512,1280]{1,0:T(8,128)(2,1)} %collective-permute-done.11.refs_3_), channel_id=1, source_target_pairs={{0,1},{2,0},{4,2},{6,4},{7,6},{5,7},{3,5},{1,3},{8,9},{10,8},{12,1... | collective-permute-start | bytes 3932168 | tf_op jit(solution)/shard_map/ppermute | solution.py:71
  374.1 139.5 %reduce-scatter.13.cloned.1.call-start = ((), (), s32[]{:S(2)}) async-start(), calls=%async_computation.17 | async-start | bytes 5734400 | tf_op jit(solution)/shard_map/reduce_scatter | solution.py:603
  375.5 200.8 %reduce-scatter.17.cloned.1.call-start = ((), (), s32[]{:S(2)}) async-start(), calls=%async_computation.19 | async-start | bytes 5734400 | tf_op jit(solution)/shard_map/reduce_scatter | solution.py:626
  378.7 42.8 %collective-permute-start.18 = (bf16[512,1280]{1,0:T(8,128)(2,1)}, bf16[512,1280]{1,0:T(8,128)(2,1)}, u32[]{:S(2)}, u32[]{:S(2)}) collective-permute-start(bf16[512,1280]{1,0:T(8,128)(2,1)} %collective-permute-done.14.refs_0_), channel_id=1, source_target_pairs={{0,2},{2,4},{4,6},{6,7},{7,5},{5,3},{3,1},{1,0},{8,10},{10,12},{12... | collective-permute-start | bytes 3932168 | tf_op jit(solution)/shard_map/ppermute | solution.py:71
  378.9 42.6 %collective-permute-start.19 = (bf16[512,1280]{1,0:T(8,128)(2,1)}, bf16[512,1280]{1,0:T(8,128)(2,1)}, u32[]{:S(2)}, u32[]{:S(2)}) collective-permute-start(bf16[512,1280]{1,0:T(8,128)(2,1)} %collective-permute-done.15.refs_1_), channel_id=1, source_target_pairs={{0,1},{2,0},{4,2},{6,4},{7,6},{5,7},{3,5},{1,3},{8,9},{10,8},{12,1... | collective-permute-start | bytes 3932168 | tf_op jit(solution)/shard_map/ppermute | solution.py:71
  421.5 43.0 %collective-permute-start.20 = (bf16[512,1280]{1,0:T(8,128)(2,1)}, bf16[512,1280]{1,0:T(8,128)(2,1)}, u32[]{:S(2)}, u32[]{:S(2)}) collective-permute-start(bf16[512,1280]{1,0:T(8,128)(2,1)} %collective-permute-done.18.refs_0_), channel_id=1, source_target_pairs={{0,2},{2,4},{4,6},{6,7},{7,5},{5,3},{3,1},{1,0},{8,10},{10,12},{12... | collective-permute-start | bytes 3932168 | tf_op jit(solution)/shard_map/ppermute | solution.py:590
  422.0 42.6 %collective-permute-start.21 = (bf16[512,1280]{1,0:T(8,128)(2,1)}, bf16[512,1280]{1,0:T(8,128)(2,1)}, u32[]{:S(2)}, u32[]{:S(2)}) collective-permute-start(bf16[512,1280]{1,0:T(8,128)(2,1)} %copy-done.90), channel_id=1, source_target_pairs={{0,1},{2,0},{4,2},{6,4},{7,6},{5,7},{3,5},{1,3},{8,9},{10,8},{12,1... | collective-permute-start | bytes 3932168 | tf_op jit(solution)/shard_map/ppermute | solution.py:591
  510.4 168.1 %reduce-scatter.19.cloned.1.call-start = ((), (), s32[]{:S(2)}) async-start(), calls=%async_computation.20 | async-start | bytes 5734400 | tf_op jit(solution)/shard_map/reduce_scatter | solution.py:626
  541.6 25.8 %collective-permute-start.27 = (bf16[512,1280]{1,0:T(8,128)(2,1)}, bf16[512,1280]{1,0:T(8,128)(2,1)}, u32[]{:S(2)}, u32[]{:S(2)}) collective-permute-start(bf16[512,1280]{1,0:T(8,128)(2,1)} %add_convert_fusion.11), channel_id=1, source_target_pairs={{0,1},{2,0},{4,2},{6,4},{7,6},{5,7},{3,5},{1,3},{8,9},{10,8},{12,1... | collective-permute-start | bytes 3932168 | tf_op jit(solution)/shard_map/ppermute | solution.py:97
  601.6 25.3 %collective-permute-start.31 = (bf16[256,1280]{1,0:T(8,128)(2,1)}, bf16[256,1280]{1,0:T(8,128)(2,1)}, u32[]{:S(2)}, u32[]{:S(2)}) collective-permute-start(bf16[256,1280]{1,0:T(8,128)(2,1)} %get-tuple-element.374), channel_id=1, source_target_pairs={{0,1},{2,0},{4,2},{6,4},{7,6},{5,7},{3,5},{1,3},{8,9},{10,8},{12,1... | collective-permute-start | bytes 1966088 | tf_op jit(solution)/shard_map/ppermute | solution.py:97
  629.3 49.1 %all-to-all-start.3 = ((bf16[8,640,128]{2,1,0:T(8,128)(2,1)}), bf16[8,640,128]{2,1,0:T(8,128)(2,1)S(1)}, u32[]{:S(2)}, u32[]{:S(2)}) async-start(bf16[8,640,128]{2,1,0:T(8,128)(2,1)} %pad_maximum_fusion.6), calls=%async_computation.6 | async-start | bytes 2621440 | tf_op jit(solution)/shard_map/all_to_all | solution.py:650
  633.7 87.7 %reduce-scatter.21.cloned.1.call-start = ((), (), s32[]{:S(2)}) async-start(), calls=%async_computation.21 | async-start | bytes 4096000 | tf_op jit(solution)/shard_map/reduce_scatter | solution.py:657
  636.4 40.9 %collective-permute-start.32 = (bf16[512,1280]{1,0:T(8,128)(2,1)}, bf16[512,1280]{1,0:T(8,128)(2,1)}, u32[]{:S(2)}, u32[]{:S(2)}) collective-permute-start(bf16[512,1280]{1,0:T(8,128)(2,1)} %pad_maximum_fusion.7), channel_id=1, source_target_pairs={{0,2},{2,4},{4,6},{6,7},{7,5},{5,3},{3,1},{1,0},{8,10},{10,12},{12... | collective-permute-start | bytes 3932168 | tf_op jit(solution)/shard_map/ppermute | solution.py:97
  639.6 38.9 %collective-permute-start.33 = (bf16[512,1280]{1,0:T(8,128)(2,1)}, bf16[512,1280]{1,0:T(8,128)(2,1)}, u32[]{:S(2)}, u32[]{:S(2)}) collective-permute-start(bf16[512,1280]{1,0:T(8,128)(2,1)} %pad_maximum_fusion.8), channel_id=1, source_target_pairs={{0,1},{2,0},{4,2},{6,4},{7,6},{5,7},{3,5},{1,3},{8,9},{10,8},{12,1... | collective-permute-start | bytes 3932168 | tf_op jit(solution)/shard_map/ppermute | solution.py:97
  678.5 176.1 %reduce-scatter.27.cloned.1.call-start = ((), (), s32[]{:S(2)}) async-start(), calls=%async_computation.24 | async-start | bytes 2856960
  681.3 40.1 %collective-permute-start.35 = (bf16[512,1280]{1,0:T(8,128)(2,1)}, bf16[512,1280]{1,0:T(8,128)(2,1)}, u32[]{:S(2)}, u32[]{:S(2)}) collective-permute-start(bf16[512,1280]{1,0:T(8,128)(2,1)} %add_convert_fusion.7), channel_id=1, source_target_pairs={{0,1},{2,0},{4,2},{6,4},{7,6},{5,7},{3,5},{1,3},{8,9},{10,8},{12,1... | collective-permute-start | bytes 3932168 | tf_op jit(solution)/shard_map/ppermute | solution.py:97
  686.5 34.9 %collective-permute-start.34 = (bf16[512,1280]{1,0:T(8,128)(2,1)}, bf16[512,1280]{1,0:T(8,128)(2,1)}, u32[]{:S(2)}, u32[]{:S(2)}) collective-permute-start(bf16[512,1280]{1,0:T(8,128)(2,1)} %add_convert_fusion.8), channel_id=1, source_target_pairs={{0,2},{2,4},{4,6},{6,7},{7,5},{5,3},{3,1},{1,0},{8,10},{10,12},{12... | collective-permute-start | bytes 3932168 | tf_op jit(solution)/shard_map/ppermute | solution.py:97
  724.6 62.4 %collective-permute-start.36 = (bf16[512,1280]{1,0:T(8,128)(2,1)}, bf16[512,1280]{1,0:T(8,128)(2,1)}, u32[]{:S(2)}, u32[]{:S(2)}) collective-permute-start(bf16[512,1280]{1,0:T(8,128)(2,1)} %add_convert_fusion.6), channel_id=1, source_target_pairs={{0,2},{2,4},{4,6},{6,7},{7,5},{5,3},{3,1},{1,0},{8,10},{10,12},{12... | collective-permute-start | bytes 3932168 | tf_op jit(solution)/shard_map/ppermute | solution.py:97
  727.5 59.5 %collective-permute-start.37 = (bf16[512,1280]{1,0:T(8,128)(2,1)}, bf16[512,1280]{1,0:T(8,128)(2,1)}, u32[]{:S(2)}, u32[]{:S(2)}) collective-permute-start(bf16[512,1280]{1,0:T(8,128)(2,1)} %add_convert_fusion.5), channel_id=1, source_target_pairs={{0,1},{2,0},{4,2},{6,4},{7,6},{5,7},{3,5},{1,3},{8,9},{10,8},{12,1... | collective-permute-start | bytes 3932168 | tf_op jit(solution)/shard_map/ppermute | solution.py:97
  731.1 131.5 %reduce-scatter.25.cloned.1.call-start = ((), (), s32[]{:S(2)}) async-start(), calls=%async_computation.23 | async-start | bytes 2867200
  810.9 33.7 %collective-permute-start.41 = (bf16[512,1280]{1,0:T(8,128)(2,1)}, bf16[512,1280]{1,0:T(8,128)(2,1)}, u32[]{:S(2)}, u32[]{:S(2)}) collective-permute-start(bf16[512,1280]{1,0:T(8,128)(2,1)} %pad_maximum_fusion.10), channel_id=1, source_target_pairs={{0,1},{2,0},{4,2},{6,4},{7,6},{5,7},{3,5},{1,3},{8,9},{10,8},{12,1... | collective-permute-start | bytes 3932168 | tf_op jit(solution)/shard_map/ppermute | solution.py:97
  815.8 130.2 %reduce-scatter.23.cloned.1.call-start = ((), (), s32[]{:S(2)}) async-start(), calls=%async_computation.22 | async-start | bytes 5734400 | tf_op jit(solution)/shard_map/reduce_scatter | solution.py:694
  818.6 29.8 %collective-permute-start.40 = (bf16[512,1280]{1,0:T(8,128)(2,1)S(1)}, bf16[512,1280]{1,0:T(8,128)(2,1)S(1)}, u32[]{:S(2)}, u32[]{:S(2)}) collective-permute-start(bf16[512,1280]{1,0:T(8,128)(2,1)S(1)} %pad_maximum_fusion.9), channel_id=1, source_target_pairs={{0,2},{2,4},{4,6},{6,7},{7,5},{5,3},{3,1},{1,0},{8,10},{10,12},{12... | collective-permute-start | bytes 3932168 | tf_op jit(solution)/shard_map/ppermute | solution.py:97
  851.1 28.9 %collective-permute-start.43 = (bf16[512,1280]{1,0:T(8,128)(2,1)}, bf16[512,1280]{1,0:T(8,128)(2,1)}, u32[]{:S(2)}, u32[]{:S(2)}) collective-permute-start(bf16[512,1280]{1,0:T(8,128)(2,1)} %add_convert_fusion.2), channel_id=1, source_target_pairs={{0,1},{2,0},{4,2},{6,4},{7,6},{5,7},{3,5},{1,3},{8,9},{10,8},{12,1... | collective-permute-start | bytes 3932168 | tf_op jit(solution)/shard_map/ppermute | solution.py:97
  853.9 28.7 %collective-permute-start.42 = (bf16[512,1280]{1,0:T(8,128)(2,1)}, bf16[512,1280]{1,0:T(8,128)(2,1)S(1)}, u32[]{:S(2)}, u32[]{:S(2)}) collective-permute-start(bf16[512,1280]{1,0:T(8,128)(2,1)} %add_convert_fusion.3), channel_id=1, source_target_pairs={{0,2},{2,4},{4,6},{6,7},{7,5},{5,3},{3,1},{1,0},{8,10},{10,12},{12... | collective-permute-start | bytes 3932168 | tf_op jit(solution)/shard_map/ppermute | solution.py:97
  903.9 33.7 %collective-permute-start.45 = (bf16[512,1280]{1,0:T(8,128)(2,1)}, bf16[512,1280]{1,0:T(8,128)(2,1)S(1)}, u32[]{:S(2)}, u32[]{:S(2)}) collective-permute-start(bf16[512,1280]{1,0:T(8,128)(2,1)} %add_convert_fusion), channel_id=1, source_target_pairs={{0,1},{2,0},{4,2},{6,4},{7,6},{5,7},{3,5},{1,3},{8,9},{10,8},{12,1... | collective-permute-start | bytes 3932168 | tf_op jit(solution)/shard_map/ppermute | solution.py:97
  906.8 32.7 %collective-permute-start.44 = (bf16[512,1280]{1,0:T(8,128)(2,1)}, bf16[512,1280]{1,0:T(8,128)(2,1)}, u32[]{:S(2)}, u32[]{:S(2)}) collective-permute-start(bf16[512,1280]{1,0:T(8,128)(2,1)} %add_convert_fusion.1), channel_id=1, source_target_pairs={{0,2},{2,4},{4,6},{6,7},{7,5},{5,3},{3,1},{1,0},{8,10},{10,12},{12... | collective-permute-start | bytes 3932168 | tf_op jit(solution)/shard_map/ppermute | solution.py:97
  (111 other events, 1334.3 us)
Sparse Core Ops, SparseCore 0:
  51.7 23.5 all-gather.4
  128.2 71.3 all-gather.6
  209.1 30.9 all-gather.8
  266.9 48.8 all-gather.10
  374.2 31.9 reduce-scatter.14
  408.8 46.9 reduce-scatter.12
  510.5 46.6 reduce-scatter.16
  559.9 46.9 reduce-scatter.18
  678.6 39.9 reduce-scatter.20
  731.3 95.9 reduce-scatter.26
  830.6 31.9 reduce-scatter.24
  882.7 45.1 reduce-scatter.22

commit v2 on v1

--- a/solution.py
+++ b/solution.py
@@ -59,10 +59,11 @@
             place[member] = at
         self.forward = [(self.order[i], self.order[(i + 1) % size]) for i in range(size)]
         self.backward = [(self.order[i], self.order[(i - 1) % size]) for i in range(size)]
-        self.place = jnp.array(place, jnp.int32)[lax.axis_index("ep")]
+        table = [[self.order[(place[me] + offset) % size] for offset in range(size)] for me in range(size)]
+        self.members = lax.dynamic_index_in_dim(jnp.array(table, jnp.int32), lax.axis_index("ep"), 0, keepdims=False)
 
     def member(self, offset):
-        return jnp.array(self.order, jnp.int32)[(self.place + offset) % self.size]
+        return self.members[offset % self.size]
 
     def step(self, up, down, number):
         if number == self.half:
@@ -100,7 +101,7 @@
         return parts[0].astype(f32) + came[0].astype(f32) + came[1].astype(f32)
 
 
-def qkv_kernel(base_ref, tok_ref, gain_ref, w_ref, cos_ref, sin_ref, *rest):
+def qkv_kernel(members_ref, tok_ref, gain_ref, w_ref, cos_ref, sin_ref, *rest):
     hid_ref, qkv_ref = rest[-2:]
     x = tok_ref[...].astype(f32)
     inverse = lax.rsqrt(jnp.mean(x * x, axis=-1, keepdims=True) + epsilon)
@@ -115,12 +116,13 @@
         qkv_ref[:, slot * HEAD : (slot + 1) * HEAD] = u.astype(bf16)
 
 
-def qkv_piece(base, piece, tile, gain, w_cat, cosine, sine, buffers):
+def qkv_piece(members, offset, shift, piece, tile, gain, w_cat, cosine, sine, buffers):
     rows, width = piece.shape
     length = cosine.shape[0]
     cols = w_cat.shape[1]
     aliased = () if buffers is None else tuple(buffers)
     n_in = 6
+    at = lambda i, m: (2 * m[offset] + shift + i, 0)
     return pl.pallas_call(
         qkv_kernel,
         out_shape=(jax.ShapeDtypeStruct((length, width), bf16), jax.ShapeDtypeStruct((length, cols), bf16)),
@@ -131,13 +133,13 @@
                 pl.BlockSpec((tile, width), lambda i, b: (i, 0)),
                 pl.BlockSpec((1, width), lambda i, b: (0, 0)),
                 pl.BlockSpec((width, cols), lambda i, b: (0, 0)),
-                pl.BlockSpec((tile, HEAD), lambda i, b: (b[0] + i, 0)),
-                pl.BlockSpec((tile, HEAD), lambda i, b: (b[0] + i, 0)),
+                pl.BlockSpec((tile, HEAD), at),
+                pl.BlockSpec((tile, HEAD), at),
             ]
             + [pl.BlockSpec(memory_space=pl.ANY)] * len(aliased),
             out_specs=[
-                pl.BlockSpec((tile, width), lambda i, b: (b[0] + i, 0)),
-                pl.BlockSpec((tile, cols), lambda i, b: (b[0] + i, 0)),
+                pl.BlockSpec((tile, width), at),
+                pl.BlockSpec((tile, cols), at),
             ],
         ),
         input_output_aliases={n_in + i: i for i in range(len(aliased))},
@@ -146,7 +148,7 @@
             flops=2 * rows * width * cols, bytes_accessed=4 * rows * width + 2 * (rows + width) * cols, transcendentals=0
         ),
         name="norm_project_rotate",
-    )(base, piece, gain, w_cat, cosine, sine, *aliased)
+    )(members, piece, gain, w_cat, cosine, sine, *aliased)
 
 
 def attention_forward(own, qkv, blocks, rows, main_rows, side_rows):
@@ -313,14 +315,14 @@
     )(own, qkv, grads, attended, lse, cosine, sine)
 
 
-def expert_call(sources, hidden, grads, rank_row, rank_col, route, w_gate, w_up, w_down, capacity, first, total, buffers):
+def expert_call(members, offsets, hidden, grads, rank_row, rank_col, route, w_gate, w_up, w_down, capacity, first, total, buffers):
     count = len(hidden)
     rows, width = hidden[0].shape
     local, _, inner = w_gate.shape
     aliased = () if buffers is None else tuple(buffers)
     widths = (width, width, inner, inner, inner)
 
-    def kernel(sources_ref, *refs):
+    def kernel(members_ref, *refs):
         h_refs, z_refs, row_refs, col_refs, gate_refs = (refs[i * count : (i + 1) * count] for i in range(5))
         wg_ref, wu_ref, wd_ref = refs[5 * count : 5 * count + 3]
         rest = refs[5 * count + 3 + len(aliased) :]
@@ -369,7 +371,7 @@
 
     def of_source(shape):
         zeros = (0,) * (len(shape) - 1)
-        return [pl.BlockSpec(shape, lambda e, s, p=p: (s[p],) + zeros, pipeline_mode=pl.Buffered(1)) for p in range(count)]
+        return [pl.BlockSpec(shape, lambda e, s, p=p: (s[offsets[p]],) + zeros, pipeline_mode=pl.Buffered(1)) for p in range(count)]
 
     return pl.pallas_call(
         kernel,
@@ -400,7 +402,7 @@
         ),
         name="experts",
     )(
-        sources,
+        members,
         *hidden,
         *grads,
         *[rank_row] * count,
@@ -486,10 +488,9 @@
         for step in steps:
             for i, part in enumerate(arrivals[step]):
                 offset = 0 if step == 0 else (half if step == half else (-step, step)[i])
-                base = 2 * ring.member(offset) + (i if step == half else 0)
                 known["buffers"] = qkv_piece(
-                    base.astype(jnp.int32).reshape(1), part, tile, known["gains"][0], known["w_cat"], cosine, sine,
-                    known.get("buffers"),
+                    ring.members, offset % ep, i if step == half else 0, part, tile, known["gains"][0], known["w_cat"],
+                    cosine, sine, known.get("buffers"),
                 )
 
     up, down = token_rows, token_rows
@@ -523,6 +524,8 @@
     full_out = lax.all_gather(packed[:, :width], "dp", axis=0, tiled=True)
     grad_pieces[2] = ring.step(*grad_pieces[1], 2)
     heads_in = lax.all_to_all(low, "ep", 0, 0, tiled=True)
+    rank_row, rank_col, route_row = rank[:, :, None, :], rank[:, :, :, None], route[:, :, None, :]
+    heads_in, rank_col = tie(heads_in, rank_col)
     main_in = heads_in[:, :main_rows].reshape(MAIN, rows, HEAD)
     side_in = heads_in[:, main_rows:].reshape(HEADS - MAIN, rows, HEAD)
     attended_low = jnp.concatenate([main_in, side_in], axis=0).transpose(1, 0, 2).reshape(rows, width)
@@ -539,7 +542,6 @@
     full_up = packed[:, inner : 2 * inner]
     full_down_t = packed[:, 2 * inner :]
 
-    rank_row, rank_col, route_row = rank[:, :, None, :], rank[:, :, :, None], route[:, :, None, :]
     part_y, part_x, buffers = {}, {}, [None]
 
     def run_experts(step, arrived):
@@ -551,7 +553,8 @@
         else:
             group, first = (-step, step), 2 * (step - 1)
         outs = expert_call(
-            jnp.stack([ring.member(offset) for offset in group]).astype(jnp.int32),
+            ring.members,
+            [offset % ep for offset in group],
             arrived,
             grads,
             rank_row,
@@ -643,10 +646,7 @@
     )
     part_y[half], grad_routed = tie(part_y[half], grad_routed)
     came_y = ring.scatter_step(part_y, None, 1)
-    heads_out, attended_low, grad_branch, grad_gain_two, came_y = tie(
-        heads_out, attended_low, grad_branch, grad_gain_two, came_y
-    )
-    came_y = ring.scatter_step(part_y, came_y, 2)
+    heads_out, attended_low, grad_branch, grad_gain_two = tie(heads_out, attended_low, grad_branch, grad_gain_two)
     head_grads = lax.all_to_all(heads_out, "ep", 0, 0, tiled=True)
     grad_full_out = dot_tn(attended_low, grad_branch).astype(bf16)
 
@@ -655,18 +655,19 @@
     gain_columns = dot_tn(jnp.stack([gain_high, gain_rest]), jnp.eye(2, HEAD, dtype=bf16))
     head_grads, came_y, grad_full_out, expert_grads[1] = tie(head_grads, came_y, grad_full_out, expert_grads[1])
     dense.append(lax.psum_scatter(grad_full_out, "dp", scatter_dimension=0, tiled=True))
-    for step in range(3, half):
+    for step in range(2, half - 1):
         came_y = ring.scatter_step(part_y, came_y, step)
     grad_side = attention_backward(
         own, qkv, head_grads, attended, lse, cosine, sine, ep, rows, side_rows, 1, main_rows
     )
     grad_side, came_y, qkv, dense = tie(grad_side, came_y, qkv, dense)
     dense = lax.psum_scatter(jnp.concatenate(dense, axis=1), "ep", scatter_dimension=0, tiled=True).astype(f32)
-    came_y = ring.scatter_step(part_y, came_y, half)
+    came_y = ring.scatter_step(part_y, came_y, half - 1)
     grad_main = attention_backward(
         own, qkv, head_grads, attended, lse, cosine, sine, ep, rows, main_rows, 0, 0
     )
-    grad_main, came_y = tie(grad_main, came_y)
+    grad_main, grad_side, came_y, expert_grads[:2] = tie(grad_main, grad_side, came_y, expert_grads[:2])
+    came_y = ring.scatter_step(part_y, came_y, half)
 
     part_h = {}
     for offset in range(-half + 1, half + 1):
@@ -675,19 +676,21 @@
             dot_nt(lax.dynamic_slice_in_dim(grad_main, first, rows, 0), w_cat[:, : 3 * HEAD])
             + dot_nt(lax.dynamic_slice_in_dim(grad_side, first, rows, 0), w_cat[:, 3 * HEAD :])
         ).astype(bf16)
-    hidden_all, part_h[half] = tie(hidden_all, part_h[half])
-    head_sums = jnp.concatenate([dot_tn(hidden_all, grad_main), dot_tn(hidden_all, grad_side), gain_columns], axis=1)
-    head_sums = head_sums.astype(bf16)
     came = None
+    inverse_one = lax.rsqrt(jnp.mean(residual * residual, axis=-1, keepdims=True) + epsilon)
     for step in range(1, half + 1):
         came = ring.scatter_step(part_h, came, step)
         if step == 1:
             next_parts = [part_h[offset] for offset in (half - 1, 1 - half)]
-            came, head_sums, next_parts = tie(came, head_sums, next_parts)
+            came, next_parts, hidden_all = tie(came, next_parts, hidden_all)
             part_h[half - 1], part_h[1 - half] = next_parts
+            head_sums = [dot_tn(hidden_all, grad_main), dot_tn(hidden_all, grad_side), gain_columns]
+            head_sums = jnp.concatenate(head_sums, axis=1).astype(bf16)
+            came_y, head_sums = tie(came_y, head_sums)
             head_sums = lax.psum_scatter(head_sums, "dp", scatter_dimension=0, tiled=True)
         if step == 2:
-            came, part_h = tie(came, part_h)
+            early = [item.astype(f32) for item in expert_grads[:2]]
+            came, came_y, part_h, expert_grads[:2], inverse_one = tie(came, came_y, part_h, early, inverse_one)
         if step == 3:
             came, head_sums, dense, last = tie(came, head_sums, dense, expert_grads[2])
             head_sums = lax.all_to_all(head_sums.reshape(ep, shard, 7 * HEAD), "ep", 0, 0, tiled=True)
@@ -704,7 +707,6 @@
         jnp.sum(w.astype(f32) * g, axis=1) for w, g in zip((w_query, w_key, w_value), projections)
     ) / norm1_gain.astype(f32)
 
-    inverse_one = lax.rsqrt(jnp.mean(residual * residual, axis=-1, keepdims=True) + epsilon)
     normed_one = residual * inverse_one
     scaled = grad_hidden_one * gain_one
     grad_input = grad_middle + inverse_one * (
@@ -722,8 +724,8 @@
         dense[:, :inner],
         dense[:, inner : 2 * inner],
         dense[:, 2 * inner : 3 * inner].T,
-        expert_grads[0].astype(f32),
-        expert_grads[1].astype(f32),
+        expert_grads[0],
+        expert_grads[1],
         expert_grads[2].astype(f32).transpose(0, 2, 1),
     )
 

time: 963 us -> 935 us (0.971)
  waiting for transfers between devices: 198 us -> 185 us
  between operations: 32.8 us -> 20.7 us
  matrix products: 148 us -> 138 us
    ppermute x12, waiting for transfers between devices: 45.7 us -> 25.9 us  [scatter_step(): lax.ppermute(up, 'ep', self.forward)]
    unnamed x204 -> x188, local copies, waits for them, and re-layouts: 31.5 us -> 36.9 us
  transfers between devices with their start and end apart: 62 -> 62, of which waited for: 21 -> 19; matrix products, arithmetic and copies ran while one was open for 30% -> 29% of each run, Pallas kernels for 31% -> 33%
where the time goes in v2:
time: 935 us; the launch traced here: 927 us
  Pallas kernels  302 us (32%)
  waiting for transfers between devices  185 us (20%)
  matrix products  138 us (15%)
  other arithmetic  93.1 us (10%)
  local copies, waits for them, and re-layouts  77.3 us (8%)
  starting transfers between devices  74.5 us (8%)
  blocking collectives  37.2 us (4%)
  between operations  20.7 us (2%)
    pallas_call x5, Pallas kernels, expert_call(): pl.pallas_call(kernel, out_shape=[piece] * (2 * count) + [jax.ShapeDtypeS...  169 us
    ppermute x12, waiting for transfers between devices, scatter_step(): lax.ppermute(down, 'ep', self.backward)  86.1 us
    dot_general x3, matrix products, by_rows(): jnp.einsum('ecd,ecf->edf', left, right, preferred_element_type=f32)  60.9 us
    pallas_call x2, Pallas kernels, attention_backward(): pl.pallas_call(kernel, out_shape=jax.ShapeDtypeStruct((length, cols), bf1...  60.1 us
    pallas_call x1, Pallas kernels, attention_forward(): pl.pallas_call(kernel, out_shape=(jax.ShapeDtypeStruct((blocks, tall, HEA...  40.5 us
    ppermute x10, waiting for transfers between devices, step(): lax.ppermute(up, 'ep', self.forward)  40.3 us
    dot_general x20, matrix products, dot_nt(): lax.dot_general(a, b, (((1,), (1,)), ((), ())), preferred_element_type=f32)  38.2 us
    all_to_all x1, blocking collectives, shards(): head_rows = lax.all_to_all(jnp.stack(messages), 'ep', 0, 0, tiled=True)  37.2 us
  transfers between devices with their start and end apart: 62, of which 19 were waited for; matrix products, arithmetic and copies ran while one was open for 29% of the time, Pallas kernels for 33%

profile of v2, /device:TPU:12, one launch (start us, length us, event | category | flops | bytes accessed | tf_op | source)
XLA Modules:
  0.0 926.9 jit_solution(3775333273812122616)
XLA Ops:
  14.4 37.2 %all_to_all.25 = bf16[8,40,896]{2,1,0:T(8,128)(2,1)} all-to-all(bf16[8,40,896]{2,1,0:T(8,128)(2,1)S(1)} %bitcast_dynamic-update-slice_fusion), channel_id=1, replica_groups=mesh['dp'=4,'ep'=8] {'ep'}, dimensions={0} | all-to-all | bytes 1146880 | tf_op jit(solution)/shard_map/all_to_all | solution.py:467
  52.6 5.6 all-to-all-start
  58.1 7.5 fusion.34
  71.3 23.3 %collective-permute-done.2.tok_ref = bf16[512,1280]{1,0:T(8,128)(2,1)} collective-permute-done((bf16[512,1280]{1,0:T(8,128)(2,1)}, bf16[512,1280]{1,0:T(8,128)(2,1)}, u32[]{:S(2)}, u32[]{:S(2)}) %collective-permute-start.2) | collective-permute-done | bytes 1310752 | tf_op jit(solution)/shard_map/ppermute | solution.py:72
  107.8 4.2 norm_project_rotate.10
  115.1 4.2 norm_project_rotate.12
  119.3 4.2 norm_project_rotate.13
  135.2 4.2 norm_project_rotate.14
  139.5 4.3 norm_project_rotate.15
  147.7 4.7 collective-permute-done.6.tok_ref
  160.0 40.5 %attention_forward.1 = (bf16[8,640,128]{2,1,0:T(8,128)(2,1)}, f32[8,640,128]{2,1,0:T(8,128)S(1)}, f32[8,8,640]{2,1,0:T(8,128)S(1)}) custom-call(s32[2]{0:T(128)S(1)} %pad_add_fusion.own_ref, bf16[4096,768]{1,0:T(8,128)(2,1)} %copy-done.2), custom_call_target="tpu_custom_call" | custom-call | flops 5368709120 | bytes 8388608 | tf_op jit(solution)/shard_map/attention_forward/pallas_call | solution.py:206
  205.3 7.1 all-to-all-start.2
  214.6 23.1 %all-to-all-done.2 = bf16[8,640,128]{2,1,0:T(8,128)(2,1)S(1)} async-done(((bf16[8,640,128]{2,1,0:T(8,128)(2,1)}), bf16[8,640,128]{2,1,0:T(8,128)(2,1)S(1)}, u32[]{:S(2)}, u32[]{:S(2)}) %all-to-all-start.2) | async-done | bytes 1310752 | tf_op jit(solution)/shard_map/all_to_all | solution.py:526
  240.6 4.5 multiply_reduce_fusion.2
  247.9 15.2 %collective-permute-done.10.refs_2_ = bf16[512,1280]{1,0:T(8,128)(2,1)} collective-permute-done((bf16[512,1280]{1,0:T(8,128)(2,1)}, bf16[512,1280]{1,0:T(8,128)(2,1)}, u32[]{:S(2)}, u32[]{:S(2)}) %collective-permute-start.10) | collective-permute-done | bytes 1310752 | tf_op jit(solution)/shard_map/ppermute | solution.py:72
  270.6 24.3 %experts.5 = (bf16[512,1280]{1,0:T(8,128)(2,1)}, bf16[512,1280]{1,0:T(8,128)(2,1)}, bf16[2,8,320,1280]{3,2,1,0:T(8,128)(2,1)}, bf16[2,8,320,1280]{3,2,1,0:T(8,12...) custom-call(s32[8]{0:T(128)} %copy-done.27, ...), custom_call_target="tpu_custom_call" | custom-call | flops 12163481600 | bytes 25722880 | tf_op jit(solution)/shard_map/experts/pallas_call | solution.py:376
  297.1 40.3 %experts.6 = (bf16[512,1280]{1,0:T(8,128)(2,1)}, bf16[512,1280]{1,0:T(8,128)(2,1)}, bf16[512,1280]{1,0:T(8,128)(2,1)}, bf16[512,1280]{1,0:T(8,128)(2,1)}, bf16[2...) custom-call(s32[8]{0:T(128)} %copy-done.27, ...), custom_call_target="tpu_custom_call", output_to_operand_aliasing={{4}: (14, {}), {5}: (15, {}), {6}: (16, {}), {7}: (17, {}),... | custom-call | flops 24326963200 | bytes 37683200 | tf_op jit(solution)/shard_map/experts/pallas_call | solution.py:376
  339.5 3.7 fusion.21
  356.0 4.3 convolution_convert_fusion.5
  360.2 6.3 convolution_convert_fusion.1
  366.5 5.5 convolution_add_fusion.8
  375.5 42.0 %experts.7 = (bf16[512,1280]{1,0:T(8,128)(2,1)}, bf16[512,1280]{1,0:T(8,128)(2,1)}, bf16[512,1280]{1,0:T(8,128)(2,1)}, bf16[512,1280]{1,0:T(8,128)(2,1)}, bf16[2...) custom-call(s32[8]{0:T(128)} %copy-done.27, ...), custom_call_target="tpu_custom_call", output_to_operand_aliasing={{4}: (14, {}), {5}: (15, {}), {6}: (16, {}), {7}: (17, {}),... | custom-call | flops 24326963200 | bytes 37683200 | tf_op jit(solution)/shard_map/experts/pallas_call | solution.py:376
  419.6 40.0 %experts.8 = (bf16[512,1280]{1,0:T(8,128)(2,1)}, bf16[512,1280]{1,0:T(8,128)(2,1)}, bf16[512,1280]{1,0:T(8,128)(2,1)}, bf16[512,1280]{1,0:T(8,128)(2,1)}, bf16[2...) custom-call(s32[8]{0:T(128)} %copy-done.27, ...), custom_call_target="tpu_custom_call", output_to_operand_aliasing={{4}: (14, {}), {5}: (15, {}), {6}: (16, {}), {7}: (17, {}),... | custom-call | flops 24326963200 | bytes 37683200 | tf_op jit(solution)/shard_map/experts/pallas_call | solution.py:376
  459.7 22.7 %experts.9 = (bf16[512,1280]{1,0:T(8,128)(2,1)}, bf16[512,1280]{1,0:T(8,128)(2,1)}, bf16[2,8,320,1280]{3,2,1,0:T(8,128)(2,1)}, bf16[2,8,320,1280]{3,2,1,0:T(8,12...) custom-call(s32[8]{0:T(128)} %copy-done.27, ...), custom_call_target="tpu_custom_call", output_to_operand_aliasing={{2}: (9, {}), {3}: (10, {}), {4}: (11, {}), {5}: (12, {}), ... | custom-call | flops 12163481600 | bytes 25722880 | tf_op jit(solution)/shard_map/experts/pallas_call | solution.py:376
  485.8 19.7 %convolution_convert_fusion.4 = bf16[2,1280,896]{2,1,0:T(8,128)(2,1)} fusion(bf16[2,2560,1280]{2,1,0:T(8,128)(2,1)} %bitcast.139, bf16[2,2560,896]{2,1,0:T(8,128)(2,1)} %bitcast.145), kind=kOutput, calls=%fused_computation.4 | convolution fusion | flops 11746344960 | bytes 26869760 | tf_op jit(solution)/shard_map/ecd,ecf->edf/dot_general | solution.py:619
  510.7 21.2 %convolution_convert_fusion.3 = bf16[2,1280,896]{2,1,0:T(8,128)(2,1)} fusion(bf16[2,2560,1280]{2,1,0:T(8,128)(2,1)} %bitcast.140, bf16[2,2560,896]{2,1,0:T(8,128)(2,1)} %bitcast.146), kind=kOutput, calls=%fused_computation.3 | convolution fusion | flops 11746344960 | bytes 26869760 | tf_op jit(solution)/shard_map/ecd,ecf->edf/dot_general | solution.py:619
  540.9 20.0 %convolution_convert_fusion.2 = bf16[2,1280,896]{2,1,0:T(8,128)(2,1)} fusion(bf16[2,2560,1280]{2,1,0:T(8,128)(2,1)} %bitcast.141, bf16[2,2560,896]{2,1,0:T(8,128)(2,1)} %bitcast.144), kind=kOutput, calls=%fused_computation.2 | convolution fusion | flops 11746344960 | bytes 26869760 | tf_op jit(solution)/shard_map/ecd,ecf->edf/dot_general | solution.py:619
  570.1 15.6 %collective-permute-done.29 = bf16[512,1280]{1,0:T(8,128)(2,1)} collective-permute-done((bf16[512,1280]{1,0:T(8,128)(2,1)}, bf16[512,1280]{1,0:T(8,128)(2,1)}, u32[]{:S(2)}, u32[]{:S(2)}) %collective-permute-start.29) | collective-permute-done | bytes 1310752 | tf_op jit(solution)/shard_map/ppermute | solution.py:98
  587.9 4.1 multiply_reduce_fusion
  592.0 3.8 fusion.102
  601.5 5.8 all-to-all-start.3
  611.9 3.5 convolution_convert_fusion
  615.5 21.3 %collective-permute-done.31 = bf16[256,1280]{1,0:T(8,128)(2,1)} collective-permute-done((bf16[256,1280]{1,0:T(8,128)(2,1)}, bf16[256,1280]{1,0:T(8,128)(2,1)}, u32[]{:S(2)}, u32[]{:S(2)}) %collective-permute-start.31) | collective-permute-done | bytes 655392 | tf_op jit(solution)/shard_map/ppermute | solution.py:98
  659.6 22.4 %attention_backward.2 = bf16[4096,384]{1,0:T(8,128)(2,1)S(1)} custom-call(s32[2]{0:T(128)S(1)} %copy-done.29, bf16[4096,768]{1,0:T(8,128)(2,1)} %copy-done.2, bf16[8,640,128]{2,1,0:T(8,128)(2,1)S(1)} %copy-done.16, f32[8,640,128]{2,1,0:T(8,128)S(1)} %copy-done.20, f32[8,8,640]{2,1,0:T(8,128)S(1)} %copy-done.25, f32[4096,128]{1,0:T(8,128)S(1)} %copy-done.4, ...), custom_call_target="tpu_custom_call" | custom-call | flops 2684354560 | bytes 10485760 | tf_op jit(solution)/shard_map/attention_backward/pallas_call | solution.py:293
  698.9 37.7 %attention_backward.3 = bf16[4096,384]{1,0:T(8,128)(2,1)S(1)} custom-call(s32[2]{0:T(128)S(1)} %copy-done.29, bf16[4096,768]{1,0:T(8,128)(2,1)} %copy-done.2, bf16[8,640,128]{2,1,0:T(8,128)(2,1)S(1)} %copy-done.17, f32[8,640,128]{2,1,0:T(8,128)S(1)} %copy-done.21, f32[8,8,640]{2,1,0:T(8,128)S(1)} %copy-done.26, f32[4096,128]{1,0:T(8,128)S(1)} %copy-done.4, ...), custom_call_target="tpu_custom_call" | custom-call | flops 10737418240 | bytes 10485760 | tf_op jit(solution)/shard_map/attention_backward/pallas_call | solution.py:293
  765.8 24.4 %collective-permute-done.37 = bf16[256,1280]{1,0:T(8,128)(2,1)S(1)} collective-permute-done((bf16[256,1280]{1,0:T(8,128)(2,1)S(1)}, bf16[256,1280]{1,0:T(8,128)(2,1)S(1)}, u32[]{:S(2)}, u32[]{:S(2)}) %collective-permute-start.37) | collective-permute-done | bytes 655392 | tf_op jit(solution)/shard_map/ppermute | solution.py:98
  795.1 4.4 convolution_convert_fusion.7
  799.5 4.3 convolution_convert_fusion.8
  805.3 4.3 copy.336
  821.1 13.1 %collective-permute-done.38 = bf16[512,1280]{1,0:T(8,128)(2,1)S(1)} collective-permute-done((bf16[512,1280]{1,0:T(8,128)(2,1)S(1)}, bf16[512,1280]{1,0:T(8,128)(2,1)S(1)}, u32[]{:S(2)}, u32[]{:S(2)}) %collective-permute-start.38) | collective-permute-done | bytes 1310752 | tf_op jit(solution)/shard_map/ppermute | solution.py:98
  844.3 14.7 %collective-permute-done.43 = bf16[512,1280]{1,0:T(8,128)(2,1)} collective-permute-done((bf16[512,1280]{1,0:T(8,128)(2,1)}, bf16[512,1280]{1,0:T(8,128)(2,1)}, u32[]{:S(2)}, u32[]{:S(2)}) %collective-permute-start.43) | collective-permute-done | bytes 1310752 | tf_op jit(solution)/shard_map/ppermute | solution.py:98
  859.1 3.6 collective-permute-done.42
  862.7 5.4 fusion.30
  869.2 5.1 all-to-all-start.4
  883.7 4.0 all-to-all-done.4
  898.6 7.1 collective-permute-done.45
  905.7 4.3 collective-permute-done.44
  912.8 4.3 fusion.14
  (445 shorter events, 253.4 us)
Async XLA Ops:
  7.2 91.1 %all-gather.5.cloned.1.call-start = ((), (), s32[]{:S(2)}) async-start(), calls=%async_computation.13 | async-start | bytes 2867200 | tf_op jit(solution)/shard_map/all_gather | solution.py:502
  7.2 44.3 %collective-permute-start.1 = (bf16[512,1280]{1,0:T(8,128)(2,1)}, bf16[512,1280]{1,0:T(8,128)(2,1)S(1)}, u32[]{:S(2)}, u32[]{:S(2)}) collective-permute-start(bf16[512,1280]{1,0:T(8,128)(2,1)} %bitcast.134), channel_id=1, source_target_pairs={{0,1},{2,0},{4,2},{6,4},{7,6},{5,7},{3,5},{1,3},{8,9},{10,8},{12,1... | collective-permute-start | bytes 3932168 | tf_op jit(solution)/shard_map/ppermute | solution.py:72
  8.9 42.7 %collective-permute-start = (bf16[512,1280]{1,0:T(8,128)(2,1)}, bf16[512,1280]{1,0:T(8,128)(2,1)}, u32[]{:S(2)}, u32[]{:S(2)}) collective-permute-start(bf16[512,1280]{1,0:T(8,128)(2,1)} %bitcast.135), channel_id=1, source_target_pairs={{0,2},{2,4},{4,6},{6,7},{7,5},{5,3},{3,1},{1,0},{8,10},{10,12},{12... | collective-permute-start | bytes 3932168 | tf_op jit(solution)/shard_map/ppermute | solution.py:72
  58.1 144.6 %all-gather.7.cloned.1.call-start = ((), (), s32[]{:S(2)}) async-start(), calls=%async_computation.14 | async-start | bytes 2856960 | tf_op jit(solution)/shard_map/all_gather | solution.py:513
  65.6 29.0 %collective-permute-start.2 = (bf16[512,1280]{1,0:T(8,128)(2,1)}, bf16[512,1280]{1,0:T(8,128)(2,1)}, u32[]{:S(2)}, u32[]{:S(2)}) collective-permute-start(bf16[512,1280]{1,0:T(8,128)(2,1)} %collective-permute-done.tok_ref), channel_id=1, source_target_pairs={{0,2},{2,4},{4,6},{6,7},{7,5},{5,3},{3,1},{1,0},{8,10},{10,12},{12... | collective-permute-start | bytes 3932168 | tf_op jit(solution)/shard_map/ppermute | solution.py:72
  66.2 28.4 %collective-permute-start.3 = (bf16[512,1280]{1,0:T(8,128)(2,1)S(1)}, bf16[512,1280]{1,0:T(8,128)(2,1)}, u32[]{:S(2)}, u32[]{:S(2)}) collective-permute-start(bf16[512,1280]{1,0:T(8,128)(2,1)S(1)} %collective-permute-done.1.tok_ref), channel_id=1, source_target_pairs={{0,1},{2,0},{4,2},{6,4},{7,6},{5,7},{3,5},{1,3},{8,9},{10,8},{12,1... | collective-permute-start | bytes 3932168 | tf_op jit(solution)/shard_map/ppermute | solution.py:72
  94.6 31.6 %collective-permute-start.4 = (bf16[512,1280]{1,0:T(8,128)(2,1)}, bf16[512,1280]{1,0:T(8,128)(2,1)}, u32[]{:S(2)}, u32[]{:S(2)}) collective-permute-start(bf16[512,1280]{1,0:T(8,128)(2,1)} %collective-permute-done.2.tok_ref), channel_id=1, source_target_pairs={{0,2},{2,4},{4,6},{6,7},{7,5},{5,3},{3,1},{1,0},{8,10},{10,12},{12... | collective-permute-start | bytes 3932168 | tf_op jit(solution)/shard_map/ppermute | solution.py:72
  95.2 31.0 %collective-permute-start.5 = (bf16[512,1280]{1,0:T(8,128)(2,1)}, bf16[512,1280]{1,0:T(8,128)(2,1)}, u32[]{:S(2)}, u32[]{:S(2)}) collective-permute-start(bf16[512,1280]{1,0:T(8,128)(2,1)} %collective-permute-done.3.tok_ref), channel_id=1, source_target_pairs={{0,1},{2,0},{4,2},{6,4},{7,6},{5,7},{3,5},{1,3},{8,9},{10,8},{12,1... | collective-permute-start | bytes 3932168 | tf_op jit(solution)/shard_map/ppermute | solution.py:72
  126.2 114.3 %all-gather.9.cloned.1.call-start = ((), (), s32[]{:S(2)}) async-start(), calls=%async_computation.15 | async-start | bytes 4096000 | tf_op jit(solution)/shard_map/all_gather | solution.py:524
  157.3 45.5 %collective-permute-start.9 = (bf16[512,1280]{1,0:T(8,128)(2,1)}, bf16[512,1280]{1,0:T(8,128)(2,1)S(1)}, u32[]{:S(2)}, u32[]{:S(2)}) collective-permute-start(bf16[512,1280]{1,0:T(8,128)(2,1)} %bitcast.2.refs_1_), channel_id=1, source_target_pairs={{0,1},{2,0},{4,2},{6,4},{7,6},{5,7},{3,5},{1,3},{8,9},{10,8},{12,1... | collective-permute-start | bytes 3932168 | tf_op jit(solution)/shard_map/ppermute | solution.py:72
  159.9 42.8 %collective-permute-start.8 = (bf16[512,1280]{1,0:T(8,128)(2,1)}, bf16[512,1280]{1,0:T(8,128)(2,1)}, u32[]{:S(2)}, u32[]{:S(2)}) collective-permute-start(bf16[512,1280]{1,0:T(8,128)(2,1)} %bitcast.2.refs_1_), channel_id=1, source_target_pairs={{0,2},{2,4},{4,6},{6,7},{7,5},{5,3},{3,1},{1,0},{8,10},{10,12},{12... | collective-permute-start | bytes 3932168 | tf_op jit(solution)/shard_map/ppermute | solution.py:72
  205.3 32.3 %all-to-all-start.2 = ((bf16[8,640,128]{2,1,0:T(8,128)(2,1)}), bf16[8,640,128]{2,1,0:T(8,128)(2,1)S(1)}, u32[]{:S(2)}, u32[]{:S(2)}) async-start(bf16[8,640,128]{2,1,0:T(8,128)(2,1)} %get-tuple-element.223), calls=%async_computation.2 | async-start | bytes 2621440 | tf_op jit(solution)/shard_map/all_to_all | solution.py:526
  212.4 127.1 %all-gather.11.cloned.1.call-start = ((), (), s32[]{:S(2)}) async-start(), calls=%async_computation.16 | async-start | bytes 8601600 | tf_op jit(solution)/shard_map/all_gather | solution.py:540
  212.4 50.7 %collective-permute-start.10 = (bf16[512,1280]{1,0:T(8,128)(2,1)}, bf16[512,1280]{1,0:T(8,128)(2,1)}, u32[]{:S(2)}, u32[]{:S(2)}) collective-permute-start(bf16[512,1280]{1,0:T(8,128)(2,1)} %collective-permute-done.8.refs_2_), channel_id=1, source_target_pairs={{0,2},{2,4},{4,6},{6,7},{7,5},{5,3},{3,1},{1,0},{8,10},{10,12},{12... | collective-permute-start | bytes 3932168 | tf_op jit(solution)/shard_map/ppermute | solution.py:72
  213.0 50.2 %collective-permute-start.11 = (bf16[512,1280]{1,0:T(8,128)(2,1)}, bf16[512,1280]{1,0:T(8,128)(2,1)}, u32[]{:S(2)}, u32[]{:S(2)}) collective-permute-start(bf16[512,1280]{1,0:T(8,128)(2,1)} %copy-done.82), channel_id=1, source_target_pairs={{0,1},{2,0},{4,2},{6,4},{7,6},{5,7},{3,5},{1,3},{8,9},{10,8},{12,1... | collective-permute-start | bytes 3932168 | tf_op jit(solution)/shard_map/ppermute | solution.py:72
  264.5 244.3 %reduce-scatter.15.cloned.1.call-start = ((), (), s32[]{:S(2)}) async-start(), calls=%async_computation.18 | async-start | bytes 2867200 | tf_op jit(solution)/shard_map/reduce_scatter | solution.py:606
  264.5 30.4 %collective-permute-start.13 = (bf16[512,1280]{1,0:T(8,128)(2,1)}, bf16[512,1280]{1,0:T(8,128)(2,1)}, u32[]{:S(2)}, u32[]{:S(2)}) collective-permute-start(bf16[512,1280]{1,0:T(8,128)(2,1)} %multiply_convert_fusion.refs_0_), channel_id=1, source_target_pairs={{0,1},{2,0},{4,2},{6,4},{7,6},{5,7},{3,5},{1,3},{8,9},{10,8},{12,1... | collective-permute-start | bytes 3932168 | tf_op jit(solution)/shard_map/ppermute | solution.py:72
  265.2 29.8 %collective-permute-start.12 = (bf16[512,1280]{1,0:T(8,128)(2,1)}, bf16[512,1280]{1,0:T(8,128)(2,1)}, u32[]{:S(2)}, u32[]{:S(2)}) collective-permute-start(bf16[512,1280]{1,0:T(8,128)(2,1)} %multiply_convert_fusion.refs_0_), channel_id=1, source_target_pairs={{0,2},{2,4},{4,6},{6,7},{7,5},{5,3},{3,1},{1,0},{8,10},{10,12},{12... | collective-permute-start | bytes 3932168 | tf_op jit(solution)/shard_map/ppermute | solution.py:72
  295.0 42.4 %collective-permute-start.14 = (bf16[512,1280]{1,0:T(8,128)(2,1)}, bf16[512,1280]{1,0:T(8,128)(2,1)}, u32[]{:S(2)}, u32[]{:S(2)}) collective-permute-start(bf16[512,1280]{1,0:T(8,128)(2,1)} %collective-permute-done.12.refs_0_), channel_id=1, source_target_pairs={{0,2},{2,4},{4,6},{6,7},{7,5},{5,3},{3,1},{1,0},{8,10},{10,12},{12... | collective-permute-start | bytes 3932168 | tf_op jit(solution)/shard_map/ppermute | solution.py:72
  295.2 42.1 %collective-permute-start.15 = (bf16[512,1280]{1,0:T(8,128)(2,1)}, bf16[512,1280]{1,0:T(8,128)(2,1)}, u32[]{:S(2)}, u32[]{:S(2)}) collective-permute-start(bf16[512,1280]{1,0:T(8,128)(2,1)} %collective-permute-done.13.refs_1_), channel_id=1, source_target_pairs={{0,1},{2,0},{4,2},{6,4},{7,6},{5,7},{3,5},{1,3},{8,9},{10,8},{12,1... | collective-permute-start | bytes 3932168 | tf_op jit(solution)/shard_map/ppermute | solution.py:72
  337.4 34.6 %collective-permute-start.16 = (bf16[512,1280]{1,0:T(8,128)(2,1)}, bf16[512,1280]{1,0:T(8,128)(2,1)S(1)}, u32[]{:S(2)}, u32[]{:S(2)}) collective-permute-start(bf16[512,1280]{1,0:T(8,128)(2,1)} %collective-permute-done.10.refs_2_), channel_id=1, source_target_pairs={{0,2},{2,4},{4,6},{6,7},{7,5},{5,3},{3,1},{1,0},{8,10},{10,12},{12... | collective-permute-start | bytes 3932168 | tf_op jit(solution)/shard_map/ppermute | solution.py:72
  337.6 34.4 %collective-permute-start.17 = (bf16[512,1280]{1,0:T(8,128)(2,1)}, bf16[512,1280]{1,0:T(8,128)(2,1)S(1)}, u32[]{:S(2)}, u32[]{:S(2)}) collective-permute-start(bf16[512,1280]{1,0:T(8,128)(2,1)} %collective-permute-done.11.refs_3_), channel_id=1, source_target_pairs={{0,1},{2,0},{4,2},{6,4},{7,6},{5,7},{3,5},{1,3},{8,9},{10,8},{12,1... | collective-permute-start | bytes 3932168 | tf_op jit(solution)/shard_map/ppermute | solution.py:72
  372.0 136.8 %reduce-scatter.13.cloned.1.call-start = ((), (), s32[]{:S(2)}) async-start(), calls=%async_computation.17 | async-start | bytes 5734400 | tf_op jit(solution)/shard_map/reduce_scatter | solution.py:606
  373.5 196.6 %reduce-scatter.17.cloned.1.call-start = ((), (), s32[]{:S(2)}) async-start(), calls=%async_computation.19 | async-start | bytes 5734400 | tf_op jit(solution)/shard_map/reduce_scatter | solution.py:629
  373.5 44.0 %collective-permute-start.18 = (bf16[512,1280]{1,0:T(8,128)(2,1)}, bf16[512,1280]{1,0:T(8,128)(2,1)}, u32[]{:S(2)}, u32[]{:S(2)}) collective-permute-start(bf16[512,1280]{1,0:T(8,128)(2,1)} %collective-permute-done.14.refs_0_), channel_id=1, source_target_pairs={{0,2},{2,4},{4,6},{6,7},{7,5},{5,3},{3,1},{1,0},{8,10},{10,12},{12... | collective-permute-start | bytes 3932168 | tf_op jit(solution)/shard_map/ppermute | solution.py:72
  373.7 43.8 %collective-permute-start.19 = (bf16[512,1280]{1,0:T(8,128)(2,1)}, bf16[512,1280]{1,0:T(8,128)(2,1)}, u32[]{:S(2)}, u32[]{:S(2)}) collective-permute-start(bf16[512,1280]{1,0:T(8,128)(2,1)} %collective-permute-done.15.refs_1_), channel_id=1, source_target_pairs={{0,1},{2,0},{4,2},{6,4},{7,6},{5,7},{3,5},{1,3},{8,9},{10,8},{12,1... | collective-permute-start | bytes 3932168 | tf_op jit(solution)/shard_map/ppermute | solution.py:72
  417.5 42.1 %collective-permute-start.20 = (bf16[512,1280]{1,0:T(8,128)(2,1)}, bf16[512,1280]{1,0:T(8,128)(2,1)}, u32[]{:S(2)}, u32[]{:S(2)}) collective-permute-start(bf16[512,1280]{1,0:T(8,128)(2,1)} %collective-permute-done.18.refs_0_), channel_id=1, source_target_pairs={{0,2},{2,4},{4,6},{6,7},{7,5},{5,3},{3,1},{1,0},{8,10},{10,12},{12... | collective-permute-start | bytes 3932168 | tf_op jit(solution)/shard_map/ppermute | solution.py:593
  418.0 41.7 %collective-permute-start.21 = (bf16[512,1280]{1,0:T(8,128)(2,1)}, bf16[512,1280]{1,0:T(8,128)(2,1)}, u32[]{:S(2)}, u32[]{:S(2)}) collective-permute-start(bf16[512,1280]{1,0:T(8,128)(2,1)} %copy-done.83), channel_id=1, source_target_pairs={{0,1},{2,0},{4,2},{6,4},{7,6},{5,7},{3,5},{1,3},{8,9},{10,8},{12,1... | collective-permute-start | bytes 3932168 | tf_op jit(solution)/shard_map/ppermute | solution.py:594
  505.5 133.1 %reduce-scatter.19.cloned.1.call-start = ((), (), s32[]{:S(2)}) async-start(), calls=%async_computation.20 | async-start | bytes 5734400 | tf_op jit(solution)/shard_map/reduce_scatter | solution.py:629
  536.0 27.0 %collective-permute-start.27 = (bf16[512,1280]{1,0:T(8,128)(2,1)}, bf16[512,1280]{1,0:T(8,128)(2,1)S(1)}, u32[]{:S(2)}, u32[]{:S(2)}) collective-permute-start(bf16[512,1280]{1,0:T(8,128)(2,1)} %add_convert_fusion.11), channel_id=1, source_target_pairs={{0,1},{2,0},{4,2},{6,4},{7,6},{5,7},{3,5},{1,3},{8,9},{10,8},{12,1... | collective-permute-start | bytes 3932168 | tf_op jit(solution)/shard_map/ppermute | solution.py:98
  601.5 37.1 %all-to-all-start.3 = ((bf16[8,640,128]{2,1,0:T(8,128)(2,1)}), bf16[8,640,128]{2,1,0:T(8,128)(2,1)S(1)}, u32[]{:S(2)}, u32[]{:S(2)}) async-start(bf16[8,640,128]{2,1,0:T(8,128)(2,1)} %pad_maximum_fusion.6), calls=%async_computation.6 | async-start | bytes 2621440 | tf_op jit(solution)/shard_map/all_to_all | solution.py:650
  607.3 76.3 %reduce-scatter.21.cloned.1.call-start = ((), (), s32[]{:S(2)}) async-start(), calls=%async_computation.21 | async-start | bytes 4096000 | tf_op jit(solution)/shard_map/reduce_scatter | solution.py:657
  609.9 26.9 %collective-permute-start.31 = (bf16[256,1280]{1,0:T(8,128)(2,1)}, bf16[256,1280]{1,0:T(8,128)(2,1)}, u32[]{:S(2)}, u32[]{:S(2)}) collective-permute-start(bf16[256,1280]{1,0:T(8,128)(2,1)} %get-tuple-element.392), channel_id=1, source_target_pairs={{0,1},{2,0},{4,2},{6,4},{7,6},{5,7},{3,5},{1,3},{8,9},{10,8},{12,1... | collective-permute-start | bytes 1966088 | tf_op jit(solution)/shard_map/ppermute | solution.py:98
  611.3 27.3 %collective-permute-start.30 = (bf16[256,1280]{1,0:T(8,128)(2,1)S(1)}, bf16[256,1280]{1,0:T(8,128)(2,1)}, u32[]{:S(2)}, u32[]{:S(2)}) collective-permute-start(bf16[256,1280]{1,0:T(8,128)(2,1)S(1)} %get-tuple-element.393), channel_id=1, source_target_pairs={{0,2},{2,4},{4,6},{6,7},{7,5},{5,3},{3,1},{1,0},{8,10},{10,12},{12... | collective-permute-start | bytes 1966088 | tf_op jit(solution)/shard_map/ppermute | solution.py:98
  638.7 202.4 %reduce-scatter.27.cloned.1.call-start = ((), (), s32[]{:S(2)}) async-start(), calls=%async_computation.24 | async-start | bytes 2856960
  643.3 40.4 %collective-permute-start.33 = (bf16[512,1280]{1,0:T(8,128)(2,1)}, bf16[512,1280]{1,0:T(8,128)(2,1)}, u32[]{:S(2)}, u32[]{:S(2)}) collective-permute-start(bf16[512,1280]{1,0:T(8,128)(2,1)} %pad_maximum_fusion.8), channel_id=1, source_target_pairs={{0,1},{2,0},{4,2},{6,4},{7,6},{5,7},{3,5},{1,3},{8,9},{10,8},{12,1... | collective-permute-start | bytes 3932168 | tf_op jit(solution)/shard_map/ppermute | solution.py:98
  646.3 37.4 %collective-permute-start.32 = (bf16[512,1280]{1,0:T(8,128)(2,1)}, bf16[512,1280]{1,0:T(8,128)(2,1)}, u32[]{:S(2)}, u32[]{:S(2)}) collective-permute-start(bf16[512,1280]{1,0:T(8,128)(2,1)} %pad_maximum_fusion.7), channel_id=1, source_target_pairs={{0,2},{2,4},{4,6},{6,7},{7,5},{5,3},{3,1},{1,0},{8,10},{10,12},{12... | collective-permute-start | bytes 3932168 | tf_op jit(solution)/shard_map/ppermute | solution.py:98
  686.9 49.8 %collective-permute-start.34 = (bf16[512,1280]{1,0:T(8,128)(2,1)}, bf16[512,1280]{1,0:T(8,128)(2,1)}, u32[]{:S(2)}, u32[]{:S(2)}) collective-permute-start(bf16[512,1280]{1,0:T(8,128)(2,1)} %add_convert_fusion.8), channel_id=1, source_target_pairs={{0,2},{2,4},{4,6},{6,7},{7,5},{5,3},{3,1},{1,0},{8,10},{10,12},{12... | collective-permute-start | bytes 3932168 | tf_op jit(solution)/shard_map/ppermute | solution.py:98
  689.8 46.9 %collective-permute-start.35 = (bf16[512,1280]{1,0:T(8,128)(2,1)}, bf16[512,1280]{1,0:T(8,128)(2,1)}, u32[]{:S(2)}, u32[]{:S(2)}) collective-permute-start(bf16[512,1280]{1,0:T(8,128)(2,1)} %add_convert_fusion.7), channel_id=1, source_target_pairs={{0,1},{2,0},{4,2},{6,4},{7,6},{5,7},{3,5},{1,3},{8,9},{10,8},{12,1... | collective-permute-start | bytes 3932168 | tf_op jit(solution)/shard_map/ppermute | solution.py:98
  693.3 149.6 %reduce-scatter.25.cloned.1.call-start = ((), (), s32[]{:S(2)}) async-start(), calls=%async_computation.23 | async-start | bytes 2867200
  739.5 65.8 %collective-permute-start.41 = (bf16[512,1280]{1,0:T(8,128)(2,1)S(1)}, bf16[512,1280]{1,0:T(8,128)(2,1)}, u32[]{:S(2)}, u32[]{:S(2)}) collective-permute-start(bf16[512,1280]{1,0:T(8,128)(2,1)S(1)} %add_convert_fusion.5), channel_id=1, source_target_pairs={{0,1},{2,0},{4,2},{6,4},{7,6},{5,7},{3,5},{1,3},{8,9},{10,8},{12,1... | collective-permute-start | bytes 3932168 | tf_op jit(solution)/shard_map/ppermute | solution.py:98
  741.7 63.6 %collective-permute-start.40 = (bf16[512,1280]{1,0:T(8,128)(2,1)S(1)}, bf16[512,1280]{1,0:T(8,128)(2,1)}, u32[]{:S(2)}, u32[]{:S(2)}) collective-permute-start(bf16[512,1280]{1,0:T(8,128)(2,1)S(1)} %add_convert_fusion.6), channel_id=1, source_target_pairs={{0,2},{2,4},{4,6},{6,7},{7,5},{5,3},{3,1},{1,0},{8,10},{10,12},{12... | collective-permute-start | bytes 3932168 | tf_op jit(solution)/shard_map/ppermute | solution.py:98
  749.6 40.7 %collective-permute-start.37 = (bf16[256,1280]{1,0:T(8,128)(2,1)S(1)}, bf16[256,1280]{1,0:T(8,128)(2,1)S(1)}, u32[]{:S(2)}, u32[]{:S(2)}) collective-permute-start(bf16[256,1280]{1,0:T(8,128)(2,1)S(1)} %get-tuple-element.390), channel_id=1, source_target_pairs={{0,1},{2,0},{4,2},{6,4},{7,6},{5,7},{3,5},{1,3},{8,9},{10,8},{12,1... | collective-permute-start | bytes 1966088 | tf_op jit(solution)/shard_map/ppermute | solution.py:98
  750.2 40.9 %collective-permute-start.36 = (bf16[256,1280]{1,0:T(8,128)(2,1)S(1)}, bf16[256,1280]{1,0:T(8,128)(2,1)S(1)}, u32[]{:S(2)}, u32[]{:S(2)}) collective-permute-start(bf16[256,1280]{1,0:T(8,128)(2,1)S(1)} %get-tuple-element.391), channel_id=1, source_target_pairs={{0,2},{2,4},{4,6},{6,7},{7,5},{5,3},{3,1},{1,0},{8,10},{10,12},{12... | collective-permute-start | bytes 1966088 | tf_op jit(solution)/shard_map/ppermute | solution.py:98
  793.0 28.0 %collective-permute-start.39 = (bf16[512,1280]{1,0:T(8,128)(2,1)}, bf16[512,1280]{1,0:T(8,128)(2,1)}, u32[]{:S(2)}, u32[]{:S(2)}) collective-permute-start(bf16[512,1280]{1,0:T(8,128)(2,1)} %pad_maximum_fusion.10), channel_id=1, source_target_pairs={{0,1},{2,0},{4,2},{6,4},{7,6},{5,7},{3,5},{1,3},{8,9},{10,8},{12,1... | collective-permute-start | bytes 3932168 | tf_op jit(solution)/shard_map/ppermute | solution.py:98
  809.7 107.4 %reduce-scatter.23.cloned.1.call-start = ((), (), s32[]{:S(2)}) async-start(), calls=%async_computation.22 | async-start | bytes 5734400 | tf_op jit(solution)/shard_map/reduce_scatter | solution.py:697
  878.1 27.5 %collective-permute-start.45 = (bf16[512,1280]{1,0:T(8,128)(2,1)}, bf16[512,1280]{1,0:T(8,128)(2,1)}, u32[]{:S(2)}, u32[]{:S(2)}) collective-permute-start(bf16[512,1280]{1,0:T(8,128)(2,1)} %add_convert_fusion), channel_id=1, source_target_pairs={{0,1},{2,0},{4,2},{6,4},{7,6},{5,7},{3,5},{1,3},{8,9},{10,8},{12,1... | collective-permute-start | bytes 3932168 | tf_op jit(solution)/shard_map/ppermute | solution.py:98
  882.3 27.6 %collective-permute-start.44 = (bf16[512,1280]{1,0:T(8,128)(2,1)}, bf16[512,1280]{1,0:T(8,128)(2,1)}, u32[]{:S(2)}, u32[]{:S(2)}) collective-permute-start(bf16[512,1280]{1,0:T(8,128)(2,1)} %add_convert_fusion.1), channel_id=1, source_target_pairs={{0,2},{2,4},{4,6},{6,7},{7,5},{5,3},{3,1},{1,0},{8,10},{10,12},{12... | collective-permute-start | bytes 3932168 | tf_op jit(solution)/shard_map/ppermute | solution.py:98
  (103 other events, 1359.3 us)
Sparse Core Ops, SparseCore 0:
  51.7 23.5 all-gather.4
  126.3 71.1 all-gather.6
  205.4 31.2 all-gather.8
  264.6 48.8 all-gather.10
  372.2 31.9 reduce-scatter.14
  406.7 46.9 reduce-scatter.12
  505.6 46.5 reduce-scatter.16
  554.9 46.9 reduce-scatter.18
  638.8 37.8 reduce-scatter.20
  693.4 100.1 reduce-scatter.26
  809.8 32.0 reduce-scatter.24
  862.8 45.9 reduce-scatter.22

commit v3 on v2

--- a/solution.py
+++ b/solution.py
@@ -228,7 +228,7 @@
     )(own, qkv)
 
 
-def attention_backward(own, qkv, grads, attended, lse, cosine, sine, blocks, rows, count, slot, start):
+def attention_backward(own, qkv, grads, attended, lse, cosine, sine, blocks, rows, count, slot, start, buffer=None):
     scale = 1.0 / math.sqrt(HEAD)
     scale_two = math.log2(math.e) * scale
     length = qkv.shape[0]
@@ -236,7 +236,8 @@
     cols = 3 * HEAD
     here = slice(start, start + count)
 
-    def kernel(own_ref, qkv_ref, grad_ref, att_ref, lse_ref, cos_ref, sin_ref, out_ref, key_sum, value_sum):
+    def kernel(own_ref, qkv_ref, grad_ref, att_ref, lse_ref, cos_ref, sin_ref, *rest):
+        out_ref, key_sum, value_sum = rest[-3:]
         block = pl.program_id(0)
         offset = own_ref[slot]
 
@@ -290,9 +291,10 @@
 
             lax.fori_loop(0, blocks, finish, 0)
 
+    aliased = () if buffer is None else (buffer,)
     return pl.pallas_call(
         kernel,
-        out_shape=jax.ShapeDtypeStruct((length, cols), bf16),
+        out_shape=jax.ShapeDtypeStruct((length, 2 * cols), bf16),
         grid_spec=pltpu.PrefetchScalarGridSpec(
             num_scalar_prefetch=1,
             grid=(blocks,),
@@ -303,16 +305,18 @@
                 pl.BlockSpec((1, 8, tall), lambda s, o: (s, 0, 0)),
                 spec((length, HEAD), lambda s, o: (0, 0), True),
                 spec((length, HEAD), lambda s, o: (0, 0), True),
-            ],
-            out_specs=spec((length, cols), lambda s, o: (0, 0), True),
+            ]
+            + [pl.BlockSpec(memory_space=pl.ANY)] * len(aliased),
+            out_specs=spec((length, cols), lambda s, o: (0, slot), True),
             scratch_shapes=[pltpu.VMEM((length, HEAD), f32)] * 2,
         ),
+        input_output_aliases={7 + i: i for i in range(len(aliased))},
         compiler_params=pltpu.CompilerParams(vmem_limit_bytes=40 * 1024 * 1024),
         cost_estimate=pl.CostEstimate(
             flops=10 * length * count * blocks * HEAD // 2, bytes_accessed=20 * length * HEAD, transcendentals=length * count * blocks // 2
         ),
         name="attention_backward",
-    )(own, qkv, grads, attended, lse, cosine, sine)
+    )(own, qkv, grads, attended, lse, cosine, sine, *aliased)
 
 
 def expert_call(members, offsets, hidden, grads, rank_row, rank_col, route, w_gate, w_up, w_down, capacity, first, total, buffers):
@@ -415,11 +419,49 @@
     )
 
 
-def swiglu_back(grad_act, gate_pre, up_pre):
-    sigma = jax.nn.sigmoid(gate_pre)
-    grad_up = (grad_act * gate_pre * sigma).astype(bf16)
-    grad_gate = (grad_act * up_pre * sigma * (1.0 + gate_pre * (1.0 - sigma))).astype(bf16)
-    return grad_gate, grad_up
+def shared_expert(hidden, grads, weights, inner):
+    rows, width = hidden.shape
+    tile = rows // 2
+
+    def kernel(h_ref, z_ref, wg_ref, wu_ref, wd_ref, branch_ref, back_ref, act_ref, pre_ref):
+        gate_pre = dot(h_ref[...], wg_ref[...])
+        up_pre = dot(h_ref[...], wu_ref[...])
+        grad_act = dot(z_ref[...], wd_ref[...])
+        sigma = 1.0 / (1.0 + jnp.exp(-gate_pre))
+        act = gate_pre * sigma
+        low = (act * up_pre).astype(bf16)
+        act_ref[...] = low
+        grad_up = (grad_act * act).astype(bf16)
+        grad_gate = (grad_act * up_pre * sigma * (1.0 + gate_pre * (1.0 - sigma))).astype(bf16)
+        pre_ref[:, :inner] = grad_gate
+        pre_ref[:, inner:] = grad_up
+        branch_ref[...] = dot_nt(low, wd_ref[...])
+        back_ref[...] = dot_nt(grad_gate, wg_ref[...]) + dot_nt(grad_up, wu_ref[...])
+
+    by_row = lambda i: (i, 0)
+    return pl.pallas_call(
+        kernel,
+        grid=(rows // tile,),
+        out_shape=(
+            jax.ShapeDtypeStruct((rows, width), f32),
+            jax.ShapeDtypeStruct((rows, width), f32),
+            jax.ShapeDtypeStruct((rows, inner), bf16),
+            jax.ShapeDtypeStruct((rows, 2 * inner), bf16),
+        ),
+        in_specs=[pl.BlockSpec((tile, width), by_row)] * 2
+        + [pl.BlockSpec((width, inner), lambda i, n=n: (0, n), pipeline_mode=pl.Buffered(1)) for n in range(3)],
+        out_specs=[
+            pl.BlockSpec((tile, width), by_row),
+            pl.BlockSpec((tile, width), by_row),
+            pl.BlockSpec((tile, inner), by_row),
+            pl.BlockSpec((tile, 2 * inner), by_row),
+        ],
+        compiler_params=pltpu.CompilerParams(vmem_limit_bytes=40 * 1024 * 1024),
+        cost_estimate=pl.CostEstimate(
+            flops=12 * rows * width * inner, bytes_accessed=12 * rows * width + 6 * width * inner, transcendentals=rows * inner
+        ),
+        name="shared_expert",
+    )(hidden, grads, weights, weights, weights)
 
 
 def shards(
@@ -538,10 +580,6 @@
 
     hidden_two, grad_pieces[2], packed = tie(hidden_two, grad_pieces[2], packed)
     packed = lax.all_gather(packed[:, width:], "dp", axis=0, tiled=True)
-    full_gate = packed[:, :inner]
-    full_up = packed[:, inner : 2 * inner]
-    full_down_t = packed[:, 2 * inner :]
-
     part_y, part_x, buffers = {}, {}, [None]
 
     def run_experts(step, arrived):
@@ -575,13 +613,8 @@
         return outs[len(group)]
 
     def run_shared(hidden, grads):
-        gate_pre = dot(hidden, full_gate)
-        up_pre = dot(hidden, full_up)
-        act = (jax.nn.silu(gate_pre) * up_pre).astype(bf16)
-        grad_gate_pre, grad_up_pre = swiglu_back(dot(grads, full_down_t), gate_pre, up_pre)
-        back = dot_nt(grad_gate_pre, full_gate) + dot_nt(grad_up_pre, full_up)
-        grads_in = dot_tn(hidden, jnp.concatenate([grad_gate_pre, grad_up_pre], axis=1)).astype(bf16)
-        return dot_nt(act, full_down_t), back, grads_in, dot_tn(grads, act).astype(bf16)
+        branch, back, act, grad_pre = shared_expert(hidden, grads, packed, inner)
+        return branch, back, dot_tn(hidden, grad_pre).astype(bf16), dot_tn(grads, act).astype(bf16)
 
     up, down, arrived = hidden_two, hidden_two, (hidden_two,)
     for step in range(1, half + 1):
@@ -664,18 +697,15 @@
     dense = lax.psum_scatter(jnp.concatenate(dense, axis=1), "ep", scatter_dimension=0, tiled=True).astype(f32)
     came_y = ring.scatter_step(part_y, came_y, half - 1)
     grad_main = attention_backward(
-        own, qkv, head_grads, attended, lse, cosine, sine, ep, rows, main_rows, 0, 0
-    )
-    grad_main, grad_side, came_y, expert_grads[:2] = tie(grad_main, grad_side, came_y, expert_grads[:2])
+        own, qkv, head_grads, attended, lse, cosine, sine, ep, rows, main_rows, 0, 0, grad_side
+    )
+    grad_qkv, came_y, expert_grads[:2] = tie(grad_main, came_y, expert_grads[:2])
     came_y = ring.scatter_step(part_y, came_y, half)
 
     part_h = {}
     for offset in range(-half + 1, half + 1):
-        first = ring.member(offset) * rows
-        part_h[offset] = (
-            dot_nt(lax.dynamic_slice_in_dim(grad_main, first, rows, 0), w_cat[:, : 3 * HEAD])
-            + dot_nt(lax.dynamic_slice_in_dim(grad_side, first, rows, 0), w_cat[:, 3 * HEAD :])
-        ).astype(bf16)
+        block = lax.dynamic_slice_in_dim(grad_qkv, ring.member(offset) * rows, rows, 0)
+        part_h[offset] = dot_nt(block, w_cat).astype(bf16)
     came = None
     inverse_one = lax.rsqrt(jnp.mean(residual * residual, axis=-1, keepdims=True) + epsilon)
     for step in range(1, half + 1):
@@ -684,8 +714,7 @@
             next_parts = [part_h[offset] for offset in (half - 1, 1 - half)]
             came, next_parts, hidden_all = tie(came, next_parts, hidden_all)
             part_h[half - 1], part_h[1 - half] = next_parts
-            head_sums = [dot_tn(hidden_all, grad_main), dot_tn(hidden_all, grad_side), gain_columns]
-            head_sums = jnp.concatenate(head_sums, axis=1).astype(bf16)
+            head_sums = jnp.concatenate([dot_tn(hidden_all, grad_qkv), gain_columns], axis=1).astype(bf16)
             came_y, head_sums = tie(came_y, head_sums)
             head_sums = lax.psum_scatter(head_sums, "dp", scatter_dimension=0, tiled=True)
         if step == 2:

time: 935 us -> 914 us (0.978)
  matrix products: 138 us -> 105 us
  Pallas kernels: 302 us -> 314 us
  waiting for transfers between devices: 185 us -> 175 us
    dot_general x20 -> x9, matrix products: 38.2 us -> 15.4 us  [dot_nt(): lax.dot_general(a, b, (((1,), (1,)), ((), ())), preferred_element_type=f32)]
    ppermute x12, waiting for transfers between devices: 25.9 us -> 10.2 us  [scatter_step(): lax.ppermute(up, 'ep', self.forward)]
    pallas_call x2 -> x3, Pallas kernels: 60.1 us -> 72.9 us  [the longest x2 60.8 us: attention_backward(): pl.pallas_call(kernel, out_shape=jax.ShapeDtypeStruct((length, 2 * cols),...]
    dot_general x5 -> x2, matrix products: 14.7 us -> 4.7 us  [dot(): return jnp.dot(a, b, preferred_element_type=f32)]
    unnamed x188 -> x194, local copies, waits for them, and re-layouts: 36.9 us -> 42.4 us
    dot_general x6 -> x5, matrix products: 23.8 us -> 23.2 us  [dot_tn(): lax.dot_general(a, b, (((0,), (0,)), ((), ())), preferred_element_type=f32)]
  transfers between devices with their start and end apart: 62 -> 62, of which waited for: 19 -> 20; matrix products, arithmetic and copies ran while one was open for 29% -> 26% of each run, Pallas kernels for 33% -> 35%
where the time goes in v3:
time: 914 us; the launch traced here: 904 us
  Pallas kernels  314 us (34%)
  waiting for transfers between devices  175 us (19%)
  matrix products  105 us (11%)
  other arithmetic  92 us (10%)
  local copies, waits for them, and re-layouts  85.7 us (9%)
  starting transfers between devices  75.1 us (8%)
  blocking collectives  37.2 us (4%)
  between operations  20.7 us (2%)
    pallas_call x5, Pallas kernels, expert_call(): pl.pallas_call(kernel, out_shape=[piece] * (2 * count) + [jax.ShapeDtypeS...  169 us
    ppermute x12, waiting for transfers between devices, scatter_step(): lax.ppermute(down, 'ep', self.backward)  91.9 us
    dot_general x3, matrix products, by_rows(): jnp.einsum('ecd,ecf->edf', left, right, preferred_element_type=f32)  61.2 us
    pallas_call x2, Pallas kernels, attention_backward(): pl.pallas_call(kernel, out_shape=jax.ShapeDtypeStruct((length, 2 * cols),...  60.8 us
    unnamed x194, local copies, waits for them, and re-layouts  42.4 us
    pallas_call x1, Pallas kernels, attention_forward(): pl.pallas_call(kernel, out_shape=(jax.ShapeDtypeStruct((blocks, tall, HEA...  40.5 us
    ppermute x10, waiting for transfers between devices, step(): lax.ppermute(up, 'ep', self.forward)  40.4 us
    all_to_all x1, blocking collectives, shards(): head_rows = lax.all_to_all(jnp.stack(messages), 'ep', 0, 0, tiled=True)  37.2 us
  transfers between devices with their start and end apart: 62, of which 20 were waited for; matrix products, arithmetic and copies ran while one was open for 26% of the time, Pallas kernels for 35%

profile of v3, /device:TPU:12, one launch (start us, length us, event | category | flops | bytes accessed | tf_op | source)
XLA Modules:
  0.0 904.3 jit_solution(11779321421922204279)
XLA Ops:
  14.4 37.2 %all_to_all.25 = bf16[8,40,896]{2,1,0:T(8,128)(2,1)} all-to-all(bf16[8,40,896]{2,1,0:T(8,128)(2,1)S(1)} %bitcast_dynamic-update-slice_fusion), channel_id=1, replica_groups=mesh['dp'=4,'ep'=8] {'ep'}, dimensions={0} | all-to-all | bytes 1146880 | tf_op jit(solution)/shard_map/all_to_all | solution.py:509
  52.6 5.6 all-to-all-start
  58.1 7.5 fusion.20
  71.3 23.3 %collective-permute-done.2.tok_ref = bf16[512,1280]{1,0:T(8,128)(2,1)} collective-permute-done((bf16[512,1280]{1,0:T(8,128)(2,1)}, bf16[512,1280]{1,0:T(8,128)(2,1)}, u32[]{:S(2)}, u32[]{:S(2)}) %collective-permute-start.2) | collective-permute-done | bytes 1310752 | tf_op jit(solution)/shard_map/ppermute | solution.py:72
  107.6 4.2 norm_project_rotate.10
  114.9 4.2 norm_project_rotate.12
  119.1 4.2 norm_project_rotate.13
  135.0 4.3 norm_project_rotate.14
  139.3 4.2 norm_project_rotate.15
  147.6 4.8 collective-permute-done.6.tok_ref
  159.7 40.5 %attention_forward.1 = (bf16[8,640,128]{2,1,0:T(8,128)(2,1)}, f32[8,640,128]{2,1,0:T(8,128)S(1)}, f32[8,8,640]{2,1,0:T(8,128)S(1)}) custom-call(s32[2]{0:T(128)S(1)} %pad_add_fusion.own_ref, bf16[4096,768]{1,0:T(8,128)(2,1)} %copy-done.2), custom_call_target="tpu_custom_call" | custom-call | flops 5368709120 | bytes 8388608 | tf_op jit(solution)/shard_map/attention_forward/pallas_call | solution.py:206
  205.0 7.1 all-to-all-start.2
  214.6 22.8 %all-to-all-done.2 = bf16[8,640,128]{2,1,0:T(8,128)(2,1)S(1)} async-done(((bf16[8,640,128]{2,1,0:T(8,128)(2,1)}), bf16[8,640,128]{2,1,0:T(8,128)(2,1)S(1)}, u32[]{:S(2)}, u32[]{:S(2)}) %all-to-all-start.2) | async-done | bytes 1310752 | tf_op jit(solution)/shard_map/all_to_all | solution.py:568
  240.3 4.5 multiply_reduce_fusion.2
  247.7 15.2 %collective-permute-done.10.refs_2_ = bf16[512,1280]{1,0:T(8,128)(2,1)} collective-permute-done((bf16[512,1280]{1,0:T(8,128)(2,1)}, bf16[512,1280]{1,0:T(8,128)(2,1)}, u32[]{:S(2)}, u32[]{:S(2)}) %collective-permute-start.10) | collective-permute-done | bytes 1310752 | tf_op jit(solution)/shard_map/ppermute | solution.py:72
  270.2 24.2 %experts.5 = (bf16[512,1280]{1,0:T(8,128)(2,1)}, bf16[512,1280]{1,0:T(8,128)(2,1)}, bf16[2,8,320,1280]{3,2,1,0:T(8,128)(2,1)}, bf16[2,8,320,1280]{3,2,1,0:T(8,12...) custom-call(s32[8]{0:T(128)} %copy-done.30, ...), custom_call_target="tpu_custom_call" | custom-call | flops 12163481600 | bytes 25722880 | tf_op jit(solution)/shard_map/experts/pallas_call | solution.py:380
  296.6 40.0 %experts.6 = (bf16[512,1280]{1,0:T(8,128)(2,1)}, bf16[512,1280]{1,0:T(8,128)(2,1)}, bf16[512,1280]{1,0:T(8,128)(2,1)}, bf16[512,1280]{1,0:T(8,128)(2,1)}, bf16[2...) custom-call(s32[8]{0:T(128)} %copy-done.30, ...), custom_call_target="tpu_custom_call", output_to_operand_aliasing={{4}: (14, {}), {5}: (15, {}), {6}: (16, {}), {7}: (17, {}),... | custom-call | flops 24326963200 | bytes 37683200 | tf_op jit(solution)/shard_map/experts/pallas_call | solution.py:380
  338.7 12.1 %shared_expert.1 = (f32[512,1280]{1,0:T(8,128)S(1)}, f32[512,1280]{1,0:T(8,128)S(1)}, bf16[512,896]{1,0:T(8,128)(2,1)S(1)}, bf16[512,1792]{1,0:T(8,128)(2,1)S(1)}) custom-call(bf16[512,1280]{1,0:T(8,128)(2,1)} %multiply_convert_fusion.refs_0_.h_ref, bf16[512,1280]{1,0:T(8,128)(2,1)} %bitcast.2.refs_1_.z_ref, ...), custom_call_target="tpu_custom_call" | custom-call | flops 7046430720 | bytes 14745600 | tf_op jit(solution)/shard_map/shared_expert/pallas_call | solution.py:442
  353.8 4.3 convolution_convert_fusion.5
  358.0 6.0 convolution_convert_fusion.1
  367.2 42.4 %experts.7 = (bf16[512,1280]{1,0:T(8,128)(2,1)}, bf16[512,1280]{1,0:T(8,128)(2,1)}, bf16[512,1280]{1,0:T(8,128)(2,1)}, bf16[512,1280]{1,0:T(8,128)(2,1)}, bf16[2...) custom-call(s32[8]{0:T(128)} %copy-done.30, ...), custom_call_target="tpu_custom_call", output_to_operand_aliasing={{4}: (14, {}), {5}: (15, {}), {6}: (16, {}), {7}: (17, {}),... | custom-call | flops 24326963200 | bytes 37683200 | tf_op jit(solution)/shard_map/experts/pallas_call | solution.py:380
  411.7 39.9 %experts.8 = (bf16[512,1280]{1,0:T(8,128)(2,1)}, bf16[512,1280]{1,0:T(8,128)(2,1)}, bf16[512,1280]{1,0:T(8,128)(2,1)}, bf16[512,1280]{1,0:T(8,128)(2,1)}, bf16[2...) custom-call(s32[8]{0:T(128)} %copy-done.30, ...), custom_call_target="tpu_custom_call", output_to_operand_aliasing={{4}: (14, {}), {5}: (15, {}), {6}: (16, {}), {7}: (17, {}),... | custom-call | flops 24326963200 | bytes 37683200 | tf_op jit(solution)/shard_map/experts/pallas_call | solution.py:380
  451.6 22.7 %experts.9 = (bf16[512,1280]{1,0:T(8,128)(2,1)}, bf16[512,1280]{1,0:T(8,128)(2,1)}, bf16[2,8,320,1280]{3,2,1,0:T(8,128)(2,1)}, bf16[2,8,320,1280]{3,2,1,0:T(8,12...) custom-call(s32[8]{0:T(128)} %copy-done.30, ...), custom_call_target="tpu_custom_call", output_to_operand_aliasing={{2}: (9, {}), {3}: (10, {}), {4}: (11, {}), {5}: (12, {}), ... | custom-call | flops 12163481600 | bytes 25722880 | tf_op jit(solution)/shard_map/experts/pallas_call | solution.py:380
  477.7 19.8 %convolution_convert_fusion.4 = bf16[2,1280,896]{2,1,0:T(8,128)(2,1)} fusion(bf16[2,2560,1280]{2,1,0:T(8,128)(2,1)} %bitcast.134, bf16[2,2560,896]{2,1,0:T(8,128)(2,1)} %bitcast.140), kind=kOutput, calls=%fused_computation.4 | convolution fusion | flops 11746344960 | bytes 26869760 | tf_op jit(solution)/shard_map/ecd,ecf->edf/dot_general | solution.py:652
  502.8 21.5 %convolution_convert_fusion.3 = bf16[2,1280,896]{2,1,0:T(8,128)(2,1)} fusion(bf16[2,2560,1280]{2,1,0:T(8,128)(2,1)} %bitcast.135, bf16[2,2560,896]{2,1,0:T(8,128)(2,1)} %bitcast.141), kind=kOutput, calls=%fused_computation.3 | convolution fusion | flops 11746344960 | bytes 26869760 | tf_op jit(solution)/shard_map/ecd,ecf->edf/dot_general | solution.py:652
  524.2 3.2 add_convert_fusion.11
  532.9 19.9 %convolution_convert_fusion.2 = bf16[2,1280,896]{2,1,0:T(8,128)(2,1)} fusion(bf16[2,2560,1280]{2,1,0:T(8,128)(2,1)} %bitcast.136, bf16[2,2560,896]{2,1,0:T(8,128)(2,1)} %bitcast.139), kind=kOutput, calls=%fused_computation.2 | convolution fusion | flops 11746344960 | bytes 26869760 | tf_op jit(solution)/shard_map/ecd,ecf->edf/dot_general | solution.py:652
  561.9 15.2 %collective-permute-done.29 = bf16[512,1280]{1,0:T(8,128)(2,1)} collective-permute-done((bf16[512,1280]{1,0:T(8,128)(2,1)}, bf16[512,1280]{1,0:T(8,128)(2,1)}, u32[]{:S(2)}, u32[]{:S(2)}) %collective-permute-start.29) | collective-permute-done | bytes 1310752 | tf_op jit(solution)/shard_map/ppermute | solution.py:98
  579.3 4.1 multiply_reduce_fusion
  583.4 4.0 fusion.47
  593.0 5.8 all-to-all-start.3
  603.4 3.5 convolution_convert_fusion
  606.9 21.4 %collective-permute-done.31 = bf16[256,1280]{1,0:T(8,128)(2,1)} collective-permute-done((bf16[256,1280]{1,0:T(8,128)(2,1)}, bf16[256,1280]{1,0:T(8,128)(2,1)}, u32[]{:S(2)}, u32[]{:S(2)}) %collective-permute-start.31) | collective-permute-done | bytes 655392 | tf_op jit(solution)/shard_map/ppermute | solution.py:98
  651.3 22.7 %attention_backward.2.rest_0_ = bf16[4096,768]{1,0:T(8,128)(2,1)S(1)} custom-call(s32[2]{0:T(128)S(1)} %copy-done.32, bf16[4096,768]{1,0:T(8,128)(2,1)} %copy-done.2, bf16[8,640,128]{2,1,0:T(8,128)(2,1)S(1)} %copy-done.19, f32[8,640,128]{2,1,0:T(8,128)S(1)} %copy-done.23, f32[8,8,640]{2,1,0:T(8,128)S(1)} %copy-done.28, f32[4096,128]{1,0:T(8,128)S(1)} %copy-done.4, ...), custom_call_target="tpu_custom_call" | custom-call | flops 2684354560 | bytes 10485760 | tf_op jit(solution)/shard_map/attention_backward/pallas_call | solution.py:295
  694.9 38.1 %attention_backward.3 = bf16[4096,768]{1,0:T(8,128)(2,1)S(1)} custom-call(s32[2]{0:T(128)S(1)} %copy-done.32, bf16[4096,768]{1,0:T(8,128)(2,1)} %copy-done.2, bf16[8,640,128]{2,1,0:T(8,128)(2,1)S(1)} %copy-done.20, f32[8,640,128]{2,1,0:T(8,128)S(1)} %copy-done.24, f32[8,8,640]{2,1,0:T(8,128)S(1)} %copy-done.29, ...), custom_call_target="tpu_custom_call", output_to_operand_aliasing={{}: (7, {})} | custom-call | flops 10737418240 | bytes 10485760 | tf_op jit(solution)/shard_map/attention_backward/pallas_call | solution.py:295
  746.1 6.0 collective-permute-done.37
  753.2 8.4 convolution_convert_fusion.6
  764.5 18.8 %collective-permute-done.41 = bf16[512,1280]{1,0:T(8,128)(2,1)} collective-permute-done((bf16[512,1280]{1,0:T(8,128)(2,1)S(1)}, bf16[512,1280]{1,0:T(8,128)(2,1)}, u32[]{:S(2)}, u32[]{:S(2)}) %collective-permute-start.41) | collective-permute-done | bytes 1310752 | tf_op jit(solution)/shard_map/ppermute | solution.py:98
  783.7 4.4 copy.337
  806.2 10.5 %collective-permute-done.39 = bf16[512,1280]{1,0:T(8,128)(2,1)S(1)} collective-permute-done((bf16[512,1280]{1,0:T(8,128)(2,1)S(1)}, bf16[512,1280]{1,0:T(8,128)(2,1)S(1)}, u32[]{:S(2)}, u32[]{:S(2)}) %collective-permute-start.39) | collective-permute-done | bytes 1310752 | tf_op jit(solution)/shard_map/ppermute | solution.py:98
  825.7 13.9 %collective-permute-done.43 = bf16[512,1280]{1,0:T(8,128)(2,1)} collective-permute-done((bf16[512,1280]{1,0:T(8,128)(2,1)}, bf16[512,1280]{1,0:T(8,128)(2,1)}, u32[]{:S(2)}, u32[]{:S(2)}) %collective-permute-start.43) | collective-permute-done | bytes 1310752 | tf_op jit(solution)/shard_map/ppermute | solution.py:98
  841.0 5.4 fusion.8
  848.8 5.4 all-to-all-start.4
  854.2 3.2 add_convert_fusion
  863.7 3.8 all-to-all-done.4
  878.6 4.8 collective-permute-done.45
  883.3 3.9 collective-permute-done.44
  890.2 4.3 fusion.6
  (440 shorter events, 230.5 us)
Async XLA Ops:
  7.2 90.9 %all-gather.5.cloned.1.call-start = ((), (), s32[]{:S(2)}) async-start(), calls=%async_computation.13 | async-start | bytes 2867200 | tf_op jit(solution)/shard_map/all_gather | solution.py:544
  7.2 44.3 %collective-permute-start.1 = (bf16[512,1280]{1,0:T(8,128)(2,1)}, bf16[512,1280]{1,0:T(8,128)(2,1)S(1)}, u32[]{:S(2)}, u32[]{:S(2)}) collective-permute-start(bf16[512,1280]{1,0:T(8,128)(2,1)} %bitcast.127), channel_id=1, source_target_pairs={{0,1},{2,0},{4,2},{6,4},{7,6},{5,7},{3,5},{1,3},{8,9},{10,8},{12,1... | collective-permute-start | bytes 3932168 | tf_op jit(solution)/shard_map/ppermute | solution.py:72
  8.9 42.7 %collective-permute-start = (bf16[512,1280]{1,0:T(8,128)(2,1)}, bf16[512,1280]{1,0:T(8,128)(2,1)}, u32[]{:S(2)}, u32[]{:S(2)}) collective-permute-start(bf16[512,1280]{1,0:T(8,128)(2,1)} %bitcast.128), channel_id=1, source_target_pairs={{0,2},{2,4},{4,6},{6,7},{7,5},{5,3},{3,1},{1,0},{8,10},{10,12},{12... | collective-permute-start | bytes 3932168 | tf_op jit(solution)/shard_map/ppermute | solution.py:72
  58.1 144.3 %all-gather.7.cloned.1.call-start = ((), (), s32[]{:S(2)}) async-start(), calls=%async_computation.14 | async-start | bytes 2856960 | tf_op jit(solution)/shard_map/all_gather | solution.py:555
  65.6 29.0 %collective-permute-start.2 = (bf16[512,1280]{1,0:T(8,128)(2,1)}, bf16[512,1280]{1,0:T(8,128)(2,1)}, u32[]{:S(2)}, u32[]{:S(2)}) collective-permute-start(bf16[512,1280]{1,0:T(8,128)(2,1)} %collective-permute-done.tok_ref), channel_id=1, source_target_pairs={{0,2},{2,4},{4,6},{6,7},{7,5},{5,3},{3,1},{1,0},{8,10},{10,12},{12... | collective-permute-start | bytes 3932168 | tf_op jit(solution)/shard_map/ppermute | solution.py:72
  66.2 28.4 %collective-permute-start.3 = (bf16[512,1280]{1,0:T(8,128)(2,1)S(1)}, bf16[512,1280]{1,0:T(8,128)(2,1)}, u32[]{:S(2)}, u32[]{:S(2)}) collective-permute-start(bf16[512,1280]{1,0:T(8,128)(2,1)S(1)} %collective-permute-done.1.tok_ref), channel_id=1, source_target_pairs={{0,1},{2,0},{4,2},{6,4},{7,6},{5,7},{3,5},{1,3},{8,9},{10,8},{12,1... | collective-permute-start | bytes 3932168 | tf_op jit(solution)/shard_map/ppermute | solution.py:72
  94.6 31.3 %collective-permute-start.4 = (bf16[512,1280]{1,0:T(8,128)(2,1)}, bf16[512,1280]{1,0:T(8,128)(2,1)}, u32[]{:S(2)}, u32[]{:S(2)}) collective-permute-start(bf16[512,1280]{1,0:T(8,128)(2,1)} %collective-permute-done.2.tok_ref), channel_id=1, source_target_pairs={{0,2},{2,4},{4,6},{6,7},{7,5},{5,3},{3,1},{1,0},{8,10},{10,12},{12... | collective-permute-start | bytes 3932168 | tf_op jit(solution)/shard_map/ppermute | solution.py:72
  95.2 30.8 %collective-permute-start.5 = (bf16[512,1280]{1,0:T(8,128)(2,1)}, bf16[512,1280]{1,0:T(8,128)(2,1)}, u32[]{:S(2)}, u32[]{:S(2)}) collective-permute-start(bf16[512,1280]{1,0:T(8,128)(2,1)} %collective-permute-done.3.tok_ref), channel_id=1, source_target_pairs={{0,1},{2,0},{4,2},{6,4},{7,6},{5,7},{3,5},{1,3},{8,9},{10,8},{12,1... | collective-permute-start | bytes 3932168 | tf_op jit(solution)/shard_map/ppermute | solution.py:72
  126.0 114.3 %all-gather.9.cloned.1.call-start = ((), (), s32[]{:S(2)}) async-start(), calls=%async_computation.15 | async-start | bytes 4096000 | tf_op jit(solution)/shard_map/all_gather | solution.py:566
  157.2 45.2 %collective-permute-start.9 = (bf16[512,1280]{1,0:T(8,128)(2,1)}, bf16[512,1280]{1,0:T(8,128)(2,1)S(1)}, u32[]{:S(2)}, u32[]{:S(2)}) collective-permute-start(bf16[512,1280]{1,0:T(8,128)(2,1)} %bitcast.2.refs_1_.z_ref), channel_id=1, source_target_pairs={{0,1},{2,0},{4,2},{6,4},{7,6},{5,7},{3,5},{1,3},{8,9},{10,8},{12,1... | collective-permute-start | bytes 3932168 | tf_op jit(solution)/shard_map/ppermute | solution.py:72
  159.7 42.7 %collective-permute-start.8 = (bf16[512,1280]{1,0:T(8,128)(2,1)}, bf16[512,1280]{1,0:T(8,128)(2,1)}, u32[]{:S(2)}, u32[]{:S(2)}) collective-permute-start(bf16[512,1280]{1,0:T(8,128)(2,1)} %bitcast.2.refs_1_.z_ref), channel_id=1, source_target_pairs={{0,2},{2,4},{4,6},{6,7},{7,5},{5,3},{3,1},{1,0},{8,10},{10,12},{12... | collective-permute-start | bytes 3932168 | tf_op jit(solution)/shard_map/ppermute | solution.py:72
  205.0 32.4 %all-to-all-start.2 = ((bf16[8,640,128]{2,1,0:T(8,128)(2,1)}), bf16[8,640,128]{2,1,0:T(8,128)(2,1)S(1)}, u32[]{:S(2)}, u32[]{:S(2)}) async-start(bf16[8,640,128]{2,1,0:T(8,128)(2,1)} %get-tuple-element.226), calls=%async_computation.2 | async-start | bytes 2621440 | tf_op jit(solution)/shard_map/all_to_all | solution.py:568
  212.1 126.5 %all-gather.11.cloned.1.call-start = ((), (), s32[]{:S(2)}) async-start(), calls=%async_computation.16 | async-start | bytes 8601600 | tf_op jit(solution)/shard_map/all_gather | solution.py:582
  212.1 50.7 %collective-permute-start.10 = (bf16[512,1280]{1,0:T(8,128)(2,1)}, bf16[512,1280]{1,0:T(8,128)(2,1)}, u32[]{:S(2)}, u32[]{:S(2)}) collective-permute-start(bf16[512,1280]{1,0:T(8,128)(2,1)} %collective-permute-done.8.refs_2_), channel_id=1, source_target_pairs={{0,2},{2,4},{4,6},{6,7},{7,5},{5,3},{3,1},{1,0},{8,10},{10,12},{12... | collective-permute-start | bytes 3932168 | tf_op jit(solution)/shard_map/ppermute | solution.py:72
  212.7 50.1 %collective-permute-start.11 = (bf16[512,1280]{1,0:T(8,128)(2,1)}, bf16[512,1280]{1,0:T(8,128)(2,1)}, u32[]{:S(2)}, u32[]{:S(2)}) collective-permute-start(bf16[512,1280]{1,0:T(8,128)(2,1)} %copy-done.85), channel_id=1, source_target_pairs={{0,1},{2,0},{4,2},{6,4},{7,6},{5,7},{3,5},{1,3},{8,9},{10,8},{12,1... | collective-permute-start | bytes 3932168 | tf_op jit(solution)/shard_map/ppermute | solution.py:72
  264.2 236.3 %reduce-scatter.15.cloned.1.call-start = ((), (), s32[]{:S(2)}) async-start(), calls=%async_computation.18 | async-start | bytes 2867200 | tf_op jit(solution)/shard_map/reduce_scatter | solution.py:639
  264.2 30.3 %collective-permute-start.13 = (bf16[512,1280]{1,0:T(8,128)(2,1)}, bf16[512,1280]{1,0:T(8,128)(2,1)}, u32[]{:S(2)}, u32[]{:S(2)}) collective-permute-start(bf16[512,1280]{1,0:T(8,128)(2,1)} %multiply_convert_fusion.refs_0_.h_ref), channel_id=1, source_target_pairs={{0,1},{2,0},{4,2},{6,4},{7,6},{5,7},{3,5},{1,3},{8,9},{10,8},{12,1... | collective-permute-start | bytes 3932168 | tf_op jit(solution)/shard_map/ppermute | solution.py:72
  264.8 29.6 %collective-permute-start.12 = (bf16[512,1280]{1,0:T(8,128)(2,1)}, bf16[512,1280]{1,0:T(8,128)(2,1)}, u32[]{:S(2)}, u32[]{:S(2)}) collective-permute-start(bf16[512,1280]{1,0:T(8,128)(2,1)} %multiply_convert_fusion.refs_0_.h_ref), channel_id=1, source_target_pairs={{0,2},{2,4},{4,6},{6,7},{7,5},{5,3},{3,1},{1,0},{8,10},{10,12},{12... | collective-permute-start | bytes 3932168 | tf_op jit(solution)/shard_map/ppermute | solution.py:72
  294.5 42.1 %collective-permute-start.14 = (bf16[512,1280]{1,0:T(8,128)(2,1)}, bf16[512,1280]{1,0:T(8,128)(2,1)}, u32[]{:S(2)}, u32[]{:S(2)}) collective-permute-start(bf16[512,1280]{1,0:T(8,128)(2,1)} %collective-permute-done.12.refs_0_), channel_id=1, source_target_pairs={{0,2},{2,4},{4,6},{6,7},{7,5},{5,3},{3,1},{1,0},{8,10},{10,12},{12... | collective-permute-start | bytes 3932168 | tf_op jit(solution)/shard_map/ppermute | solution.py:72
  294.6 41.9 %collective-permute-start.15 = (bf16[512,1280]{1,0:T(8,128)(2,1)}, bf16[512,1280]{1,0:T(8,128)(2,1)}, u32[]{:S(2)}, u32[]{:S(2)}) collective-permute-start(bf16[512,1280]{1,0:T(8,128)(2,1)} %collective-permute-done.13.refs_1_), channel_id=1, source_target_pairs={{0,1},{2,0},{4,2},{6,4},{7,6},{5,7},{3,5},{1,3},{8,9},{10,8},{12,1... | collective-permute-start | bytes 3932168 | tf_op jit(solution)/shard_map/ppermute | solution.py:72
  336.6 27.5 %collective-permute-start.16 = (bf16[512,1280]{1,0:T(8,128)(2,1)}, bf16[512,1280]{1,0:T(8,128)(2,1)}, u32[]{:S(2)}, u32[]{:S(2)}) collective-permute-start(bf16[512,1280]{1,0:T(8,128)(2,1)} %collective-permute-done.10.refs_2_), channel_id=1, source_target_pairs={{0,2},{2,4},{4,6},{6,7},{7,5},{5,3},{3,1},{1,0},{8,10},{10,12},{12... | collective-permute-start | bytes 3932168 | tf_op jit(solution)/shard_map/ppermute | solution.py:72
  336.7 27.3 %collective-permute-start.17 = (bf16[512,1280]{1,0:T(8,128)(2,1)}, bf16[512,1280]{1,0:T(8,128)(2,1)S(1)}, u32[]{:S(2)}, u32[]{:S(2)}) collective-permute-start(bf16[512,1280]{1,0:T(8,128)(2,1)} %collective-permute-done.11.refs_3_), channel_id=1, source_target_pairs={{0,1},{2,0},{4,2},{6,4},{7,6},{5,7},{3,5},{1,3},{8,9},{10,8},{12,1... | collective-permute-start | bytes 3932168 | tf_op jit(solution)/shard_map/ppermute | solution.py:72
  364.1 136.4 %reduce-scatter.13.cloned.1.call-start = ((), (), s32[]{:S(2)}) async-start(), calls=%async_computation.17 | async-start | bytes 5734400 | tf_op jit(solution)/shard_map/reduce_scatter | solution.py:639
  365.1 196.7 %reduce-scatter.17.cloned.1.call-start = ((), (), s32[]{:S(2)}) async-start(), calls=%async_computation.19 | async-start | bytes 5734400 | tf_op jit(solution)/shard_map/reduce_scatter | solution.py:662
  365.1 44.5 %collective-permute-start.18 = (bf16[512,1280]{1,0:T(8,128)(2,1)}, bf16[512,1280]{1,0:T(8,128)(2,1)}, u32[]{:S(2)}, u32[]{:S(2)}) collective-permute-start(bf16[512,1280]{1,0:T(8,128)(2,1)} %collective-permute-done.14.refs_0_), channel_id=1, source_target_pairs={{0,2},{2,4},{4,6},{6,7},{7,5},{5,3},{3,1},{1,0},{8,10},{10,12},{12... | collective-permute-start | bytes 3932168 | tf_op jit(solution)/shard_map/ppermute | solution.py:72
  365.2 44.4 %collective-permute-start.19 = (bf16[512,1280]{1,0:T(8,128)(2,1)}, bf16[512,1280]{1,0:T(8,128)(2,1)}, u32[]{:S(2)}, u32[]{:S(2)}) collective-permute-start(bf16[512,1280]{1,0:T(8,128)(2,1)} %collective-permute-done.15.refs_1_), channel_id=1, source_target_pairs={{0,1},{2,0},{4,2},{6,4},{7,6},{5,7},{3,5},{1,3},{8,9},{10,8},{12,1... | collective-permute-start | bytes 3932168 | tf_op jit(solution)/shard_map/ppermute | solution.py:72
  409.6 41.9 %collective-permute-start.20 = (bf16[512,1280]{1,0:T(8,128)(2,1)}, bf16[512,1280]{1,0:T(8,128)(2,1)}, u32[]{:S(2)}, u32[]{:S(2)}) collective-permute-start(bf16[512,1280]{1,0:T(8,128)(2,1)} %collective-permute-done.18.refs_0_), channel_id=1, source_target_pairs={{0,2},{2,4},{4,6},{6,7},{7,5},{5,3},{3,1},{1,0},{8,10},{10,12},{12... | collective-permute-start | bytes 3932168 | tf_op jit(solution)/shard_map/ppermute | solution.py:626
  409.8 41.8 %collective-permute-start.21 = (bf16[512,1280]{1,0:T(8,128)(2,1)}, bf16[512,1280]{1,0:T(8,128)(2,1)}, u32[]{:S(2)}, u32[]{:S(2)}) collective-permute-start(bf16[512,1280]{1,0:T(8,128)(2,1)} %copy-done.86), channel_id=1, source_target_pairs={{0,1},{2,0},{4,2},{6,4},{7,6},{5,7},{3,5},{1,3},{8,9},{10,8},{12,1... | collective-permute-start | bytes 3932168 | tf_op jit(solution)/shard_map/ppermute | solution.py:627
  497.5 132.7 %reduce-scatter.19.cloned.1.call-start = ((), (), s32[]{:S(2)}) async-start(), calls=%async_computation.20 | async-start | bytes 5734400 | tf_op jit(solution)/shard_map/reduce_scatter | solution.py:662
  500.3 23.9 %collective-permute-start.24 = (bf16[512,1280]{1,0:T(8,128)(2,1)S(1)}, bf16[512,1280]{1,0:T(8,128)(2,1)}, u32[]{:S(2)}, u32[]{:S(2)}) collective-permute-start(bf16[512,1280]{1,0:T(8,128)(2,1)S(1)} %pad_maximum_fusion.4), channel_id=1, source_target_pairs={{0,2},{2,4},{4,6},{6,7},{7,5},{5,3},{3,1},{1,0},{8,10},{10,12},{12... | collective-permute-start | bytes 3932168 | tf_op jit(solution)/shard_map/ppermute | solution.py:98
  527.5 26.7 %collective-permute-start.27 = (bf16[512,1280]{1,0:T(8,128)(2,1)}, bf16[512,1280]{1,0:T(8,128)(2,1)S(1)}, u32[]{:S(2)}, u32[]{:S(2)}) collective-permute-start(bf16[512,1280]{1,0:T(8,128)(2,1)} %add_convert_fusion.11), channel_id=1, source_target_pairs={{0,1},{2,0},{4,2},{6,4},{7,6},{5,7},{3,5},{1,3},{8,9},{10,8},{12,1... | collective-permute-start | bytes 3932168 | tf_op jit(solution)/shard_map/ppermute | solution.py:98
  593.0 37.2 %all-to-all-start.3 = ((bf16[8,640,128]{2,1,0:T(8,128)(2,1)}), bf16[8,640,128]{2,1,0:T(8,128)(2,1)S(1)}, u32[]{:S(2)}, u32[]{:S(2)}) async-start(bf16[8,640,128]{2,1,0:T(8,128)(2,1)} %pad_maximum_fusion.6), calls=%async_computation.6 | async-start | bytes 2621440 | tf_op jit(solution)/shard_map/all_to_all | solution.py:683
  598.8 77.8 %reduce-scatter.21.cloned.1.call-start = ((), (), s32[]{:S(2)}) async-start(), calls=%async_computation.21 | async-start | bytes 4096000 | tf_op jit(solution)/shard_map/reduce_scatter | solution.py:690
  601.4 27.0 %collective-permute-start.31 = (bf16[256,1280]{1,0:T(8,128)(2,1)}, bf16[256,1280]{1,0:T(8,128)(2,1)}, u32[]{:S(2)}, u32[]{:S(2)}) collective-permute-start(bf16[256,1280]{1,0:T(8,128)(2,1)} %get-tuple-element.395), channel_id=1, source_target_pairs={{0,1},{2,0},{4,2},{6,4},{7,6},{5,7},{3,5},{1,3},{8,9},{10,8},{12,1... | collective-permute-start | bytes 1966088 | tf_op jit(solution)/shard_map/ppermute | solution.py:98
  602.8 27.4 %collective-permute-start.30 = (bf16[256,1280]{1,0:T(8,128)(2,1)S(1)}, bf16[256,1280]{1,0:T(8,128)(2,1)}, u32[]{:S(2)}, u32[]{:S(2)}) collective-permute-start(bf16[256,1280]{1,0:T(8,128)(2,1)S(1)} %get-tuple-element.396), channel_id=1, source_target_pairs={{0,2},{2,4},{4,6},{6,7},{7,5},{5,3},{3,1},{1,0},{8,10},{10,12},{12... | collective-permute-start | bytes 1966088 | tf_op jit(solution)/shard_map/ppermute | solution.py:98
  630.3 191.4 %reduce-scatter.27.cloned.1.call-start = ((), (), s32[]{:S(2)}) async-start(), calls=%async_computation.24 | async-start | bytes 2856960
  634.8 41.8 %collective-permute-start.33 = (bf16[512,1280]{1,0:T(8,128)(2,1)}, bf16[512,1280]{1,0:T(8,128)(2,1)}, u32[]{:S(2)}, u32[]{:S(2)}) collective-permute-start(bf16[512,1280]{1,0:T(8,128)(2,1)} %pad_maximum_fusion.8), channel_id=1, source_target_pairs={{0,1},{2,0},{4,2},{6,4},{7,6},{5,7},{3,5},{1,3},{8,9},{10,8},{12,1... | collective-permute-start | bytes 3932168 | tf_op jit(solution)/shard_map/ppermute | solution.py:98
  637.8 38.8 %collective-permute-start.32 = (bf16[512,1280]{1,0:T(8,128)(2,1)}, bf16[512,1280]{1,0:T(8,128)(2,1)}, u32[]{:S(2)}, u32[]{:S(2)}) collective-permute-start(bf16[512,1280]{1,0:T(8,128)(2,1)} %pad_maximum_fusion.7), channel_id=1, source_target_pairs={{0,2},{2,4},{4,6},{6,7},{7,5},{5,3},{3,1},{1,0},{8,10},{10,12},{12... | collective-permute-start | bytes 3932168 | tf_op jit(solution)/shard_map/ppermute | solution.py:98
  679.9 53.1 %collective-permute-start.34 = (bf16[512,1280]{1,0:T(8,128)(2,1)}, bf16[512,1280]{1,0:T(8,128)(2,1)}, u32[]{:S(2)}, u32[]{:S(2)}) collective-permute-start(bf16[512,1280]{1,0:T(8,128)(2,1)} %add_convert_fusion.8), channel_id=1, source_target_pairs={{0,2},{2,4},{4,6},{6,7},{7,5},{5,3},{3,1},{1,0},{8,10},{10,12},{12... | collective-permute-start | bytes 3932168 | tf_op jit(solution)/shard_map/ppermute | solution.py:98
  682.8 50.2 %collective-permute-start.35 = (bf16[512,1280]{1,0:T(8,128)(2,1)}, bf16[512,1280]{1,0:T(8,128)(2,1)}, u32[]{:S(2)}, u32[]{:S(2)}) collective-permute-start(bf16[512,1280]{1,0:T(8,128)(2,1)} %add_convert_fusion.7), channel_id=1, source_target_pairs={{0,1},{2,0},{4,2},{6,4},{7,6},{5,7},{3,5},{1,3},{8,9},{10,8},{12,1... | collective-permute-start | bytes 3932168 | tf_op jit(solution)/shard_map/ppermute | solution.py:98
  686.3 137.2 %reduce-scatter.25.cloned.1.call-start = ((), (), s32[]{:S(2)}) async-start(), calls=%async_computation.23 | async-start | bytes 2867200
  738.3 44.9 %collective-permute-start.41 = (bf16[512,1280]{1,0:T(8,128)(2,1)S(1)}, bf16[512,1280]{1,0:T(8,128)(2,1)}, u32[]{:S(2)}, u32[]{:S(2)}) collective-permute-start(bf16[512,1280]{1,0:T(8,128)(2,1)S(1)} %add_convert_fusion.5), channel_id=1, source_target_pairs={{0,1},{2,0},{4,2},{6,4},{7,6},{5,7},{3,5},{1,3},{8,9},{10,8},{12,1... | collective-permute-start | bytes 3932168 | tf_op jit(solution)/shard_map/ppermute | solution.py:98
  741.5 42.2 %collective-permute-start.40 = (bf16[512,1280]{1,0:T(8,128)(2,1)}, bf16[512,1280]{1,0:T(8,128)(2,1)}, u32[]{:S(2)}, u32[]{:S(2)}) collective-permute-start(bf16[512,1280]{1,0:T(8,128)(2,1)} %add_convert_fusion.6), channel_id=1, source_target_pairs={{0,2},{2,4},{4,6},{6,7},{7,5},{5,3},{3,1},{1,0},{8,10},{10,12},{12... | collective-permute-start | bytes 3932168 | tf_op jit(solution)/shard_map/ppermute | solution.py:98
  788.1 106.3 %reduce-scatter.23.cloned.1.call-start = ((), (), s32[]{:S(2)}) async-start(), calls=%async_computation.22 | async-start | bytes 5734400 | tf_op jit(solution)/shard_map/reduce_scatter | solution.py:726
  790.5 26.3 %collective-permute-start.39 = (bf16[512,1280]{1,0:T(8,128)(2,1)S(1)}, bf16[512,1280]{1,0:T(8,128)(2,1)S(1)}, u32[]{:S(2)}, u32[]{:S(2)}) collective-permute-start(bf16[512,1280]{1,0:T(8,128)(2,1)S(1)} %pad_maximum_fusion.10), channel_id=1, source_target_pairs={{0,1},{2,0},{4,2},{6,4},{7,6},{5,7},{3,5},{1,3},{8,9},{10,8},{12,1... | collective-permute-start | bytes 3932168 | tf_op jit(solution)/shard_map/ppermute | solution.py:98
  792.1 24.7 %collective-permute-start.38 = (bf16[512,1280]{1,0:T(8,128)(2,1)S(1)}, bf16[512,1280]{1,0:T(8,128)(2,1)S(1)}, u32[]{:S(2)}, u32[]{:S(2)}) collective-permute-start(bf16[512,1280]{1,0:T(8,128)(2,1)S(1)} %pad_maximum_fusion.9), channel_id=1, source_target_pairs={{0,2},{2,4},{4,6},{6,7},{7,5},{5,3},{3,1},{1,0},{8,10},{10,12},{12... | collective-permute-start | bytes 3932168 | tf_op jit(solution)/shard_map/ppermute | solution.py:98
  858.1 25.2 %collective-permute-start.45 = (bf16[512,1280]{1,0:T(8,128)(2,1)}, bf16[512,1280]{1,0:T(8,128)(2,1)}, u32[]{:S(2)}, u32[]{:S(2)}) collective-permute-start(bf16[512,1280]{1,0:T(8,128)(2,1)} %add_convert_fusion), channel_id=1, source_target_pairs={{0,1},{2,0},{4,2},{6,4},{7,6},{5,7},{3,5},{1,3},{8,9},{10,8},{12,1... | collective-permute-start | bytes 3932168 | tf_op jit(solution)/shard_map/ppermute | solution.py:98
  862.4 24.9 %collective-permute-start.44 = (bf16[512,1280]{1,0:T(8,128)(2,1)}, bf16[512,1280]{1,0:T(8,128)(2,1)}, u32[]{:S(2)}, u32[]{:S(2)}) collective-permute-start(bf16[512,1280]{1,0:T(8,128)(2,1)} %add_convert_fusion.1), channel_id=1, source_target_pairs={{0,2},{2,4},{4,6},{6,7},{7,5},{5,3},{3,1},{1,0},{8,10},{10,12},{12... | collective-permute-start | bytes 3932168 | tf_op jit(solution)/shard_map/ppermute | solution.py:98
  (108 other events, 1281.6 us)
Sparse Core Ops, SparseCore 0:
  51.7 23.5 all-gather.4
  126.1 71.0 all-gather.6
  205.1 31.3 all-gather.8
  264.3 48.8 all-gather.10
  364.2 31.9 reduce-scatter.14
  398.8 46.9 reduce-scatter.12
  497.7 46.2 reduce-scatter.16
  546.7 46.9 reduce-scatter.18
  630.4 37.7 reduce-scatter.20
  686.4 98.6 reduce-scatter.26
  788.3 33.6 reduce-scatter.24
  841.1 47.3 reduce-scatter.22

commit v4 on v3

--- a/solution.py
+++ b/solution.py
@@ -720,13 +720,13 @@
         if step == 2:
             early = [item.astype(f32) for item in expert_grads[:2]]
             came, came_y, part_h, expert_grads[:2], inverse_one = tie(came, came_y, part_h, early, inverse_one)
+            output = (middle + shared_branch + ring.scatter_end(part_y, came_y)).astype(bf16)
         if step == 3:
-            came, head_sums, dense, last = tie(came, head_sums, dense, expert_grads[2])
+            came, head_sums, dense, last, output = tie(came, head_sums, dense, expert_grads[2], output)
             head_sums = lax.all_to_all(head_sums.reshape(ep, shard, 7 * HEAD), "ep", 0, 0, tiled=True)
             expert_grads[2] = lax.psum_scatter(last, "dp", scatter_dimension=1, tiled=True)
     head_sums = head_sums.astype(f32)
     grad_hidden_one = ring.scatter_end(part_h, came)
-    output = (middle + shared_branch + ring.scatter_end(part_y, came_y)).astype(bf16)
     main_sums = head_sums[:, :, : 3 * HEAD].reshape(MAIN, copies, shard, 3, HEAD).sum(1)
     gain_sums = head_sums[:, :, 6 * HEAD] + head_sums[:, :, 6 * HEAD + 1]
     side_sums = head_sums[:, :, 3 * HEAD : 6 * HEAD].reshape(HEADS - MAIN, sharers * copies, shard, 3, HEAD).sum(1)

time: 914 us -> 908 us (level)
    ppermute x12, waiting for transfers between devices: 91.9 us -> 51.8 us  [scatter_step(): lax.ppermute(down, 'ep', self.backward)]
    ppermute x12, waiting for transfers between devices: 10.2 us -> 41 us  [scatter_step(): lax.ppermute(up, 'ep', self.forward)]
    unnamed x194 -> x192, local copies, waits for them, and re-layouts: 42.4 us -> 42.9 us
  transfers between devices with their start and end apart: 62 -> 62, of which waited for: 20 -> 19; matrix products, arithmetic and copies ran while one was open for 26% -> 26% of each run, Pallas kernels for 35% -> 35%
where the time goes in v4:
time: 908 us; the launch traced here: 898 us
  Pallas kernels  314 us (35%)
  waiting for transfers between devices  167 us (18%)
  matrix products  105 us (12%)
  other arithmetic  92.4 us (10%)
  local copies, waits for them, and re-layouts  85.5 us (9%)
  starting transfers between devices  76.1 us (8%)
  blocking collectives  37.1 us (4%)
  between operations  20.7 us (2%)
    pallas_call x5, Pallas kernels, expert_call(): pl.pallas_call(kernel, out_shape=[piece] * (2 * count) + [jax.ShapeDtypeS...  169 us
    dot_general x3, matrix products, by_rows(): jnp.einsum('ecd,ecf->edf', left, right, preferred_element_type=f32)  61.1 us
    pallas_call x2, Pallas kernels, attention_backward(): pl.pallas_call(kernel, out_shape=jax.ShapeDtypeStruct((length, 2 * cols),...  60.8 us
    ppermute x12, waiting for transfers between devices, scatter_step(): lax.ppermute(down, 'ep', self.backward)  51.8 us
    unnamed x192, local copies, waits for them, and re-layouts  42.9 us
    ppermute x12, waiting for transfers between devices, scatter_step(): lax.ppermute(up, 'ep', self.forward)  41 us
    pallas_call x1, Pallas kernels, attention_forward(): pl.pallas_call(kernel, out_shape=(jax.ShapeDtypeStruct((blocks, tall, HEA...  40.5 us
    ppermute x10, waiting for transfers between devices, step(): lax.ppermute(up, 'ep', self.forward)  40 us
  transfers between devices with their start and end apart: 62, of which 19 were waited for; matrix products, arithmetic and copies ran while one was open for 26% of the time, Pallas kernels for 35%

profile of v4, /device:TPU:12, one launch (start us, length us, event | category | flops | bytes accessed | tf_op | source)
XLA Modules:
  0.0 898.2 jit_solution(5403701292642309940)
XLA Ops:
  14.4 37.1 %all_to_all.25 = bf16[8,40,896]{2,1,0:T(8,128)(2,1)} all-to-all(bf16[8,40,896]{2,1,0:T(8,128)(2,1)S(1)} %bitcast_dynamic-update-slice_fusion), channel_id=1, replica_groups=mesh['dp'=4,'ep'=8] {'ep'}, dimensions={0} | all-to-all | bytes 1146880 | tf_op jit(solution)/shard_map/all_to_all | solution.py:509
  52.4 5.2 all-to-all-start
  57.7 7.5 fusion.19
  70.8 23.3 %collective-permute-done.2.tok_ref = bf16[512,1280]{1,0:T(8,128)(2,1)} collective-permute-done((bf16[512,1280]{1,0:T(8,128)(2,1)}, bf16[512,1280]{1,0:T(8,128)(2,1)}, u32[]{:S(2)}, u32[]{:S(2)}) %collective-permute-start.2) | collective-permute-done | bytes 1310752 | tf_op jit(solution)/shard_map/ppermute | solution.py:72
  107.1 4.2 norm_project_rotate.10
  114.4 4.2 norm_project_rotate.12
  118.6 4.2 norm_project_rotate.13
  134.5 4.2 norm_project_rotate.14
  138.7 4.3 norm_project_rotate.15
  146.7 4.6 collective-permute-done.6.tok_ref
  159.0 40.5 %attention_forward.1 = (bf16[8,640,128]{2,1,0:T(8,128)(2,1)}, f32[8,640,128]{2,1,0:T(8,128)S(1)}, f32[8,8,640]{2,1,0:T(8,128)S(1)}) custom-call(s32[2]{0:T(128)S(1)} %pad_add_fusion.own_ref, bf16[4096,768]{1,0:T(8,128)(2,1)} %copy-done.2), custom_call_target="tpu_custom_call" | custom-call | flops 5368709120 | bytes 8388608 | tf_op jit(solution)/shard_map/attention_forward/pallas_call | solution.py:206
  204.3 7.0 all-to-all-start.2
  213.7 22.8 %all-to-all-done.2 = bf16[8,640,128]{2,1,0:T(8,128)(2,1)S(1)} async-done(((bf16[8,640,128]{2,1,0:T(8,128)(2,1)}), bf16[8,640,128]{2,1,0:T(8,128)(2,1)S(1)}, u32[]{:S(2)}, u32[]{:S(2)}) %all-to-all-start.2) | async-done | bytes 1310752 | tf_op jit(solution)/shard_map/all_to_all | solution.py:568
  239.5 4.5 multiply_reduce_fusion.2
  246.8 15.1 %collective-permute-done.10.refs_2_ = bf16[512,1280]{1,0:T(8,128)(2,1)} collective-permute-done((bf16[512,1280]{1,0:T(8,128)(2,1)}, bf16[512,1280]{1,0:T(8,128)(2,1)}, u32[]{:S(2)}, u32[]{:S(2)}) %collective-permute-start.10) | collective-permute-done | bytes 1310752 | tf_op jit(solution)/shard_map/ppermute | solution.py:72
  269.5 24.3 %experts.5 = (bf16[512,1280]{1,0:T(8,128)(2,1)}, bf16[512,1280]{1,0:T(8,128)(2,1)}, bf16[2,8,320,1280]{3,2,1,0:T(8,128)(2,1)}, bf16[2,8,320,1280]{3,2,1,0:T(8,12...) custom-call(s32[8]{0:T(128)} %copy-done.31, ...), custom_call_target="tpu_custom_call" | custom-call | flops 12163481600 | bytes 25722880 | tf_op jit(solution)/shard_map/experts/pallas_call | solution.py:380
  295.8 39.9 %experts.6 = (bf16[512,1280]{1,0:T(8,128)(2,1)}, bf16[512,1280]{1,0:T(8,128)(2,1)}, bf16[512,1280]{1,0:T(8,128)(2,1)}, bf16[512,1280]{1,0:T(8,128)(2,1)}, bf16[2...) custom-call(s32[8]{0:T(128)} %copy-done.31, ...), custom_call_target="tpu_custom_call", output_to_operand_aliasing={{4}: (14, {}), {5}: (15, {}), {6}: (16, {}), {7}: (17, {}),... | custom-call | flops 24326963200 | bytes 37683200 | tf_op jit(solution)/shard_map/experts/pallas_call | solution.py:380
  337.9 12.1 %shared_expert.1 = (f32[512,1280]{1,0:T(8,128)S(1)}, f32[512,1280]{1,0:T(8,128)S(1)}, bf16[512,896]{1,0:T(8,128)(2,1)S(1)}, bf16[512,1792]{1,0:T(8,128)(2,1)S(1)}) custom-call(bf16[512,1280]{1,0:T(8,128)(2,1)} %multiply_convert_fusion.refs_0_.h_ref, bf16[512,1280]{1,0:T(8,128)(2,1)} %bitcast.1.refs_1_.z_ref, ...), custom_call_target="tpu_custom_call" | custom-call | flops 7046430720 | bytes 14745600 | tf_op jit(solution)/shard_map/shared_expert/pallas_call | solution.py:442
  353.0 4.3 convolution_convert_fusion.5
  357.3 6.0 convolution_convert_fusion.1
  366.4 42.3 %experts.7 = (bf16[512,1280]{1,0:T(8,128)(2,1)}, bf16[512,1280]{1,0:T(8,128)(2,1)}, bf16[512,1280]{1,0:T(8,128)(2,1)}, bf16[512,1280]{1,0:T(8,128)(2,1)}, bf16[2...) custom-call(s32[8]{0:T(128)} %copy-done.31, ...), custom_call_target="tpu_custom_call", output_to_operand_aliasing={{4}: (14, {}), {5}: (15, {}), {6}: (16, {}), {7}: (17, {}),... | custom-call | flops 24326963200 | bytes 37683200 | tf_op jit(solution)/shard_map/experts/pallas_call | solution.py:380
  410.8 39.8 %experts.8 = (bf16[512,1280]{1,0:T(8,128)(2,1)}, bf16[512,1280]{1,0:T(8,128)(2,1)}, bf16[512,1280]{1,0:T(8,128)(2,1)}, bf16[512,1280]{1,0:T(8,128)(2,1)}, bf16[2...) custom-call(s32[8]{0:T(128)} %copy-done.31, ...), custom_call_target="tpu_custom_call", output_to_operand_aliasing={{4}: (14, {}), {5}: (15, {}), {6}: (16, {}), {7}: (17, {}),... | custom-call | flops 24326963200 | bytes 37683200 | tf_op jit(solution)/shard_map/experts/pallas_call | solution.py:380
  450.6 22.7 %experts.9 = (bf16[512,1280]{1,0:T(8,128)(2,1)}, bf16[512,1280]{1,0:T(8,128)(2,1)}, bf16[2,8,320,1280]{3,2,1,0:T(8,128)(2,1)}, bf16[2,8,320,1280]{3,2,1,0:T(8,12...) custom-call(s32[8]{0:T(128)} %copy-done.31, ...), custom_call_target="tpu_custom_call", output_to_operand_aliasing={{2}: (9, {}), {3}: (10, {}), {4}: (11, {}), {5}: (12, {}), ... | custom-call | flops 12163481600 | bytes 25722880 | tf_op jit(solution)/shard_map/experts/pallas_call | solution.py:380
  476.7 19.8 %convolution_convert_fusion.4 = bf16[2,1280,896]{2,1,0:T(8,128)(2,1)} fusion(bf16[2,2560,1280]{2,1,0:T(8,128)(2,1)} %bitcast.133, bf16[2,2560,896]{2,1,0:T(8,128)(2,1)} %bitcast.139), kind=kOutput, calls=%fused_computation.4 | convolution fusion | flops 11746344960 | bytes 26869760 | tf_op jit(solution)/shard_map/ecd,ecf->edf/dot_general | solution.py:652
  501.8 21.5 %convolution_convert_fusion.3 = bf16[2,1280,896]{2,1,0:T(8,128)(2,1)} fusion(bf16[2,2560,1280]{2,1,0:T(8,128)(2,1)} %bitcast.134, bf16[2,2560,896]{2,1,0:T(8,128)(2,1)} %bitcast.140), kind=kOutput, calls=%fused_computation.3 | convolution fusion | flops 11746344960 | bytes 26869760 | tf_op jit(solution)/shard_map/ecd,ecf->edf/dot_general | solution.py:652
  523.2 3.2 add_convert_fusion.11
  531.9 19.9 %convolution_convert_fusion.2 = bf16[2,1280,896]{2,1,0:T(8,128)(2,1)} fusion(bf16[2,2560,1280]{2,1,0:T(8,128)(2,1)} %bitcast.135, bf16[2,2560,896]{2,1,0:T(8,128)(2,1)} %bitcast.138), kind=kOutput, calls=%fused_computation.2 | convolution fusion | flops 11746344960 | bytes 26869760 | tf_op jit(solution)/shard_map/ecd,ecf->edf/dot_general | solution.py:652
  556.7 3.3 add_convert_fusion.10
  560.9 15.0 %collective-permute-done.29 = bf16[512,1280]{1,0:T(8,128)(2,1)} collective-permute-done((bf16[512,1280]{1,0:T(8,128)(2,1)}, bf16[512,1280]{1,0:T(8,128)(2,1)}, u32[]{:S(2)}, u32[]{:S(2)}) %collective-permute-start.29) | collective-permute-done | bytes 1310752 | tf_op jit(solution)/shard_map/ppermute | solution.py:98
  578.1 4.1 multiply_reduce_fusion
  582.2 3.9 fusion.46
  591.8 5.9 all-to-all-start.3
  602.3 3.6 convolution_convert_fusion
  605.9 23.2 %collective-permute-done.30 = bf16[256,1280]{1,0:T(8,128)(2,1)} collective-permute-done((bf16[256,1280]{1,0:T(8,128)(2,1)}, bf16[256,1280]{1,0:T(8,128)(2,1)}, u32[]{:S(2)}, u32[]{:S(2)}) %collective-permute-start.30) | collective-permute-done | bytes 655392 | tf_op jit(solution)/shard_map/ppermute | solution.py:98
  649.6 22.7 %attention_backward.2.rest_0_ = bf16[4096,768]{1,0:T(8,128)(2,1)S(1)} custom-call(s32[2]{0:T(128)S(1)} %copy-done.33, bf16[4096,768]{1,0:T(8,128)(2,1)} %copy-done.2, bf16[8,640,128]{2,1,0:T(8,128)(2,1)S(1)} %copy-done.19, f32[8,640,128]{2,1,0:T(8,128)S(1)} %copy-done.22, f32[8,8,640]{2,1,0:T(8,128)S(1)} %copy-done.29, f32[4096,128]{1,0:T(8,128)S(1)} %copy-done.4, ...), custom_call_target="tpu_custom_call" | custom-call | flops 2684354560 | bytes 10485760 | tf_op jit(solution)/shard_map/attention_backward/pallas_call | solution.py:295
  693.1 38.1 %attention_backward.3 = bf16[4096,768]{1,0:T(8,128)(2,1)S(1)} custom-call(s32[2]{0:T(128)S(1)} %copy-done.33, bf16[4096,768]{1,0:T(8,128)(2,1)} %copy-done.2, bf16[8,640,128]{2,1,0:T(8,128)(2,1)S(1)} %copy-done.20, f32[8,640,128]{2,1,0:T(8,128)S(1)} %copy-done.23, f32[8,8,640]{2,1,0:T(8,128)S(1)} %copy-done.30, ...), custom_call_target="tpu_custom_call", output_to_operand_aliasing={{}: (7, {})} | custom-call | flops 10737418240 | bytes 10485760 | tf_op jit(solution)/shard_map/attention_backward/pallas_call | solution.py:295
  745.3 5.0 collective-permute-done.36
  751.2 8.4 convolution_convert_fusion.6
  764.6 24.3 %collective-permute-done.41 = bf16[512,1280]{1,0:T(8,128)(2,1)} collective-permute-done((bf16[512,1280]{1,0:T(8,128)(2,1)}, bf16[512,1280]{1,0:T(8,128)(2,1)}, u32[]{:S(2)}, u32[]{:S(2)}) %collective-permute-start.41) | collective-permute-done | bytes 1310752 | tf_op jit(solution)/shard_map/ppermute | solution.py:98
  788.8 4.4 copy.337
  795.4 4.2 convolution_convert_fusion.10
  818.0 3.7 add_convert_fusion.2
  828.9 9.1 %collective-permute-done.43 = bf16[512,1280]{1,0:T(8,128)(2,1)} collective-permute-done((bf16[512,1280]{1,0:T(8,128)(2,1)}, bf16[512,1280]{1,0:T(8,128)(2,1)}, u32[]{:S(2)}, u32[]{:S(2)}) %collective-permute-start.43) | collective-permute-done | bytes 1310752 | tf_op jit(solution)/shard_map/ppermute | solution.py:98
  841.8 6.7 all-to-all-start.4
  848.6 3.9 add_convert_fusion.1
  858.7 3.3 all-to-all-done.4
  873.0 8.3 collective-permute-done.44
  884.1 4.3 fusion.6
  (436 shorter events, 227.8 us)
Async XLA Ops:
  7.2 90.4 %all-gather.5.cloned.1.call-start = ((), (), s32[]{:S(2)}) async-start(), calls=%async_computation.13 | async-start | bytes 2867200 | tf_op jit(solution)/shard_map/all_gather | solution.py:544
  7.2 44.2 %collective-permute-start = (bf16[512,1280]{1,0:T(8,128)(2,1)}, bf16[512,1280]{1,0:T(8,128)(2,1)}, u32[]{:S(2)}, u32[]{:S(2)}) collective-permute-start(bf16[512,1280]{1,0:T(8,128)(2,1)} %bitcast.126), channel_id=1, source_target_pairs={{0,2},{2,4},{4,6},{6,7},{7,5},{5,3},{3,1},{1,0},{8,10},{10,12},{12... | collective-permute-start | bytes 3932168 | tf_op jit(solution)/shard_map/ppermute | solution.py:72
  7.7 43.7 %collective-permute-start.1 = (bf16[512,1280]{1,0:T(8,128)(2,1)}, bf16[512,1280]{1,0:T(8,128)(2,1)S(1)}, u32[]{:S(2)}, u32[]{:S(2)}) collective-permute-start(bf16[512,1280]{1,0:T(8,128)(2,1)} %bitcast.127), channel_id=1, source_target_pairs={{0,1},{2,0},{4,2},{6,4},{7,6},{5,7},{3,5},{1,3},{8,9},{10,8},{12,1... | collective-permute-start | bytes 3932168 | tf_op jit(solution)/shard_map/ppermute | solution.py:72
  57.7 144.1 %all-gather.7.cloned.1.call-start = ((), (), s32[]{:S(2)}) async-start(), calls=%async_computation.14 | async-start | bytes 2856960 | tf_op jit(solution)/shard_map/all_gather | solution.py:555
  65.2 29.0 %collective-permute-start.2 = (bf16[512,1280]{1,0:T(8,128)(2,1)}, bf16[512,1280]{1,0:T(8,128)(2,1)}, u32[]{:S(2)}, u32[]{:S(2)}) collective-permute-start(bf16[512,1280]{1,0:T(8,128)(2,1)} %collective-permute-done.tok_ref), channel_id=1, source_target_pairs={{0,2},{2,4},{4,6},{6,7},{7,5},{5,3},{3,1},{1,0},{8,10},{10,12},{12... | collective-permute-start | bytes 3932168 | tf_op jit(solution)/shard_map/ppermute | solution.py:72
  65.8 28.4 %collective-permute-start.3 = (bf16[512,1280]{1,0:T(8,128)(2,1)S(1)}, bf16[512,1280]{1,0:T(8,128)(2,1)}, u32[]{:S(2)}, u32[]{:S(2)}) collective-permute-start(bf16[512,1280]{1,0:T(8,128)(2,1)S(1)} %collective-permute-done.1.tok_ref), channel_id=1, source_target_pairs={{0,1},{2,0},{4,2},{6,4},{7,6},{5,7},{3,5},{1,3},{8,9},{10,8},{12,1... | collective-permute-start | bytes 3932168 | tf_op jit(solution)/shard_map/ppermute | solution.py:72
  94.2 31.3 %collective-permute-start.4 = (bf16[512,1280]{1,0:T(8,128)(2,1)}, bf16[512,1280]{1,0:T(8,128)(2,1)}, u32[]{:S(2)}, u32[]{:S(2)}) collective-permute-start(bf16[512,1280]{1,0:T(8,128)(2,1)} %collective-permute-done.2.tok_ref), channel_id=1, source_target_pairs={{0,2},{2,4},{4,6},{6,7},{7,5},{5,3},{3,1},{1,0},{8,10},{10,12},{12... | collective-permute-start | bytes 3932168 | tf_op jit(solution)/shard_map/ppermute | solution.py:72
  94.7 30.7 %collective-permute-start.5 = (bf16[512,1280]{1,0:T(8,128)(2,1)}, bf16[512,1280]{1,0:T(8,128)(2,1)}, u32[]{:S(2)}, u32[]{:S(2)}) collective-permute-start(bf16[512,1280]{1,0:T(8,128)(2,1)} %collective-permute-done.3.tok_ref), channel_id=1, source_target_pairs={{0,1},{2,0},{4,2},{6,4},{7,6},{5,7},{3,5},{1,3},{8,9},{10,8},{12,1... | collective-permute-start | bytes 3932168 | tf_op jit(solution)/shard_map/ppermute | solution.py:72
  125.4 114.0 %all-gather.9.cloned.1.call-start = ((), (), s32[]{:S(2)}) async-start(), calls=%async_computation.15 | async-start | bytes 4096000 | tf_op jit(solution)/shard_map/all_gather | solution.py:566
  156.2 45.5 %collective-permute-start.8 = (bf16[512,1280]{1,0:T(8,128)(2,1)}, bf16[512,1280]{1,0:T(8,128)(2,1)S(1)}, u32[]{:S(2)}, u32[]{:S(2)}) collective-permute-start(bf16[512,1280]{1,0:T(8,128)(2,1)} %bitcast.1.refs_1_.z_ref), channel_id=1, source_target_pairs={{0,2},{2,4},{4,6},{6,7},{7,5},{5,3},{3,1},{1,0},{8,10},{10,12},{12... | collective-permute-start | bytes 3932168 | tf_op jit(solution)/shard_map/ppermute | solution.py:72
  156.2 45.5 %collective-permute-start.9 = (bf16[512,1280]{1,0:T(8,128)(2,1)}, bf16[512,1280]{1,0:T(8,128)(2,1)}, u32[]{:S(2)}, u32[]{:S(2)}) collective-permute-start(bf16[512,1280]{1,0:T(8,128)(2,1)} %bitcast.1.refs_1_.z_ref), channel_id=1, source_target_pairs={{0,1},{2,0},{4,2},{6,4},{7,6},{5,7},{3,5},{1,3},{8,9},{10,8},{12,1... | collective-permute-start | bytes 3932168 | tf_op jit(solution)/shard_map/ppermute | solution.py:72
  204.3 32.2 %all-to-all-start.2 = ((bf16[8,640,128]{2,1,0:T(8,128)(2,1)}), bf16[8,640,128]{2,1,0:T(8,128)(2,1)S(1)}, u32[]{:S(2)}, u32[]{:S(2)}) async-start(bf16[8,640,128]{2,1,0:T(8,128)(2,1)} %get-tuple-element.227), calls=%async_computation.2 | async-start | bytes 2621440 | tf_op jit(solution)/shard_map/all_to_all | solution.py:568
  211.3 126.5 %all-gather.11.cloned.1.call-start = ((), (), s32[]{:S(2)}) async-start(), calls=%async_computation.16 | async-start | bytes 8601600 | tf_op jit(solution)/shard_map/all_gather | solution.py:582
  211.3 50.7 %collective-permute-start.10 = (bf16[512,1280]{1,0:T(8,128)(2,1)}, bf16[512,1280]{1,0:T(8,128)(2,1)}, u32[]{:S(2)}, u32[]{:S(2)}) collective-permute-start(bf16[512,1280]{1,0:T(8,128)(2,1)} %copy-done.84), channel_id=1, source_target_pairs={{0,2},{2,4},{4,6},{6,7},{7,5},{5,3},{3,1},{1,0},{8,10},{10,12},{12... | collective-permute-start | bytes 3932168 | tf_op jit(solution)/shard_map/ppermute | solution.py:72
  211.9 50.1 %collective-permute-start.11 = (bf16[512,1280]{1,0:T(8,128)(2,1)}, bf16[512,1280]{1,0:T(8,128)(2,1)}, u32[]{:S(2)}, u32[]{:S(2)}) collective-permute-start(bf16[512,1280]{1,0:T(8,128)(2,1)} %collective-permute-done.9.refs_3_), channel_id=1, source_target_pairs={{0,1},{2,0},{4,2},{6,4},{7,6},{5,7},{3,5},{1,3},{8,9},{10,8},{12,1... | collective-permute-start | bytes 3932168 | tf_op jit(solution)/shard_map/ppermute | solution.py:72
  263.3 236.4 %reduce-scatter.15.cloned.1.call-start = ((), (), s32[]{:S(2)}) async-start(), calls=%async_computation.18 | async-start | bytes 2867200 | tf_op jit(solution)/shard_map/reduce_scatter | solution.py:639
  263.4 30.3 %collective-permute-start.12 = (bf16[512,1280]{1,0:T(8,128)(2,1)}, bf16[512,1280]{1,0:T(8,128)(2,1)}, u32[]{:S(2)}, u32[]{:S(2)}) collective-permute-start(bf16[512,1280]{1,0:T(8,128)(2,1)} %multiply_convert_fusion.refs_0_.h_ref), channel_id=1, source_target_pairs={{0,2},{2,4},{4,6},{6,7},{7,5},{5,3},{3,1},{1,0},{8,10},{10,12},{12... | collective-permute-start | bytes 3932168 | tf_op jit(solution)/shard_map/ppermute | solution.py:72
  263.5 30.3 %collective-permute-start.13 = (bf16[512,1280]{1,0:T(8,128)(2,1)}, bf16[512,1280]{1,0:T(8,128)(2,1)}, u32[]{:S(2)}, u32[]{:S(2)}) collective-permute-start(bf16[512,1280]{1,0:T(8,128)(2,1)} %multiply_convert_fusion.refs_0_.h_ref), channel_id=1, source_target_pairs={{0,1},{2,0},{4,2},{6,4},{7,6},{5,7},{3,5},{1,3},{8,9},{10,8},{12,1... | collective-permute-start | bytes 3932168 | tf_op jit(solution)/shard_map/ppermute | solution.py:72
  293.7 42.0 %collective-permute-start.14 = (bf16[512,1280]{1,0:T(8,128)(2,1)}, bf16[512,1280]{1,0:T(8,128)(2,1)}, u32[]{:S(2)}, u32[]{:S(2)}) collective-permute-start(bf16[512,1280]{1,0:T(8,128)(2,1)} %collective-permute-done.12.refs_0_), channel_id=1, source_target_pairs={{0,2},{2,4},{4,6},{6,7},{7,5},{5,3},{3,1},{1,0},{8,10},{10,12},{12... | collective-permute-start | bytes 3932168 | tf_op jit(solution)/shard_map/ppermute | solution.py:72
  294.0 41.8 %collective-permute-start.15 = (bf16[512,1280]{1,0:T(8,128)(2,1)}, bf16[512,1280]{1,0:T(8,128)(2,1)}, u32[]{:S(2)}, u32[]{:S(2)}) collective-permute-start(bf16[512,1280]{1,0:T(8,128)(2,1)} %collective-permute-done.13.refs_1_), channel_id=1, source_target_pairs={{0,1},{2,0},{4,2},{6,4},{7,6},{5,7},{3,5},{1,3},{8,9},{10,8},{12,1... | collective-permute-start | bytes 3932168 | tf_op jit(solution)/shard_map/ppermute | solution.py:72
  335.8 27.5 %collective-permute-start.16 = (bf16[512,1280]{1,0:T(8,128)(2,1)}, bf16[512,1280]{1,0:T(8,128)(2,1)}, u32[]{:S(2)}, u32[]{:S(2)}) collective-permute-start(bf16[512,1280]{1,0:T(8,128)(2,1)} %collective-permute-done.10.refs_2_), channel_id=1, source_target_pairs={{0,2},{2,4},{4,6},{6,7},{7,5},{5,3},{3,1},{1,0},{8,10},{10,12},{12... | collective-permute-start | bytes 3932168 | tf_op jit(solution)/shard_map/ppermute | solution.py:72
  336.0 27.3 %collective-permute-start.17 = (bf16[512,1280]{1,0:T(8,128)(2,1)}, bf16[512,1280]{1,0:T(8,128)(2,1)S(1)}, u32[]{:S(2)}, u32[]{:S(2)}) collective-permute-start(bf16[512,1280]{1,0:T(8,128)(2,1)} %collective-permute-done.11.refs_3_), channel_id=1, source_target_pairs={{0,1},{2,0},{4,2},{6,4},{7,6},{5,7},{3,5},{1,3},{8,9},{10,8},{12,1... | collective-permute-start | bytes 3932168 | tf_op jit(solution)/shard_map/ppermute | solution.py:72
  363.3 136.4 %reduce-scatter.13.cloned.1.call-start = ((), (), s32[]{:S(2)}) async-start(), calls=%async_computation.17 | async-start | bytes 5734400 | tf_op jit(solution)/shard_map/reduce_scatter | solution.py:639
  364.3 196.6 %reduce-scatter.17.cloned.1.call-start = ((), (), s32[]{:S(2)}) async-start(), calls=%async_computation.19 | async-start | bytes 5734400 | tf_op jit(solution)/shard_map/reduce_scatter | solution.py:662
  364.3 44.3 %collective-permute-start.18 = (bf16[512,1280]{1,0:T(8,128)(2,1)}, bf16[512,1280]{1,0:T(8,128)(2,1)}, u32[]{:S(2)}, u32[]{:S(2)}) collective-permute-start(bf16[512,1280]{1,0:T(8,128)(2,1)} %collective-permute-done.14.refs_0_), channel_id=1, source_target_pairs={{0,2},{2,4},{4,6},{6,7},{7,5},{5,3},{3,1},{1,0},{8,10},{10,12},{12... | collective-permute-start | bytes 3932168 | tf_op jit(solution)/shard_map/ppermute | solution.py:72
  364.6 44.1 %collective-permute-start.19 = (bf16[512,1280]{1,0:T(8,128)(2,1)}, bf16[512,1280]{1,0:T(8,128)(2,1)}, u32[]{:S(2)}, u32[]{:S(2)}) collective-permute-start(bf16[512,1280]{1,0:T(8,128)(2,1)} %collective-permute-done.15.refs_1_), channel_id=1, source_target_pairs={{0,1},{2,0},{4,2},{6,4},{7,6},{5,7},{3,5},{1,3},{8,9},{10,8},{12,1... | collective-permute-start | bytes 3932168 | tf_op jit(solution)/shard_map/ppermute | solution.py:72
  408.7 41.9 %collective-permute-start.20 = (bf16[512,1280]{1,0:T(8,128)(2,1)}, bf16[512,1280]{1,0:T(8,128)(2,1)}, u32[]{:S(2)}, u32[]{:S(2)}) collective-permute-start(bf16[512,1280]{1,0:T(8,128)(2,1)} %collective-permute-done.18.refs_0_), channel_id=1, source_target_pairs={{0,2},{2,4},{4,6},{6,7},{7,5},{5,3},{3,1},{1,0},{8,10},{10,12},{12... | collective-permute-start | bytes 3932168 | tf_op jit(solution)/shard_map/ppermute | solution.py:626
  409.1 41.5 %collective-permute-start.21 = (bf16[512,1280]{1,0:T(8,128)(2,1)}, bf16[512,1280]{1,0:T(8,128)(2,1)}, u32[]{:S(2)}, u32[]{:S(2)}) collective-permute-start(bf16[512,1280]{1,0:T(8,128)(2,1)} %copy-done.85), channel_id=1, source_target_pairs={{0,1},{2,0},{4,2},{6,4},{7,6},{5,7},{3,5},{1,3},{8,9},{10,8},{12,1... | collective-permute-start | bytes 3932168 | tf_op jit(solution)/shard_map/ppermute | solution.py:627
  496.6 132.5 %reduce-scatter.19.cloned.1.call-start = ((), (), s32[]{:S(2)}) async-start(), calls=%async_computation.20 | async-start | bytes 5734400 | tf_op jit(solution)/shard_map/reduce_scatter | solution.py:662
  499.3 23.9 %collective-permute-start.24 = (bf16[512,1280]{1,0:T(8,128)(2,1)S(1)}, bf16[512,1280]{1,0:T(8,128)(2,1)}, u32[]{:S(2)}, u32[]{:S(2)}) collective-permute-start(bf16[512,1280]{1,0:T(8,128)(2,1)S(1)} %pad_maximum_fusion.4), channel_id=1, source_target_pairs={{0,2},{2,4},{4,6},{6,7},{7,5},{5,3},{3,1},{1,0},{8,10},{10,12},{12... | collective-permute-start | bytes 3932168 | tf_op jit(solution)/shard_map/ppermute | solution.py:98
  526.5 26.6 %collective-permute-start.27 = (bf16[512,1280]{1,0:T(8,128)(2,1)}, bf16[512,1280]{1,0:T(8,128)(2,1)S(1)}, u32[]{:S(2)}, u32[]{:S(2)}) collective-permute-start(bf16[512,1280]{1,0:T(8,128)(2,1)} %add_convert_fusion.11), channel_id=1, source_target_pairs={{0,1},{2,0},{4,2},{6,4},{7,6},{5,7},{3,5},{1,3},{8,9},{10,8},{12,1... | collective-permute-start | bytes 3932168 | tf_op jit(solution)/shard_map/ppermute | solution.py:98
  591.8 37.3 %all-to-all-start.3 = ((bf16[8,640,128]{2,1,0:T(8,128)(2,1)}), bf16[8,640,128]{2,1,0:T(8,128)(2,1)S(1)}, u32[]{:S(2)}, u32[]{:S(2)}) async-start(bf16[8,640,128]{2,1,0:T(8,128)(2,1)} %pad_maximum_fusion.6), calls=%async_computation.6 | async-start | bytes 2621440 | tf_op jit(solution)/shard_map/all_to_all | solution.py:683
  597.7 77.3 %reduce-scatter.21.cloned.1.call-start = ((), (), s32[]{:S(2)}) async-start(), calls=%async_computation.21 | async-start | bytes 4096000 | tf_op jit(solution)/shard_map/reduce_scatter | solution.py:690
  600.3 28.8 %collective-permute-start.30 = (bf16[256,1280]{1,0:T(8,128)(2,1)}, bf16[256,1280]{1,0:T(8,128)(2,1)}, u32[]{:S(2)}, u32[]{:S(2)}) collective-permute-start(bf16[256,1280]{1,0:T(8,128)(2,1)} %get-tuple-element.398), channel_id=1, source_target_pairs={{0,2},{2,4},{4,6},{6,7},{7,5},{5,3},{3,1},{1,0},{8,10},{10,12},{12... | collective-permute-start | bytes 1966088 | tf_op jit(solution)/shard_map/ppermute | solution.py:98
  600.8 28.3 %collective-permute-start.31 = (bf16[256,1280]{1,0:T(8,128)(2,1)S(1)}, bf16[256,1280]{1,0:T(8,128)(2,1)}, u32[]{:S(2)}, u32[]{:S(2)}) collective-permute-start(bf16[256,1280]{1,0:T(8,128)(2,1)S(1)} %get-tuple-element.397), channel_id=1, source_target_pairs={{0,1},{2,0},{4,2},{6,4},{7,6},{5,7},{3,5},{1,3},{8,9},{10,8},{12,1... | collective-permute-start | bytes 1966088 | tf_op jit(solution)/shard_map/ppermute | solution.py:98
  629.1 192.6 %reduce-scatter.27.cloned.1.call-start = ((), (), s32[]{:S(2)}) async-start(), calls=%async_computation.24 | async-start | bytes 2856960
  633.5 41.5 %collective-permute-start.33 = (bf16[512,1280]{1,0:T(8,128)(2,1)}, bf16[512,1280]{1,0:T(8,128)(2,1)}, u32[]{:S(2)}, u32[]{:S(2)}) collective-permute-start(bf16[512,1280]{1,0:T(8,128)(2,1)} %pad_maximum_fusion.8), channel_id=1, source_target_pairs={{0,1},{2,0},{4,2},{6,4},{7,6},{5,7},{3,5},{1,3},{8,9},{10,8},{12,1... | collective-permute-start | bytes 3932168 | tf_op jit(solution)/shard_map/ppermute | solution.py:98
  636.6 38.4 %collective-permute-start.32 = (bf16[512,1280]{1,0:T(8,128)(2,1)}, bf16[512,1280]{1,0:T(8,128)(2,1)}, u32[]{:S(2)}, u32[]{:S(2)}) collective-permute-start(bf16[512,1280]{1,0:T(8,128)(2,1)} %pad_maximum_fusion.7), channel_id=1, source_target_pairs={{0,2},{2,4},{4,6},{6,7},{7,5},{5,3},{3,1},{1,0},{8,10},{10,12},{12... | collective-permute-start | bytes 3932168 | tf_op jit(solution)/shard_map/ppermute | solution.py:98
  678.2 53.0 %collective-permute-start.35 = (bf16[512,1280]{1,0:T(8,128)(2,1)}, bf16[512,1280]{1,0:T(8,128)(2,1)}, u32[]{:S(2)}, u32[]{:S(2)}) collective-permute-start(bf16[512,1280]{1,0:T(8,128)(2,1)} %add_convert_fusion.7), channel_id=1, source_target_pairs={{0,1},{2,0},{4,2},{6,4},{7,6},{5,7},{3,5},{1,3},{8,9},{10,8},{12,1... | collective-permute-start | bytes 3932168 | tf_op jit(solution)/shard_map/ppermute | solution.py:98
  681.9 49.3 %collective-permute-start.34 = (bf16[512,1280]{1,0:T(8,128)(2,1)}, bf16[512,1280]{1,0:T(8,128)(2,1)}, u32[]{:S(2)}, u32[]{:S(2)}) collective-permute-start(bf16[512,1280]{1,0:T(8,128)(2,1)} %add_convert_fusion.8), channel_id=1, source_target_pairs={{0,2},{2,4},{4,6},{6,7},{7,5},{5,3},{3,1},{1,0},{8,10},{10,12},{12... | collective-permute-start | bytes 3932168 | tf_op jit(solution)/shard_map/ppermute | solution.py:98
  684.6 142.1 %reduce-scatter.25.cloned.1.call-start = ((), (), s32[]{:S(2)}) async-start(), calls=%async_computation.23 | async-start | bytes 2867200
  737.6 51.2 %collective-permute-start.41 = (bf16[512,1280]{1,0:T(8,128)(2,1)}, bf16[512,1280]{1,0:T(8,128)(2,1)}, u32[]{:S(2)}, u32[]{:S(2)}) collective-permute-start(bf16[512,1280]{1,0:T(8,128)(2,1)} %add_convert_fusion.5), channel_id=1, source_target_pairs={{0,1},{2,0},{4,2},{6,4},{7,6},{5,7},{3,5},{1,3},{8,9},{10,8},{12,1... | collective-permute-start | bytes 3932168 | tf_op jit(solution)/shard_map/ppermute | solution.py:98
  741.3 47.5 %collective-permute-start.40 = (bf16[512,1280]{1,0:T(8,128)(2,1)}, bf16[512,1280]{1,0:T(8,128)(2,1)}, u32[]{:S(2)}, u32[]{:S(2)}) collective-permute-start(bf16[512,1280]{1,0:T(8,128)(2,1)} %add_convert_fusion.6), channel_id=1, source_target_pairs={{0,2},{2,4},{4,6},{6,7},{7,5},{5,3},{3,1},{1,0},{8,10},{10,12},{12... | collective-permute-start | bytes 3932168 | tf_op jit(solution)/shard_map/ppermute | solution.py:98
  761.1 49.8 %collective-permute-start.39 = (bf16[512,1280]{1,0:T(8,128)(2,1)}, bf16[512,1280]{1,0:T(8,128)(2,1)}, u32[]{:S(2)}, u32[]{:S(2)}) collective-permute-start(bf16[512,1280]{1,0:T(8,128)(2,1)} %pad_maximum_fusion.10), channel_id=1, source_target_pairs={{0,1},{2,0},{4,2},{6,4},{7,6},{5,7},{3,5},{1,3},{8,9},{10,8},{12,1... | collective-permute-start | bytes 3932168 | tf_op jit(solution)/shard_map/ppermute | solution.py:98
  793.2 95.2 %reduce-scatter.23.cloned.1.call-start = ((), (), s32[]{:S(2)}) async-start(), calls=%async_computation.22 | async-start | bytes 5734400 | tf_op jit(solution)/shard_map/reduce_scatter | solution.py:727
  814.5 23.6 %collective-permute-start.43 = (bf16[512,1280]{1,0:T(8,128)(2,1)}, bf16[512,1280]{1,0:T(8,128)(2,1)}, u32[]{:S(2)}, u32[]{:S(2)}) collective-permute-start(bf16[512,1280]{1,0:T(8,128)(2,1)} %add_convert_fusion.3), channel_id=1, source_target_pairs={{0,1},{2,0},{4,2},{6,4},{7,6},{5,7},{3,5},{1,3},{8,9},{10,8},{12,1... | collective-permute-start | bytes 3932168 | tf_op jit(solution)/shard_map/ppermute | solution.py:98
  852.5 28.8 %collective-permute-start.44 = (bf16[512,1280]{1,0:T(8,128)(2,1)}, bf16[512,1280]{1,0:T(8,128)(2,1)}, u32[]{:S(2)}, u32[]{:S(2)}) collective-permute-start(bf16[512,1280]{1,0:T(8,128)(2,1)} %add_convert_fusion.1), channel_id=1, source_target_pairs={{0,2},{2,4},{4,6},{6,7},{7,5},{5,3},{3,1},{1,0},{8,10},{10,12},{12... | collective-permute-start | bytes 3932168 | tf_op jit(solution)/shard_map/ppermute | solution.py:98
  855.7 25.5 %collective-permute-start.45 = (bf16[512,1280]{1,0:T(8,128)(2,1)}, bf16[512,1280]{1,0:T(8,128)(2,1)}, u32[]{:S(2)}, u32[]{:S(2)}) collective-permute-start(bf16[512,1280]{1,0:T(8,128)(2,1)} %add_convert_fusion), channel_id=1, source_target_pairs={{0,1},{2,0},{4,2},{6,4},{7,6},{5,7},{3,5},{1,3},{8,9},{10,8},{12,1... | collective-permute-start | bytes 3932168 | tf_op jit(solution)/shard_map/ppermute | solution.py:98
  (105 other events, 1262.9 us)
Sparse Core Ops, SparseCore 0:
  51.6 23.8 all-gather.4
  125.6 70.1 all-gather.6
  204.4 31.1 all-gather.8
  263.5 48.7 all-gather.10
  363.4 31.8 reduce-scatter.14
  397.9 46.9 reduce-scatter.12
  496.7 46.2 reduce-scatter.16
  545.7 46.9 reduce-scatter.18
  629.3 37.8 reduce-scatter.20
  684.7 101.9 reduce-scatter.26
  793.3 33.3 reduce-scatter.24
  839.8 47.7 reduce-scatter.22
